TPU v7x, 32 devices: a whole 2x2x4 slice. The times are simulated.
32 devices in a mesh: row: 8 (over y, x, core), col: 4 (over z).
Axes of the slice: x: 2, y: 2, z: 4, core: 2. Of those that a mesh axis runs over, the one named last changes fastest.
Arguments:
- right_side: float32 [4096, 4096], P('row', 'col'), may hold values from -170 to 170, as said below
- kappa_sq: float32 [4096, 4096], P('row', 'col'), may hold values from 0.02 to 0.5
- block_tract: int32 [256, 256], P('row', 'col'), may hold values from 0 to 63
- tract_county: int32 [2048], P(('row', 'col')), may hold values from 0 to 511
- county_state: int32 [512], replicated, may hold values from 0 to 55
- schur: float32 [4, 2048, 8, 1024], P(None, 'row', None, 'col'), may hold values from -64 to 65, as said below
Outputs:
- solution: float32 [4096, 4096], P('row', 'col')
- residual: float32 [4096, 4096], P('row', 'col')
- tract_totals: float32 [2048], P(('row', 'col'))
- county_totals: float32 [512], replicated
- state_totals: float32 [56], replicated
- updated: float32 [4, 2048, 8, 1024], P(None, 'row', None, 'col')
- panel: float32 [4, 2048, 256], P(None, 'row')
Inputs may be any that keep to these rules, and one draw needn't show every extreme that they name: `right_side`: a real field; its size varies strongly between rows, columns and regions. `schur`: symmetric positive definite.
All inputs are finite; a program needn't handle non-finite values.
Results may differ from a plain program's by a relative error of at most 0.0003.
Values sent between devices are 32-bit elements; how exact they have to be, the bound alone decides.
No kernel may reach another device: no remote copies, remote signals or barrier semaphores. Data moves between devices by JAX's collectives and lax.ppermute only.
A program may use at most 128 MiB of HBM per device.

v0:
```python
import jax
import jax.numpy as jnp
from jax import lax
from jax.sharding import PartitionSpec as P

BLOCK = 16
TRACTS_DEV = 64
ITERS = 2
COUNTIES = 512
STATES = 56


def extended(shard, sides, width):
    for axis, dim in sides:
        size, length = (lax.axis_size(axis), shard.shape[dim])
        up = [(i, (i + 1) % size) for i in range(size - 1)]
        down = [(j, i) for i, j in up]
        last = lax.slice_in_dim(shard, length - width, length, axis=dim)
        initial = lax.slice_in_dim(shard, 0, width, axis=dim)
        before = lax.ppermute(last, axis, up)
        after = lax.ppermute(initial, axis, down)
        shard = jnp.concatenate([before, shard, after], axis=dim)
    return shard


def broadcast(block, axis, owner):
    block = jnp.where(lax.axis_index(axis) == owner, block, jnp.zeros_like(block))
    return lax.psum(block, axis)


def rate_apart(grid_field, rate_field):
    padded = extended(grid_field, (("row", 0), ("col", 1)), 1)
    beside_all = padded[:-2, 1:-1] + padded[2:, 1:-1]
    beside_all = beside_all + padded[1:-1, :-2] + padded[1:-1, 2:]
    return (4.0 + rate_field) * grid_field - beside_all


def residual_sum(residual):
    return lax.psum(jnp.sum(residual * residual), ("row", "col"))


def per_device(right_side, kappa_sq, block_tract, tract_county, county_state, schur):
    col_count = lax.axis_size("col")
    tile_rows, tile_cols = right_side.shape
    solution = jnp.zeros_like(right_side)
    residual = right_side
    direction = right_side
    norm_now = residual_sum(residual)
    for iteration in range(ITERS):
        applied = rate_apart(rate_apart(direction, kappa_sq), kappa_sq)
        step_size = norm_now / lax.psum(jnp.sum(direction * applied), ("row", "col"))
        solution = solution + step_size * direction
        residual = residual - step_size * applied
        norm_next = residual_sum(residual)
        direction = residual + norm_next / norm_now * direction
        norm_now = norm_next
    block_sums = solution.reshape(tile_rows // BLOCK, BLOCK, tile_cols // BLOCK, BLOCK).sum(
        axis=(1, 3)
    )
    matches = block_tract[:, :, None] == jnp.arange(TRACTS_DEV, dtype=jnp.int32)
    tract_totals = jnp.sum(jnp.where(matches, block_sums[:, :, None], 0.0), axis=(0, 1))
    county_match = tract_county[:, None] == jnp.arange(COUNTIES, dtype=jnp.int32)
    county_part = jnp.sum(jnp.where(county_match, tract_totals[:, None], 0.0), axis=0)
    county_totals = lax.psum(county_part, ("row", "col"))
    state_match = county_state[:, None] == jnp.arange(STATES, dtype=jnp.int32)
    state_totals = jnp.sum(jnp.where(state_match, county_totals[:, None], 0.0), axis=0)
    block_rows, width, block_cols, _ = schur.shape
    col_index = lax.axis_index("col")
    diagonal = broadcast(schur[0, :, 0, :], "row", 0)
    diagonal = jnp.where(col_index == 0, diagonal, jnp.eye(width, dtype=jnp.float32))
    factor = jnp.linalg.cholesky(diagonal)
    column = schur[:, :, 0, :].reshape(block_rows * width, width)
    own_panel = jax.scipy.linalg.solve_triangular(factor, column.T, lower=True).T.reshape(
        block_rows, width, width
    )
    row_panel = broadcast(own_panel, "col", 0)
    gathered = lax.all_gather(row_panel, "row", axis=1, tiled=True)
    blocks = gathered.reshape(block_cols, col_count, width, width)
    col_panel = lax.dynamic_index_in_dim(blocks, col_index, 1, keepdims=False)
    product = jnp.einsum("ank,cmk->ancm", row_panel, col_panel, precision=lax.Precision.HIGHEST)
    updated = schur - product
    return (solution, residual, tract_totals, county_totals, state_totals, updated, row_panel)


def solution(mesh):
    in_specs = (
        P("row", "col"),
        P("row", "col"),
        P("row", "col"),
        P(("row", "col")),
        P(),
        P(None, "row", None, "col"),
    )
    out_specs = (
        P("row", "col"),
        P("row", "col"),
        P(("row", "col")),
        P(),
        P(),
        P(None, "row", None, "col"),
        P(None, "row", None),
    )
    return jax.shard_map(
        per_device, mesh=mesh, in_specs=in_specs, out_specs=out_specs, check_vma=False
    )
```

profile of v0, /device:TPU:0, one launch (start us, length us, event | category | flops | bytes accessed | tf_op | source)
XLA Modules:
  0.0 507.9 jit_solution(1229873474889484876)
XLA Ops:
  7.2 1.8 slice.197
  10.4 57.5 %all-reduce.5.cloned.1.call-done = f32[256,256]{0,1:T(8,128)} async-done(((f32[256,256]{0,1:T(8,128)}), f32[256,256]{0,1:T(8,128)}) %all-reduce.5.cloned.1.call-update) | async-done | bytes 262160 | tf_op jit(solution)/shard_map/psum | solution.py:28
  70.0 11.7 %cholesky.49 = f32[128,128]{1,0:T(8,128)S(1)} custom-call(f32[128,128]{1,0:T(8,128)S(1)} %cholesky.115), custom_call_target="Cholesky" | custom-call | tf_op jit(solution)/shard_map/jit(cholesky)/cholesky | solution.py:71
  81.8 9.8 %custom-call.15 = f32[1,128,128]{1,2,0:T(8,128)S(1)} custom-call(f32[1,128,128]{2,1,0:T(8,128)S(1)} %get-tuple-element.74), custom_call_target="InvertDiagBlocksLowerTriangular" | custom-call | tf_op jit(solution)/shard_map/jit(cholesky)/cholesky | solution.py:71
  92.1 11.7 %cholesky.103 = f32[128,128]{1,0:T(8,128)S(1)} custom-call(f32[128,128]{1,0:T(8,128)S(1)} %convolution_subtract_fusion.1), custom_call_target="Cholesky" | custom-call | tf_op jit(solution)/shard_map/jit(cholesky)/cholesky | solution.py:71
  105.9 4.2 while.1
  106.7 1.4 bitcast_dynamic-update-slice_fusion.2
  108.7 1.4 bitcast_dynamic-update-slice_fusion.2
  110.1 19.7 %custom-call.16 = f32[2,128,128]{1,2,0:T(8,128)S(1)} custom-call(f32[2,128,128]{2,1,0:T(8,128)S(1)} %get-tuple-element.14), custom_call_target="InvertDiagBlocksLowerTriangular" | custom-call | tf_op jit(solution)/shard_map/jit(_solve_triangular)/triangular_solve | solution.py:73
  131.7 1.3 copy.35
  133.1 49.4 %all-reduce.7.cloned.1.call-done = f32[4,256,256]{2,1,0:T(8,128)} async-done(((f32[4,256,256]{2,1,0:T(8,128)}), f32[4,256,256]{2,1,0:T(8,128)}) %all-reduce.7.cloned.1.call-update) | async-done | bytes 1048592 | tf_op jit(solution)/shard_map/psum | solution.py:28
  182.6 1.4 collective-permute-start.1
  184.0 3.0 collective-permute-start
  188.0 1.3 collective-permute-start.3
  189.3 4.6 collective-permute-start.2
  193.9 5.0 collective-permute-done.3
  198.9 1.7 collective-permute-done.2
  200.7 3.1 fusion.13
  203.8 1.3 collective-permute-start.5
  205.1 3.0 collective-permute-start.4
  209.1 1.3 collective-permute-start.7
  210.4 5.0 collective-permute-start.6
  215.4 4.0 collective-permute-done.7
  219.4 1.8 collective-permute-done.6
  221.2 4.9 multiply_reduce_fusion.2
  226.1 42.6 %all-reduce.1 = (f32[]{:T(128)}, f32[]{:T(128)}) all-reduce(f32[]{:T(128)} %get-tuple-element.37, f32[]{:T(128)} %get-tuple-element.36), channel_id=1, replica_groups=mesh['row'=8,'col'=4] {'row','col'}, use_global_device_ids=true, to_apply=%region_1.0 | all-reduce | flops 2 | bytes 16 | tf_op jit(solution)/shard_map/psum | solution.py:39
  270.0 2.7 multiply_reduce_fusion.1
  272.7 40.8 %psum.51 = f32[]{:T(128)} all-reduce(f32[]{:T(128)} %multiply_reduce_fusion.1), channel_id=1, replica_groups=mesh['row'=8,'col'=4] {'row','col'}, use_global_device_ids=true, to_apply=%region_5.0 | all-reduce | flops 1 | bytes 8 | tf_op jit(solution)/shard_map/psum | solution.py:39
  314.9 2.1 multiply_add_fusion.1
  317.0 1.6 collective-permute-start.9
  318.6 3.0 collective-permute-start.8
  322.5 1.3 collective-permute-start.11
  323.8 4.6 collective-permute-start.10
  328.4 4.5 collective-permute-done.11
  332.9 1.8 collective-permute-done.10
  334.7 3.4 fusion.5
  339.4 3.2 collective-permute-start.12
  344.8 4.9 collective-permute-start.14
  349.7 3.6 collective-permute-done.15
  353.4 1.8 collective-permute-done.14
  355.1 10.6 %multiply_reduce_fusion = (f32[]{:T(128)}, f32[512,1024]{1,0:T(8,128)}) fusion(f32[512,1024]{1,0:T(8,128)} %copy-done.1, f32[514,1]{1,0:T(8,128)S(1)} %collective-permute-done.15, f32[1,1024]{1,0:T(1,128)S(1)} %collective-permute-done.13, f32[512,1024]{1,0:T(8,128)} %copy-done.4, f32[1,1024]{1,0:T(1,128)S(1)} %collective-permute-done.12, ...), kind=kLoop, calls=%fused_computation.55 | loop fusion | flops 8388607 | bytes 8400916 | tf_op jit(solution)/shard_map/reduce_sum | solution.py:51
  365.8 42.9 %psum.52 = f32[]{:T(128)} all-reduce(f32[]{:T(128)} %get-tuple-element.48), channel_id=1, replica_groups=mesh['row'=8,'col'=4] {'row','col'}, use_global_device_ids=true, to_apply=%region_7.0 | all-reduce | flops 1 | bytes 8 | tf_op jit(solution)/shard_map/psum | solution.py:51
  410.0 6.1 %multiply_subtract_fusion = (f32[512,1024]{1,0:T(8,128)}, f32[512,1024]{1,0:T(8,128)}) fusion(f32[512,1024]{1,0:T(8,128)} %get-tuple-element.49, f32[]{:T(128)S(6)} %div.19, f32[512,1024]{1,0:T(8,128)S(1)} %copy-done, f32[512,1024]{1,0:T(8,128)} %get-tuple-element.50, f32[]{:T(128)S(6)} %div.17, f32[512,1024]{1,0:T(8,128)} %copy-done.1), kind=kLoop, calls=%fused_computation.53 | loop fusion | flops 3670016 | bytes 12582920 | tf_op jit(solution)/shard_map/sub | solution.py:53
  416.1 10.3 %reshape.52 = f32[32,16,64,16]{3,2,1,0:T(8,128)} reshape(f32[512,1024]{1,0:T(8,128)} %get-tuple-element.123) | data formatting | bytes 4194304 | tf_op jit(solution)/shard_map/reshape | solution.py:57
  426.5 7.1 %reduce_sum.76 = f32[32,64]{1,0:T(8,128)S(1)} reduce(f32[32,16,64,16]{3,2,1,0:T(8,128)} %reshape.52, f32[]{:T(128)} %constant.89.clone.1), dimensions={1,3}, to_apply=%region_8.0 | reduce | flops 522240 | bytes 2105348 | tf_op jit(solution)/shard_map/reduce_sum | solution.py:57
  434.4 41.8 %psum.53 = f32[512]{0:T(512)S(1)} all-reduce(f32[512]{0:T(512)S(1)} %select_reduce_fusion.1), channel_id=1, replica_groups=mesh['row'=8,'col'=4] {'row','col'}, use_global_device_ids=true, to_apply=%region_11.12 | all-reduce | flops 512 | bytes 4096 | tf_op jit(solution)/shard_map/psum | solution.py:64
  476.9 14.8 %copy_subtract_fusion = f32[4,256,8,256]{3,1,2,0:T(8,128)S(1)} fusion(f32[4,256,8,256]{3,2,1,0:T(8,128)} %param.11, f32[8,4,256,256]{3,2,1,0:T(8,128)} %bitcast.54, s32[]{:T(128)S(6)} %select_n.64, f32[4,256,256]{2,1,0:T(8,128)S(1)} %copy-done.5), kind=kOutput, calls=%fused_computation.2 | convolution fusion | flops 6444548096 | bytes 19922948 | tf_op jit(solution)/shard_map/ank,cmk->ancm/dot_general | solution.py:80
  491.7 8.3 %copy.33 = f32[4,256,8,256]{3,2,1,0:T(8,128)} copy(f32[4,256,8,256]{3,1,2,0:T(8,128)S(1)} %copy_subtract_fusion) | data formatting | bytes 16777216
  (79 shorter events, 16.8 us)
Async XLA Ops:
  7.2 2.8 slice-start
  7.2 60.7 %all-reduce.5.cloned.1.call-start = ((), (), s32[]{:S(2)}) async-start(), calls=%async_computation | async-start | bytes 524288 | tf_op jit(solution)/shard_map/psum | solution.py:28
  9.9 172.6 %all-reduce.7.cloned.1.call-start = ((), (), s32[]{:S(2)}) async-start(), calls=%async_computation.1 | async-start | bytes 2097152 | tf_op jit(solution)/shard_map/psum | solution.py:28
  131.7 50.8 %copy-start = (f32[512,1024]{1,0:T(8,128)S(1)}, f32[512,1024]{1,0:T(8,128)}, u32[]{:S(2)}) copy-start(f32[512,1024]{1,0:T(8,128)} %param.6) | copy-start | bytes 6291460
  133.1 343.8 %all-gather.2.cloned.1.call-start = ((), (), s32[]{:S(2)}) async-start(), calls=%async_computation.2 | async-start | bytes 9437184 | tf_op jit(solution)/shard_map/all_gather | solution.py:77
  182.6 18.1 %copy-start.2 = (f32[512,1024]{1,0:T(8,128)S(1)}, f32[512,1024]{1,0:T(8,128)}, u32[]{:S(2)}) copy-start(f32[512,1024]{1,0:T(8,128)} %param.7) | copy-start | bytes 6291460
  182.6 4.5 collective-permute-start.1
  184.0 3.8 collective-permute-start
  188.0 10.9 %collective-permute-start.3 = (f32[514,1]{1,0:T(8,128)S(1)}, f32[514,1]{1,0:T(8,128)S(1)}, u32[]{:S(2)}, u32[]{:S(2)}) collective-permute-start(f32[514,1]{1,0:T(8,128)S(1)} %get-tuple-element.60), channel_id=1, source_target_pairs={{1,0},{2,1},{3,2},{5,4},{6,5},{7,6},{9,8},{10,9},{11,10},{13,12},{... | collective-permute-start | bytes 6176 | tf_op jit(solution)/shard_map/ppermute | solution.py:21
  189.3 11.3 %collective-permute-start.2 = (f32[514,1]{1,0:T(8,128)S(1)}, f32[514,1]{1,0:T(8,128)S(1)}, u32[]{:S(2)}, u32[]{:S(2)}) collective-permute-start(f32[514,1]{1,0:T(8,128)S(1)} %get-tuple-element.59), channel_id=1, source_target_pairs={{0,1},{1,2},{2,3},{4,5},{5,6},{6,7},{8,9},{9,10},{10,11},{12,13},{... | collective-permute-start | bytes 6176 | tf_op jit(solution)/shard_map/ppermute | solution.py:20
  203.8 4.3 collective-permute-start.5
  205.1 3.8 collective-permute-start.4
  209.1 10.3 %collective-permute-start.7 = (f32[514,1]{1,0:T(8,128)S(1)}, f32[514,1]{1,0:T(8,128)S(1)}, u32[]{:S(2)}, u32[]{:S(2)}) collective-permute-start(f32[514,1]{1,0:T(8,128)S(1)} %get-tuple-element.58), channel_id=1, source_target_pairs={{1,0},{2,1},{3,2},{5,4},{6,5},{7,6},{9,8},{10,9},{11,10},{13,12},{... | collective-permute-start | bytes 6176 | tf_op jit(solution)/shard_map/ppermute | solution.py:21
  210.4 10.8 %collective-permute-start.6 = (f32[514,1]{1,0:T(8,128)S(1)}, f32[514,1]{1,0:T(8,128)S(1)}, u32[]{:S(2)}, u32[]{:S(2)}) collective-permute-start(f32[514,1]{1,0:T(8,128)S(1)} %get-tuple-element.57), channel_id=1, source_target_pairs={{0,1},{1,2},{2,3},{4,5},{5,6},{6,7},{8,9},{9,10},{10,11},{12,13},{... | collective-permute-start | bytes 6176 | tf_op jit(solution)/shard_map/ppermute | solution.py:20
  317.0 21.1 %copy-start.1 = (f32[512,1024]{1,0:T(8,128)}, f32[512,1024]{1,0:T(8,128)S(1)}, u32[]{:S(2)}) copy-start(f32[512,1024]{1,0:T(8,128)S(1)} %multiply_add_fusion.1) | copy-start | bytes 6291460
  317.0 17.7 %copy-start.3 = (f32[512,1024]{1,0:T(8,128)S(1)}, f32[512,1024]{1,0:T(8,128)}, u32[]{:S(2)}) copy-start(f32[512,1024]{1,0:T(8,128)} %param.7) | copy-start | bytes 6291460
  317.0 4.6 collective-permute-start.9
  318.6 3.8 collective-permute-start.8
  322.5 10.3 %collective-permute-start.11 = (f32[514,1]{1,0:T(8,128)S(1)}, f32[514,1]{1,0:T(8,128)S(1)}, u32[]{:S(2)}, u32[]{:S(2)}) collective-permute-start(f32[514,1]{1,0:T(8,128)S(1)} %get-tuple-element.56), channel_id=1, source_target_pairs={{1,0},{2,1},{3,2},{5,4},{6,5},{7,6},{9,8},{10,9},{11,10},{13,12},{... | collective-permute-start | bytes 6176 | tf_op jit(solution)/shard_map/ppermute | solution.py:21
  323.8 10.8 %collective-permute-start.10 = (f32[514,1]{1,0:T(8,128)S(1)}, f32[514,1]{1,0:T(8,128)S(1)}, u32[]{:S(2)}, u32[]{:S(2)}) collective-permute-start(f32[514,1]{1,0:T(8,128)S(1)} %get-tuple-element.55), channel_id=1, source_target_pairs={{0,1},{1,2},{2,3},{4,5},{5,6},{6,7},{8,9},{9,10},{10,11},{12,13},{... | collective-permute-start | bytes 6176 | tf_op jit(solution)/shard_map/ppermute | solution.py:20
  338.1 5.3 %copy-start.4 = (f32[512,1024]{1,0:T(8,128)}, f32[512,1024]{1,0:T(8,128)S(1)}, u32[]{:S(2)}) copy-start(f32[512,1024]{1,0:T(8,128)S(1)} %fusion.5) | copy-start | bytes 6291460
  338.1 4.5 collective-permute-start.13
  339.4 4.0 collective-permute-start.12
  343.5 9.8 %collective-permute-start.15 = (f32[514,1]{1,0:T(8,128)S(1)}, f32[514,1]{1,0:T(8,128)S(1)}, u32[]{:S(2)}, u32[]{:S(2)}) collective-permute-start(f32[514,1]{1,0:T(8,128)S(1)} %get-tuple-element.54), channel_id=1, source_target_pairs={{1,0},{2,1},{3,2},{5,4},{6,5},{7,6},{9,8},{10,9},{11,10},{13,12},{... | collective-permute-start | bytes 6176 | tf_op jit(solution)/shard_map/ppermute | solution.py:21
  344.8 10.3 %collective-permute-start.14 = (f32[514,1]{1,0:T(8,128)S(1)}, f32[514,1]{1,0:T(8,128)S(1)}, u32[]{:S(2)}, u32[]{:S(2)}) collective-permute-start(f32[514,1]{1,0:T(8,128)S(1)} %get-tuple-element.53), channel_id=1, source_target_pairs={{0,1},{1,2},{2,3},{4,5},{5,6},{6,7},{8,9},{9,10},{10,11},{12,13},{... | collective-permute-start | bytes 6176 | tf_op jit(solution)/shard_map/ppermute | solution.py:20
  426.5 7.2 %copy-start.6 = (s32[32,64]{1,0:T(8,128)S(1)}, s32[32,64]{1,0:T(8,128)}, u32[]{:S(2)}) copy-start(s32[32,64]{1,0:T(8,128)} %param.8) | copy-start | bytes 24580
  426.5 7.9 %copy-start.10 = (s32[64]{0:T(128)S(1)}, s32[64]{0:T(128)}, u32[]{:S(2)}) copy-start(s32[64]{0:T(128)} %param.9) | copy-start | bytes 772
  426.5 49.8 %copy-start.9 = (s32[512]{0:T(512)S(1)}, s32[512]{0:T(512)}, u32[]{:S(2)}) copy-start(s32[512]{0:T(512)} %param.10) | copy-start | bytes 6148
  426.5 50.5 %copy-start.5 = (f32[4,256,256]{2,1,0:T(8,128)S(1)}, f32[4,256,256]{2,1,0:T(8,128)}, u32[]{:S(2)}) copy-start(f32[4,256,256]{2,1,0:T(8,128)} %all-reduce.7.cloned.1.call-done) | copy-start | bytes 3145732
  434.3 57.4 %copy-start.8 = (f32[64]{0:T(128)}, f32[64]{0:T(128)S(1)}, u32[]{:S(2)}) copy-start(f32[64]{0:T(128)S(1)} %select_reduce_fusion) | copy-start | bytes 772
  476.3 15.4 %copy-start.7 = (f32[512]{0:T(512)}, f32[512]{0:T(512)S(1)}, u32[]{:S(2)}) copy-start(f32[512]{0:T(512)S(1)} %psum.53) | copy-start | bytes 6148
Sparse Core Ops, SparseCore 0:
  11.6 56.2 all-reduce.4
  133.2 49.2 all-reduce.6
  184.5 53.9 all-gather.1
where the time goes:
time: 517 us; the launch traced here: 508 us
  blocking collectives  168 us (32%)
  waiting for transfers between devices  134 us (26%)
  other arithmetic  98.5 us (19%)
  starting transfers between devices  42.1 us (8%)
  local copies, waits for them, and re-layouts  27.5 us (5%)
  between operations  20 us (4%)
  matrix products  17.1 us (3%)
    psum x2, waiting for transfers between devices, broadcast(): return lax.psum(block, axis)  107 us
    psum x2, blocking collectives, residual_sum(): return lax.psum(jnp.sum(residual * residual), ('row', 'col'))  83.4 us
    psum x1, blocking collectives, per_device(): lax.psum(jnp.sum(direction * applied), ('row', 'col'))  42.9 us
    psum x1, blocking collectives, per_device(): county_totals = lax.psum(county_part, ('row', 'col'))  41.8 us
    another operation x6, other arithmetic, per_device(): factor = jnp.linalg.cholesky(diagonal)  33.9 us
    ppermute x8, starting transfers between devices, extended(): before = lax.ppermute(last, axis, up)  31.3 us
    another operation x3, other arithmetic, per_device(): jax.scipy.linalg.solve_triangular(factor, column.T, lower=True)  19.7 us
    ppermute x8, waiting for transfers between devices, extended(): after = lax.ppermute(initial, axis, down)  17.2 us
  transfers between devices with their start and end apart: 19, of which 14 were waited for; matrix products, arithmetic and copies ran while one was open for 10% of the time, Pallas kernels for 0%

commit v1 on v0

v1 whole, which is shorter than its diff:
```python
import functools
import jax
import jax.numpy as jnp
from jax import lax
from jax.experimental import pallas as pl
from jax.experimental.pallas import tpu as pltpu
from jax.sharding import PartitionSpec as P

BLOCK = 16
TRACTS_DEV = 64
COUNTIES = 512
STATES = 56
HALO = 4
PAD = 16
LANES = 128
HIGHEST = lax.Precision.HIGHEST
F32 = jnp.float32


def iota(shape, dim):
    return lax.broadcasted_iota(jnp.int32, shape, dim)


def dot(a, b, contract=(1, 0)):
    dims = (((contract[0],), (contract[1],)), ((), ()))
    return lax.dot_general(a, b, dims, precision=HIGHEST, preferred_element_type=F32)


def params(mib):
    return pltpu.CompilerParams(vmem_limit_bytes=mib << 20)


def pair_exchange(first, last, axis):
    size, odd = lax.axis_size(axis), lax.axis_index(axis) % 2 == 1
    near = [(i, i ^ 1) for i in range(size)]
    far = [(i, i + 1) for i in range(1, size - 1, 2)]
    far = far + [(j, i) for i, j in far]
    got_near = lax.ppermute(jnp.where(odd, first, last), axis, near)
    got_far = lax.ppermute(jnp.where(odd, last, first), axis, far)
    before = jnp.where(odd, got_near, got_far)
    after = jnp.where(odd, got_far, got_near)
    return before, after


def tree(block, axis, strides):
    size, index = lax.axis_size(axis), lax.axis_index(axis)
    for stride in strides:
        pairs = [(i, i + stride) for i in range(0, size, 2 * stride)]
        got = lax.ppermute(block, axis, pairs)
        block = jnp.where(index % (2 * stride) == stride, got, block)
    return block


def halvings(size):
    strides = []
    while size > 1:
        size //= 2
        strides.append(size)
    return strides


def spread_row(block, axis):
    size, index = lax.axis_size(axis), lax.axis_index(axis)
    strides = halvings(size)
    if len(strides) < 2:
        return tree(block, axis, strides)
    far, near = strides[:2]
    half = block.shape[0] // 2
    one, two = block[:half], block[half:]
    got_one = lax.ppermute(one, axis, [(0, near)])
    got_two = lax.ppermute(two, axis, [(0, far)])
    one = jnp.where(index == near, got_one, one)
    two = jnp.where(index == far, got_two, two)
    got_one = lax.ppermute(one, axis, [(0, far), (near, near + far)])
    got_two = lax.ppermute(two, axis, [(0, near), (far, near + far)])
    one = jnp.where(index % (2 * far) >= far, got_one, one)
    two = jnp.where((index == near) | (index == near + far), got_two, two)
    return tree(jnp.concatenate([one, two], axis=0), axis, strides[2:])


def raster_kernel(
    flags, b_hbm, k_hbm, above, below, sides, tracts, county, pay, sums, two, four,
    bx, kx, v1, v2, v3, rows_b, rows_2, sems
):
    rows, cols = two.shape
    wide = cols + 2 * LANES
    inner = (slice(PAD, PAD + rows), slice(LANES, LANES + cols))
    copy_b = pltpu.make_async_copy(b_hbm, bx.at[inner], sems.at[0])
    copy_k = pltpu.make_async_copy(k_hbm, kx.at[inner], sems.at[1])
    copy_b.start()
    copy_k.start()
    turned = sides[...].T
    lane = iota((rows, LANES), 1)
    for ref, left, right in (
        (bx, turned, turned),
        (kx, pltpu.roll(turned, HALO, 1), pltpu.roll(turned, LANES - HALO, 1)),
    ):
        ref[PAD - 8 : PAD, :] = jnp.zeros((8, wide), F32)
        ref[PAD + rows : PAD + rows + 8, :] = jnp.zeros((8, wide), F32)
        for start, part, keep in (
            (0, left, lane >= LANES - HALO),
            (LANES + cols, right, lane < HALO),
        ):
            own = slice(start, start + LANES)
            ref[PAD : PAD + rows, own] = jnp.where(keep, part[:rows], 0.0)
            keep = keep[:HALO]
            ref[PAD - HALO : PAD, own] = jnp.where(keep, part[rows : rows + HALO], 0.0)
            ref[PAD + rows : PAD + rows + HALO, own] = jnp.where(
                keep, part[rows + HALO : rows + 2 * HALO], 0.0
            )
    for ref, part in ((bx, slice(0, HALO)), (kx, slice(HALO, 2 * HALO))):
        ref[PAD - HALO : PAD, inner[1]] = above[part, :]
        ref[PAD + rows : PAD + rows + HALO, inner[1]] = below[part, :]
    copy_b.wait()
    copy_k.wait()

    column, sub = iota((8, wide), 1), iota((8, wide), 0)
    inside = jnp.logical_and(
        jnp.logical_or(column >= LANES, flags[2] > 0),
        jnp.logical_or(column < LANES + cols, flags[3] > 0),
    )

    def apply(src, row):
        centre = src[pl.ds(row, 8), :]
        up, down = src[pl.ds(row - 1, 1), :], src[pl.ds(row + 8, 1), :]
        beside = jnp.where(sub == 0, up, pltpu.roll(centre, 1, 0))
        beside = beside + jnp.where(sub == 7, down, pltpu.roll(centre, 7, 0))
        beside = beside + (pltpu.roll(centre, 1, 1) + pltpu.roll(centre, wide - 1, 1))
        out = (4.0 + kx[pl.ds(row, 8), :]) * centre - beside
        return centre[:, inner[1]], jnp.where(inside, out, 0.0)

    def edges(src, dst):
        for row, flag in ((PAD - 8, flags[0]), (PAD + rows, flags[1])):
            _, out = apply(src, row)
            dst[row : row + 8, :] = jnp.where(flag > 0, out, 0.0)

    def fold(value):
        return jnp.sum(value, axis=0, keepdims=True)

    def sweep_one(step, carry):
        sum_0, sum_1 = carry
        total = jnp.zeros((8, cols), F32)
        for part in range(2):
            row = pl.multiple_of(PAD + step * BLOCK + 8 * part, 8)
            centre, out = apply(bx, row)
            v1[pl.ds(row, 8), :] = out
            out = out[:, inner[1]]
            sum_0, sum_1 = sum_0 + centre * centre, sum_1 + out * out
            total = total + centre
        rows_b[pl.ds(step, 1), :] = fold(total)
        return sum_0, sum_1

    def sweep_two(step, sum_2):
        total = jnp.zeros((8, cols), F32)
        for part in range(2):
            row = pl.multiple_of(PAD + step * BLOCK + 8 * part, 8)
            _, out = apply(v1, row)
            v2[pl.ds(row, 8), :] = out
            out = out[:, inner[1]]
            two[pl.ds(row - PAD, 8), :] = out
            sum_2 = sum_2 + out * out
            total = total + out
        rows_2[pl.ds(step, 1), :] = fold(total)
        return sum_2

    def sweep_three(step, sum_3):
        row = pl.multiple_of(PAD + step * 8, 8)
        _, out = apply(v2, row)
        v3[pl.ds(row, 8), :] = out
        out = out[:, inner[1]]
        return sum_3 + out * out

    def sweep_four(step, carry):
        row = pl.multiple_of(PAD + step * 8, 8)
        _, out = apply(v3, row)
        four[pl.ds(row - PAD, 8), :] = out[:, inner[1]]
        return carry

    zero = jnp.zeros((8, cols), F32)
    edges(bx, v1)
    sum_0, sum_1 = lax.fori_loop(0, rows // BLOCK, sweep_one, (zero, zero))
    edges(v1, v2)
    sum_2 = lax.fori_loop(0, rows // BLOCK, sweep_two, zero)
    edges(v2, v3)
    sum_3 = lax.fori_loop(0, rows // 8, sweep_three, zero)
    lax.fori_loop(0, rows // 8, sweep_four, 0)

    pay[...] = jnp.zeros(pay.shape, F32)
    for index, value in enumerate((sum_0, sum_1, sum_2, sum_3)):
        value = fold(value)
        folded = value[:, :LANES]
        for start in range(LANES, cols, LANES):
            folded = folded + value[:, start : start + LANES]
        pay[8 + index : 9 + index, :] = folded

    group, place = iota((cols, LANES), 0) // BLOCK, iota((cols, LANES), 1)
    blocks = dot(rows_b[...], jnp.where(group == place, 1.0, 0.0))
    blocks = blocks + dot(rows_2[...], jnp.where(group + cols // BLOCK == place, 1.0, 0.0))
    for tract in range(TRACTS_DEV):
        sums[tract : tract + 1, :] = fold(jnp.where(tracts[...] == tract, blocks, 0.0))
    totals = sums[...]
    first = iota(totals.shape, 1) < cols // BLOCK
    for index, keep in enumerate((first, jnp.logical_not(first))):
        total = jnp.sum(jnp.where(keep, totals, 0.0), axis=1, keepdims=True)
        match = county[...] == iota((TRACTS_DEV, COUNTIES), 1)
        by_county = fold(jnp.where(match, total, 0.0))
        for part in range(COUNTIES // LANES):
            pay[4 * index + part : 4 * index + part + 1, :] = by_county[
                :, part * LANES : (part + 1) * LANES
            ]


def raster(flags, b, kappa, above, below, sides, tracts, county):
    rows, cols = b.shape
    shape = (rows + 2 * PAD, cols + 2 * LANES)
    any_spec = pl.BlockSpec(memory_space=pl.ANY)
    vmem = pl.BlockSpec(memory_space=pltpu.VMEM)
    return pl.pallas_call(
        raster_kernel,
        out_shape=(
            jax.ShapeDtypeStruct((16, LANES), F32),
            jax.ShapeDtypeStruct((TRACTS_DEV, LANES), F32),
            jax.ShapeDtypeStruct(b.shape, F32),
            jax.ShapeDtypeStruct(b.shape, F32),
        ),
        in_specs=[pl.BlockSpec(memory_space=pltpu.SMEM), any_spec, any_spec] + [vmem] * 5,
        out_specs=(vmem, vmem, vmem, vmem),
        scratch_shapes=[pltpu.VMEM(shape, F32)] * 5
        + [pltpu.VMEM((rows // BLOCK, cols), F32)] * 2
        + [pltpu.SemaphoreType.DMA((2,))],
        compiler_params=params(40),
        cost_estimate=pl.CostEstimate(flops=40 * rows * cols, transcendentals=0, bytes_accessed=16 * rows * cols),
        name="raster",
    )(flags, b, kappa, above, below, sides, tracts, county)


def two_sum(a, b):
    s = a + b
    t = s - a
    return s, (a - (s - t)) + (b - t)


def two_prod(a, b):
    def split(x):
        big = x * 4097.0
        high = big - (big - x)
        return high, x - high

    product = a * b
    a_high, a_low = split(a)
    b_high, b_low = split(b)
    low = ((a_high * b_high - product) + a_high * b_low + a_low * b_high) + a_low * b_low
    return product, low


def pair_add(a, b):
    high, low = two_sum(a[0], b[0])
    return two_sum(high, low + (a[1] + b[1]))


def pair_mul(a, b):
    high, low = two_prod(a[0], b[0])
    return two_sum(high, low + (a[0] * b[1] + a[1] * b[0]))


def pair_cross(a, b, c, d):
    minus = pair_mul(c, d)
    high, low = pair_add(pair_mul(a, b), (-minus[0], -minus[1]))
    return high + low


def finish_kernel(devices, got, sums, state, b, two, four, solution, residual, tract, county, states, scal):
    @pl.when(pl.program_id(0) == 0)
    def _():
        whole = got[0:16, :]
        err = jnp.zeros_like(whole)
        for device in range(1, devices):
            whole, low = two_sum(whole, got[16 * device : 16 * device + 16, :])
            err = err + low
        pair = (whole[8:12, :], err[8:12, :])
        shift = LANES // 2
        while shift:
            pair = pair_add(pair, (pltpu.roll(pair[0], shift, 1), pltpu.roll(pair[1], shift, 1)))
            shift //= 2
        scale = 1.0 / pair[0][0:1, :]
        m = []
        for index in range(4):
            m.append(pair_mul((scale, jnp.zeros_like(scale)), (pair[0][index : index + 1, :], pair[1][index : index + 1, :])))
        below = pair_cross(m[1], m[3], m[2], m[2])
        c_0 = pair_cross(m[0], m[3], m[1], m[2]) / below
        c_1 = pair_cross(m[0], m[2], m[1], m[1]) / below
        scal[0:1, :] = c_0
        scal[1:2, :] = c_1
        by_county = c_0 * whole[0:4, :] - c_1 * whole[4:8, :]
        county[...] = by_county
        place = iota((64, LANES), 0)
        total = jnp.zeros((64, LANES), F32)
        for part in range(COUNTIES // LANES):
            total = total + jnp.where(state[part : part + 1, :] == place, by_county[part : part + 1, :], 0.0)
        states[...] = dot(jnp.ones((8, LANES), F32), total, (1, 1))[0:1, :]
        first = iota((1, LANES), 1) < LANES // 2
        mixed = jnp.where(first, c_0, -c_1) * sums[...]
        tract[...] = dot(jnp.ones((8, LANES), F32), mixed, (1, 1))[0:1, :]

    c_0, c_1 = scal[0:1, 0:1], scal[1:2, 0:1]
    solution[...] = c_0 * b[...] - c_1 * two[...]
    residual[...] = b[...] - c_0 * two[...] + c_1 * four[...]


def finish(got, sums, state, b, two, four):
    rows, cols = b.shape
    step = 64
    devices = got.shape[0] // 16

    def fixed(shape):
        return pl.BlockSpec(shape, lambda i: (0, 0))

    tile = pl.BlockSpec((step, cols), lambda i: (i, 0))
    small = [(1, 64), (COUNTIES // LANES, LANES), (1, 64)]
    return pl.pallas_call(
        functools.partial(finish_kernel, devices),
        grid=(rows // step,),
        out_shape=[jax.ShapeDtypeStruct(b.shape, F32)] * 2
        + [jax.ShapeDtypeStruct(shape, F32) for shape in small],
        in_specs=[fixed(got.shape), fixed(sums.shape), fixed(state.shape), tile, tile, tile],
        out_specs=[tile, tile] + [fixed(shape) for shape in small],
        scratch_shapes=[pltpu.VMEM((8, LANES), F32)],
        compiler_params=params(24),
        cost_estimate=pl.CostEstimate(flops=6 * rows * cols, transcendentals=0, bytes_accessed=20 * rows * cols),
        name="finish",
    )(got, sums, state, b, two, four)


def invert_block(rows):
    size = LANES
    lane, sub = iota((8, size), 1), iota((8, size), 0)
    groups = size // 8
    pivots = [jnp.ones((8, size), F32)] * groups
    for k in range(size):
        g, s = divmod(k, 8)
        pivot = jnp.broadcast_to(rows[g][s : s + 1, k : k + 1], (8, size))
        line = jnp.broadcast_to(rows[g][s : s + 1, :], (8, size))
        scaled = jnp.where(lane == k, 1.0, line) * (1.0 / pivot)
        pivots[g] = jnp.where(sub == s, pivot, pivots[g])
        for h in range(g, groups):
            factor = jnp.broadcast_to(rows[h][:, k : k + 1], (8, size))
            updated = jnp.where(lane == k, 0.0, rows[h]) - factor * scaled
            rows[h] = jnp.where(sub > s, updated, rows[h]) if h == g else updated
    out = []
    for g in range(groups):
        row = sub + 8 * g
        kept = jnp.where(lane < row, rows[g], jnp.where(lane == row, 1.0, 0.0))
        out.append(kept / jnp.sqrt(pivots[g]))
    return out


def factor_kernel(a, inverse, part, left):
    size = LANES
    part[...] = a[0:size, 0:size]
    inverse[0:size, size:] = jnp.zeros((size, size), F32)

    def body(index, carry):
        rows = [part[8 * g : 8 * g + 8, :] for g in range(size // 8)]
        rows = invert_block(rows)
        for g in range(size // 8):
            part[8 * g : 8 * g + 8, :] = rows[g]

        @pl.when(index == 0)
        def _():
            first = part[...]
            inverse[0:size, 0:size] = first
            left[...] = dot(a[size:, 0:size], first, (1, 1))
            part[...] = a[size:, size:] - dot(left[...], left[...], (1, 1))

        return carry

    lax.fori_loop(0, 2, body, 0)
    inverse[size:, size:] = part[...]
    inverse[size:, 0:size] = -dot(part[...], dot(left[...], inverse[0:size, 0:size]))


def factor(a):
    size = a.shape[0]
    half = pltpu.VMEM((LANES, LANES), F32)
    return pl.pallas_call(
        factor_kernel,
        out_shape=jax.ShapeDtypeStruct(a.shape, F32),
        in_specs=[pl.BlockSpec(memory_space=pltpu.VMEM)],
        out_specs=pl.BlockSpec(memory_space=pltpu.VMEM),
        scratch_shapes=[half, half],
        compiler_params=params(16),
        cost_estimate=pl.CostEstimate(flops=200 * size * size * size, transcendentals=0, bytes_accessed=8 * size * size),
        name="factor",
    )(a)


def split(value):
    high = value.astype(jnp.bfloat16)
    return high, (value - high.astype(F32)).astype(jnp.bfloat16)


def update_kernel(column, wide, inverse, schur, panel, updated, other):
    size = inverse.shape[0]
    count = other.shape[0]

    @pl.when(pl.program_id(0) == 0)
    def _():
        for index in range(count):
            high, low = split(dot(inverse[...], wide[:, index, :]))
            other[index, 0:size, :] = high
            other[index, size : 2 * size, :] = low
            other[index, 2 * size :, :] = high

    own = dot(column[0], inverse[...], (1, 1))
    panel[0] = own
    high, low = split(own)
    lhs = jnp.concatenate([high, high, low], axis=1)
    for index in range(count):
        product = jnp.dot(lhs, other[index], preferred_element_type=F32)
        updated[0, :, index, :] = schur[0, :, index, :] - product


def update(column, wide, inverse, schur):
    count_rows, size, count, _ = schur.shape

    def step(*block):
        return pl.BlockSpec((1,) + block, lambda i: (i,) + (0,) * len(block))

    def fixed(shape):
        return pl.BlockSpec(shape, lambda i: (0,) * len(shape))

    panel, updated = pl.pallas_call(
        update_kernel,
        grid=(count_rows,),
        out_shape=(
            jax.ShapeDtypeStruct(column.shape, F32),
            jax.ShapeDtypeStruct(schur.shape, F32),
        ),
        in_specs=[step(size, size), fixed(wide.shape), fixed(inverse.shape), step(size, count, size)],
        out_specs=(step(size, size), step(size, count, size)),
        scratch_shapes=[pltpu.VMEM((count, 3 * size, size), jnp.bfloat16)],
        compiler_params=params(40),
        cost_estimate=pl.CostEstimate(flops=6 * schur.size * size, transcendentals=0, bytes_accessed=8 * schur.size),
        name="update",
    )(column, wide, inverse, schur)
    return panel, updated


def halo_messages(b, kappa):
    rows, cols = b.shape
    top = jnp.concatenate([b[:HALO], kappa[:HALO]], axis=0)
    bottom = jnp.concatenate([b[rows - HALO :], kappa[rows - HALO :]], axis=0)
    above, below = pair_exchange(top, bottom, "row")

    def strip(columns, which):
        field, at = ((b, 0), (kappa, HALO))[which]
        parts = [field[:, columns].T, above[at : at + HALO, columns].T, below[at : at + HALO, columns].T]
        return jnp.concatenate(parts, axis=1)

    first, last = slice(0, HALO), slice(cols - HALO, cols)
    left = jnp.concatenate([strip(first, 0), strip(first, 1)], axis=0)
    right = jnp.concatenate([strip(last, 1), strip(last, 0)], axis=0)
    before, after = pair_exchange(left, right, "col")
    length = before.shape[1]
    sides = jnp.zeros((LANES, -(-length // LANES) * LANES), F32)
    sides = sides.at[: 2 * HALO, :length].set(after)
    sides = sides.at[LANES - 2 * HALO :, :length].set(before)
    return above, below, sides


def per_device(right_side, kappa_sq, block_tract, tract_county, county_state, schur):
    n_row, n_col = lax.axis_size("row"), lax.axis_size("col")
    row, col = lax.axis_index("row"), lax.axis_index("col")
    above, below, sides = halo_messages(right_side, kappa_sq)
    flags = jnp.stack([row > 0, row < n_row - 1, col > 0, col < n_col - 1]).astype(jnp.int32)

    corner = tree(tree(schur[0, :, 0, :], "col", halvings(n_col)), "row", halvings(n_row))
    column = tree(schur[:, :, 0, :], "col", halvings(n_col))
    wide = spread_row(schur[0], "row")

    tracts = jnp.concatenate([block_tract, block_tract], axis=1)
    pay, sums, two, four = raster(
        flags, right_side, kappa_sq, above, below, sides, tracts, tract_county[:, None]
    )
    devices = n_row * n_col
    got = lax.all_to_all(jnp.broadcast_to(pay[None], (devices,) + pay.shape), ("row", "col"), 0, 0)
    inverse = factor(corner)
    solution, residual, tract_totals, county_totals, state_totals = finish(
        got.reshape(devices * 16, LANES),
        sums,
        county_state.reshape(COUNTIES // LANES, LANES),
        right_side,
        two,
        four,
    )
    panel, updated = update(column, wide, inverse, schur)
    return (
        solution,
        residual,
        tract_totals.reshape(-1)[:TRACTS_DEV],
        county_totals.reshape(-1),
        state_totals.reshape(-1)[:STATES],
        updated,
        panel,
    )


def solution(mesh):
    in_specs = (
        P("row", "col"),
        P("row", "col"),
        P("row", "col"),
        P(("row", "col")),
        P(),
        P(None, "row", None, "col"),
    )
    out_specs = (
        P("row", "col"),
        P("row", "col"),
        P(("row", "col")),
        P(),
        P(),
        P(None, "row", None, "col"),
        P(None, "row", None),
    )
    return jax.shard_map(
        per_device, mesh=mesh, in_specs=in_specs, out_specs=out_specs, check_vma=False
    )
```

time: 517 us -> 183 us (0.35); the launches traced: 508 us -> 182 us
  blocking collectives: 168 us -> 0 us
  waiting for transfers between devices: 134 us -> 10.3 us
  other arithmetic: 98.5 us -> 16.6 us
  Pallas kernels: 0 us -> 75.5 us
  between operations: 20 us -> 1.05 us
  matrix products: 17.1 us -> 0 us
    psum x4 -> x0, blocking collectives: 168 us -> none  [the longest x2 83.4 us: residual_sum(): return lax.psum(jnp.sum(residual * residual), ('row', 'col'))]
    psum x2 -> x0, waiting for transfers between devices: 107 us -> none  [broadcast(): return lax.psum(block, axis)]
    pallas_call x0 -> x4, Pallas kernels: none -> 75.5 us  [the longest x1 35.5 us: factor(): pl.pallas_call(factor_kernel, out_shape=jax.ShapeDtypeStruct(a.shape, F32...]
    another operation x9 -> x0, other arithmetic: 53.7 us -> none  [the longest x6 33.9 us: per_device(): factor = jnp.linalg.cholesky(diagonal)]
    reduce_sum x7 -> x0, other arithmetic: 26.8 us -> none  [the longest x2 15.5 us: per_device(): jnp.sum(direction * applied)]
    ppermute x16, waiting for transfers between devices: 27.4 us -> 10.3 us  [the longest x8 10.3 us: tree(): got = lax.ppermute(block, axis, pairs)]
    dot_general x1 -> x0, matrix products: 14.8 us -> none  [per_device(): jnp.einsum('ank,cmk->ancm', row_panel, col_panel, precision=lax.Precision...]
    select_n x3 -> x16, other arithmetic: 1.81 us -> 14.7 us  [the longest x8 7.58 us: tree(): block = jnp.where(index % (2 * stride) == stride, got, block)]
  transfers between devices with their start and end apart: 19 -> 17, of which waited for: 14 -> 1; matrix products, arithmetic and copies ran while one was open for 10% -> 21% of each run, Pallas kernels for 0% -> 34%
where the time goes in v1:
time: 183 us; the launch traced here: 182 us
  Pallas kernels  75.5 us (41%)
  starting transfers between devices  47 us (26%)
  local copies, waits for them, and re-layouts  31.1 us (17%)
  other arithmetic  16.6 us (9%)
  waiting for transfers between devices  10.3 us (6%)
    pallas_call x1, Pallas kernels, factor(): pl.pallas_call(factor_kernel, out_shape=jax.ShapeDtypeStruct(a.shape, F32...  35.5 us
    ppermute x8, starting transfers between devices, tree(): got = lax.ppermute(block, axis, pairs)  25.5 us
    pallas_call x1, Pallas kernels, raster(): pl.pallas_call(raster_kernel, out_shape=(jax.ShapeDtypeStruct((16, LANES)...  22.1 us
    unnamed x42, local copies, waits for them, and re-layouts  14 us
    pallas_call x1, Pallas kernels, update(): pl.pallas_call(update_kernel, grid=(count_rows,), out_shape=(jax.ShapeDty...  13.3 us
    ppermute x8, waiting for transfers between devices, tree(): got = lax.ppermute(block, axis, pairs)  10.3 us
    select_n x8, other arithmetic, tree(): block = jnp.where(index % (2 * stride) == stride, got, block)  7.58 us
    pallas_call x1, Pallas kernels, finish(): pl.pallas_call(functools.partial(finish_kernel, devices), grid=(rows // s...  4.56 us
  transfers between devices with their start and end apart: 17, of which 1 were waited for; matrix products, arithmetic and copies ran while one was open for 21% of the time, Pallas kernels for 34%

profile of v1, /device:TPU:0, one launch (start us, length us, event | category | flops | bytes accessed | tf_op | source)
XLA Modules:
  0.0 181.6 jit_solution(6229204018058681661)
XLA Ops:
  0.6 1.7 slice.141
  3.1 6.8 %collective-permute-start.11 = (f32[256,256]{1,0:T(8,128)}, f32[256,256]{1,0:T(8,128)}, u32[]{:S(2)}, u32[]{:S(2)}) collective-permute-start(f32[256,256]{1,0:T(8,128)} %bitcast.48), channel_id=1, source_target_pairs={{0,2},{4,6},{8,10},{12,14},{16,18},{20,22},{24,26},{28,30}} | collective-permute-start | bytes 786440 | tf_op jit(solution)/shard_map/ppermute | solution.py:49
  9.9 3.0 %slice_bitcast_fusion.1 = (f32[128,8,256]{2,1,0:T(8,128)}, f32[128,8,256]{2,1,0:T(8,128)}) fusion(f32[4,256,8,256]{3,2,1,0:T(8,128)} %schur.1), kind=kLoop, calls=%fused_computation.3 | loop fusion | bytes 4194304 | tf_op jit(solution)/shard_map/slice | solution.py:69
  12.9 4.5 %collective-permute-start.6 = (f32[128,8,256]{2,1,0:T(8,128)}, f32[128,8,256]{2,1,0:T(8,128)}, u32[]{:S(2)}, u32[]{:S(2)}) collective-permute-start(f32[128,8,256]{2,1,0:T(8,128)} %get-tuple-element.55), channel_id=1, source_target_pairs={{0,8},{1,9},{2,10},{3,11}} | collective-permute-start | bytes 3145736 | tf_op jit(solution)/shard_map/ppermute | solution.py:70
  17.4 2.3 %collective-permute-start.8 = (f32[128,8,256]{2,1,0:T(8,128)}, f32[128,8,256]{2,1,0:T(8,128)}, u32[]{:S(2)}, u32[]{:S(2)}) collective-permute-start(f32[128,8,256]{2,1,0:T(8,128)} %get-tuple-element.56), channel_id=1, source_target_pairs={{0,16},{1,17},{2,18},{3,19}} | collective-permute-start | bytes 3145736 | tf_op jit(solution)/shard_map/ppermute | solution.py:71
  19.7 0.8 fusion.3
  20.9 1.0 broadcast_select_fusion.9
  22.0 1.5 collective-permute-start.1
  23.5 1.9 %fusion = (f32[512,4]{1,0:T(8,128)}, f32[512,4]{1,0:T(8,128)}) fusion(f32[512,1024]{1,0:T(8,128)} %k_hbm.1), kind=kLoop, calls=%fused_computation.40 | loop fusion | bytes 32768 | tf_op jit(solution)/shard_map/slice | solution.py:457
  25.4 0.9 fusion.1
  26.4 3.9 %slice.136 = f32[4,256,1,256]{3,2,1,0:T(1,128)S(1)} slice(f32[4,256,8,256]{3,2,1,0:T(8,128)} %schur.1), slice={[0:4], [0:256], [0:1], [0:256]} | slice | bytes 2097152 | tf_op jit(solution)/shard_map/slice | solution.py:478
  30.5 1.3 copy.39
  31.7 1.1 copy.42
  32.8 1.1 copy.40
  33.9 1.1 copy.41
  34.9 1.1 copy.51
  36.0 2.3 %collective-permute-start.4 = (f32[4,256,256]{2,1,0:T(8,128)}, f32[4,256,256]{2,1,0:T(8,128)}, u32[]{:S(2)}, u32[]{:S(2)}) collective-permute-start(f32[4,256,256]{2,1,0:T(8,128)} %bitcast.53), channel_id=1, source_target_pairs={{0,2},{4,6},{8,10},{12,14},{16,18},{20,22},{24,26},{28,30}} | collective-permute-start | bytes 3145736 | tf_op jit(solution)/shard_map/ppermute | solution.py:49
  38.3 1.3 broadcast_select_fusion.7
  39.6 3.1 %broadcast_select_fusion.3 = (f32[128,8,256]{2,1,0:T(8,128)}, f32[128,8,256]{2,1,0:T(8,128)S(1)}) fusion(f32[128,8,256]{2,1,0:T(8,128)} %collective-permute-done.6, pred[]{:T(512)S(6)} %eq.45, f32[4,256,8,256]{3,2,1,0:T(8,128)} %schur.1, f32[128,8,256]{2,1,0:T(8,128)} %collective-permute-done.8, pred[]{:T(512)S(6)} %eq.47), kind=kLoop, calls=%fused_computation.7 | loop fusion | flops 524288 | bytes 6291458 | tf_op jit(solution)/shard_map/jit(_where)/select_n | solution.py:72
  42.7 3.5 %collective-permute-start.7 = (f32[128,8,256]{2,1,0:T(8,128)}, f32[128,8,256]{2,1,0:T(8,128)}, u32[]{:S(2)}, u32[]{:S(2)}) collective-permute-start(f32[128,8,256]{2,1,0:T(8,128)} %get-tuple-element.53), channel_id=1, source_target_pairs={{0,16},{8,24},{1,17},{9,25},{2,18},{10,26},{3,19},{11,27}} | collective-permute-start | bytes 3145736 | tf_op jit(solution)/shard_map/ppermute | solution.py:74
  46.3 4.0 %collective-permute-start.9 = (f32[128,8,256]{2,1,0:T(8,128)S(1)}, f32[128,8,256]{2,1,0:T(8,128)}, u32[]{:S(2)}, u32[]{:S(2)}) collective-permute-start(f32[128,8,256]{2,1,0:T(8,128)S(1)} %get-tuple-element.54), channel_id=1, source_target_pairs={{0,8},{16,24},{1,9},{17,25},{2,10},{18,26},{3,11},{19,27}} | collective-permute-start | bytes 3145736 | tf_op jit(solution)/shard_map/ppermute | solution.py:75
  50.3 0.7 broadcast_select_fusion.11
  51.0 2.0 %collective-permute-start.12 = (f32[256,256]{1,0:T(8,128)}, f32[256,256]{1,0:T(8,128)}, u32[]{:S(2)}, u32[]{:S(2)}) collective-permute-start(f32[256,256]{1,0:T(8,128)} %broadcast_select_fusion.11), channel_id=1, source_target_pairs={{0,1},{2,3},{4,5},{6,7},{8,9},{10,11},{12,13},{14,15},{16,17},{18,... | collective-permute-start | bytes 786440 | tf_op jit(solution)/shard_map/ppermute | solution.py:49
  53.1 1.2 copy.35.below
  54.3 1.2 copy.34.above
  56.4 10.3 %collective-permute-done.12 = f32[256,256]{1,0:T(8,128)} collective-permute-done((f32[256,256]{1,0:T(8,128)}, f32[256,256]{1,0:T(8,128)}, u32[]{:S(2)}, u32[]{:S(2)}) %collective-permute-start.12) | collective-permute-done | bytes 262176 | tf_op jit(solution)/shard_map/ppermute | solution.py:49
  66.6 2.5 %collective-permute-start.3 = (f32[8,520]{1,0:T(8,128)S(1)}, f32[8,520]{1,0:T(8,128)S(1)}, u32[]{:S(2)}, u32[]{:S(2)}) collective-permute-start(f32[8,520]{1,0:T(8,128)S(1)} %broadcast_select_fusion.18), channel_id=1, source_target_pairs={{0,1},{1,0},{2,3},{3,2},{4,5},{5,4},{6,7},{7,6},{8,9},{9,8},{10,11... | collective-permute-start | bytes 49928 | tf_op jit(solution)/shard_map/ppermute | solution.py:38
  69.1 1.7 broadcast_select_fusion.12
  70.8 2.4 %collective-permute-start.13 = (f32[256,256]{1,0:T(8,128)}, f32[256,256]{1,0:T(8,128)}, u32[]{:S(2)}, u32[]{:S(2)}) collective-permute-start(f32[256,256]{1,0:T(8,128)} %broadcast_select_fusion.12), channel_id=1, source_target_pairs={{0,16},{1,17},{2,18},{3,19}} | collective-permute-start | bytes 786440 | tf_op jit(solution)/shard_map/ppermute | solution.py:49
  73.2 1.4 broadcast_select_fusion.4
  74.8 1.7 pad_maximum_fusion
  76.5 2.6 %collective-permute-start.10 = (f32[256,8,256]{2,1,0:T(8,128)}, f32[256,8,256]{2,1,0:T(8,128)}, u32[]{:S(2)}, u32[]{:S(2)}) collective-permute-start(f32[256,8,256]{2,1,0:T(8,128)} %pad_maximum_fusion), channel_id=1, source_target_pairs={{0,4},{8,12},{16,20},{24,28},{1,5},{9,13},{17,21},{25,29},{2,6},{1... | collective-permute-start | bytes 6291464 | tf_op jit(solution)/shard_map/ppermute | solution.py:49
  79.7 1.6 copy-done.1
  81.3 22.1 %raster.1 = (f32[16,128]{1,0:T(8,128)S(1)}, f32[64,128]{1,0:T(8,128)S(1)}, f32[512,1024]{1,0:T(8,128)S(1)}, f32[512,1024]{1,0:T(8,128)S(1)}) custom-call(s32[4]{0:T(128)S(1)} %add_convert_fusion.flags, f32[512,1024]{1,0:T(8,128)S(1)} %copy-done, f32[512,1024]{1,0:T(8,128)S(1)} %copy-done.1, f32[8,1024]{1,0:T(8,128)S(1)} %copy.34.above, ...), custom_call_target="tpu_custom_call" | custom-call | flops 20971520 | bytes 8388608 | tf_op jit(solution)/shard_map/raster/pallas_call | solution.py:218
  103.5 1.3 copy-done.2
  104.8 1.3 copy-done.4
  106.8 2.6 %all-to-all-start = ((f32[32,16,128]{2,1,0:T(8,128)}), f32[32,16,128]{2,1,0:T(8,128)S(1)}, u32[]{:S(2)}, u32[]{:S(2)}) async-start(f32[32,16,128]{2,1,0:T(8,128)} %broadcast_in_dim.5), calls=%async_computation | async-start | bytes 524288 | tf_op jit(solution)/shard_map/all_to_all | solution.py:486
  109.4 1.0 broadcast_select_fusion.13
  110.4 3.6 %collective-permute-start.14 = (f32[256,256]{1,0:T(8,128)S(1)}, f32[256,256]{1,0:T(8,128)S(1)}, u32[]{:S(2)}, u32[]{:S(2)}) collective-permute-start(f32[256,256]{1,0:T(8,128)S(1)} %broadcast_select_fusion.13), channel_id=1, source_target_pairs={{0,8},{16,24},{1,9},{17,25},{2,10},{18,26},{3,11},{19,27}} | collective-permute-start | bytes 786440 | tf_op jit(solution)/shard_map/ppermute | solution.py:49
  114.0 2.4 %broadcast_select_fusion.5 = f32[4,256,256]{2,1,0:T(8,128)} fusion(f32[4,256,256]{2,1,0:T(8,128)} %collective-permute-done.4, pred[]{:T(512)S(6)} %eq.44, f32[4,256,1,256]{3,2,1,0:T(1,128)} %copy-done.7), kind=kLoop, calls=%fused_computation.9 | loop fusion | flops 262144 | bytes 3145729 | tf_op jit(solution)/shard_map/jit(_where)/select_n | solution.py:50
  116.4 4.4 %collective-permute-start.5 = (f32[4,256,256]{2,1,0:T(8,128)}, f32[4,256,256]{2,1,0:T(8,128)}, u32[]{:S(2)}, u32[]{:S(2)}) collective-permute-start(f32[4,256,256]{2,1,0:T(8,128)} %broadcast_select_fusion.5), channel_id=1, source_target_pairs={{0,1},{2,3},{4,5},{6,7},{8,9},{10,11},{12,13},{14,15},{16,17},{18,... | collective-permute-start | bytes 3145736 | tf_op jit(solution)/shard_map/ppermute | solution.py:49
  120.8 1.5 collective-permute-start.15
  122.3 1.6 copy-done.3
  123.9 1.6 copy-done.5
  125.5 4.6 %finish.1 = (f32[512,1024]{1,0:T(8,128)}, f32[512,1024]{1,0:T(8,128)}, f32[1,64]{1,0:T(1,128)}, f32[4,128]{1,0:T(4,128)}, f32[1,64]{1,0:T(1,128)S(1)}) custom-call(f32[512,128]{1,0:T(8,128)S(1)} %bitcast.51, f32[64,128]{1,0:T(8,128)S(1)} %get-tuple-element.43.sums, s32[4,128]{1,0:T(4,128)S(1)} %bitcast.52, f32[512,1024]{1,0:T(8,128)S(1)} %copy-done, ...), custom_call_target="tpu_custom_call" | custom-call | flops 3145728 | bytes 10485760 | tf_op jit(solution)/shard_map/finish/pallas_call | solution.py:320
  130.6 35.5 %factor.1.inverse = f32[256,256]{1,0:T(8,128)S(1)} custom-call(f32[256,256]{1,0:T(8,128)S(1)} %broadcast_select_fusion.15.a), custom_call_target="tpu_custom_call" | custom-call | flops 3355443200 | bytes 524288 | tf_op jit(solution)/shard_map/factor/pallas_call | solution.py:385
  166.2 1.5 broadcast_select_fusion.6.column
  168.3 13.3 %update.1 = (f32[4,256,256]{2,1,0:T(8,128)}, f32[4,256,8,256]{3,2,1,0:T(8,128)}) custom-call(f32[4,256,256]{2,1,0:T(8,128)S(1)} %broadcast_select_fusion.6.column, f32[256,8,256]{2,1,0:T(8,128)S(1)} %broadcast_select_fusion.wide, f32[256,256]{1,0:T(8,128)S(1)} %factor.1.inverse, f32[4,256,8,256]{3,2,1,0:T(8,128)S(1)} %bitcast.50), custom_call_target="tpu_custom_call" | custom-call | flops 3221225472 | bytes 16777216 | tf_op jit(solution)/shard_map/update/pallas_call | solution.py:432
  (71 shorter events, 5.0 us)
Async XLA Ops:
  3.1 17.4 %copy-start = (f32[512,1024]{1,0:T(8,128)S(1)}, f32[512,1024]{1,0:T(8,128)}, u32[]{:S(2)}) copy-start(f32[512,1024]{1,0:T(8,128)} %b.1) | copy-start | bytes 6291460
  3.1 47.2 %collective-permute-start.11 = (f32[256,256]{1,0:T(8,128)}, f32[256,256]{1,0:T(8,128)}, u32[]{:S(2)}, u32[]{:S(2)}) collective-permute-start(f32[256,256]{1,0:T(8,128)} %bitcast.48), channel_id=1, source_target_pairs={{0,2},{4,6},{8,10},{12,14},{16,18},{20,22},{24,26},{28,30}} | collective-permute-start | bytes 786440 | tf_op jit(solution)/shard_map/ppermute | solution.py:49
  12.9 10.6 %copy-start.14 = (s32[32,64]{1,0:T(8,128)S(1)}, s32[32,64]{1,0:T(8,128)}, u32[]{:S(2)}) copy-start(s32[32,64]{1,0:T(8,128)} %param.12) | copy-start | bytes 24580
  12.9 26.7 %collective-permute-start.6 = (f32[128,8,256]{2,1,0:T(8,128)}, f32[128,8,256]{2,1,0:T(8,128)}, u32[]{:S(2)}, u32[]{:S(2)}) collective-permute-start(f32[128,8,256]{2,1,0:T(8,128)} %get-tuple-element.55), channel_id=1, source_target_pairs={{0,8},{1,9},{2,10},{3,11}} | collective-permute-start | bytes 3145736 | tf_op jit(solution)/shard_map/ppermute | solution.py:70
  17.4 22.2 %collective-permute-start.8 = (f32[128,8,256]{2,1,0:T(8,128)}, f32[128,8,256]{2,1,0:T(8,128)}, u32[]{:S(2)}, u32[]{:S(2)}) collective-permute-start(f32[128,8,256]{2,1,0:T(8,128)} %get-tuple-element.56), channel_id=1, source_target_pairs={{0,16},{1,17},{2,18},{3,19}} | collective-permute-start | bytes 3145736 | tf_op jit(solution)/shard_map/ppermute | solution.py:71
  22.0 14.0 %collective-permute-start.1 = (f32[8,1024]{0,1:T(8,128)}, f32[8,1024]{0,1:T(8,128)}, u32[]{:S(2)}, u32[]{:S(2)}) collective-permute-start(f32[8,1024]{0,1:T(8,128)} %get-tuple-element.67), channel_id=1, source_target_pairs={{4,8},{12,16},{20,24},{8,4},{16,12},{24,20},{5,9},{13,17},{21,25},... | collective-permute-start | bytes 98312 | tf_op jit(solution)/shard_map/ppermute | solution.py:39
  23.4 14.8 %collective-permute-start = (f32[8,1024]{0,1:T(8,128)}, f32[8,1024]{0,1:T(8,128)}, u32[]{:S(2)}, u32[]{:S(2)}) collective-permute-start(f32[8,1024]{0,1:T(8,128)} %get-tuple-element.68), channel_id=1, source_target_pairs={{0,4},{4,0},{8,12},{12,8},{16,20},{20,16},{24,28},{28,24},{1,5},{5... | collective-permute-start | bytes 98312 | tf_op jit(solution)/shard_map/ppermute | solution.py:38
  23.5 6.9 %copy-start.15 = (s32[64]{0:T(128)S(1)}, s32[64]{0:T(128)}, u32[]{:S(2)}) copy-start(s32[64]{0:T(128)} %param.13) | copy-start | bytes 772
  30.3 9.2 %copy-start.7 = (f32[4,256,1,256]{3,2,1,0:T(1,128)}, f32[4,256,1,256]{3,2,1,0:T(1,128)S(1)}, u32[]{:S(2)}) copy-start(f32[4,256,1,256]{3,2,1,0:T(1,128)S(1)} %slice.136) | copy-start | bytes 3145732
  36.0 78.0 %collective-permute-start.4 = (f32[4,256,256]{2,1,0:T(8,128)}, f32[4,256,256]{2,1,0:T(8,128)}, u32[]{:S(2)}, u32[]{:S(2)}) collective-permute-start(f32[4,256,256]{2,1,0:T(8,128)} %bitcast.53), channel_id=1, source_target_pairs={{0,2},{4,6},{8,10},{12,14},{16,18},{20,22},{24,26},{28,30}} | collective-permute-start | bytes 3145736 | tf_op jit(solution)/shard_map/ppermute | solution.py:49
  39.5 6.6 %copy-start.13 = (f32[8,1024]{0,1:T(8,128)}, f32[8,1024]{0,1:T(8,128)S(1)}, u32[]{:S(2)}) copy-start(f32[8,1024]{0,1:T(8,128)S(1)} %get-tuple-element.65) | copy-start | bytes 98308
  39.6 13.5 %copy-start.12 = (f32[8,1024]{0,1:T(8,128)}, f32[8,1024]{0,1:T(8,128)S(1)}, u32[]{:S(2)}) copy-start(f32[8,1024]{0,1:T(8,128)S(1)} %get-tuple-element.66) | copy-start | bytes 98308
  42.7 28.1 %collective-permute-start.7 = (f32[128,8,256]{2,1,0:T(8,128)}, f32[128,8,256]{2,1,0:T(8,128)}, u32[]{:S(2)}, u32[]{:S(2)}) collective-permute-start(f32[128,8,256]{2,1,0:T(8,128)} %get-tuple-element.53), channel_id=1, source_target_pairs={{0,16},{8,24},{1,17},{9,25},{2,18},{10,26},{3,19},{11,27}} | collective-permute-start | bytes 3145736 | tf_op jit(solution)/shard_map/ppermute | solution.py:74
  46.3 28.3 %collective-permute-start.9 = (f32[128,8,256]{2,1,0:T(8,128)S(1)}, f32[128,8,256]{2,1,0:T(8,128)}, u32[]{:S(2)}, u32[]{:S(2)}) collective-permute-start(f32[128,8,256]{2,1,0:T(8,128)S(1)} %get-tuple-element.54), channel_id=1, source_target_pairs={{0,8},{16,24},{1,9},{17,25},{2,10},{18,26},{3,11},{19,27}} | collective-permute-start | bytes 3145736 | tf_op jit(solution)/shard_map/ppermute | solution.py:75
  51.0 15.6 %collective-permute-start.12 = (f32[256,256]{1,0:T(8,128)}, f32[256,256]{1,0:T(8,128)}, u32[]{:S(2)}, u32[]{:S(2)}) collective-permute-start(f32[256,256]{1,0:T(8,128)} %broadcast_select_fusion.11), channel_id=1, source_target_pairs={{0,1},{2,3},{4,5},{6,7},{8,9},{10,11},{12,13},{14,15},{16,17},{18,... | collective-permute-start | bytes 786440 | tf_op jit(solution)/shard_map/ppermute | solution.py:49
  55.6 23.6 %collective-permute-start.2 = (f32[8,520]{1,0:T(8,128)S(1)}, f32[8,520]{1,0:T(8,128)S(1)}, u32[]{:S(2)}, u32[]{:S(2)}) collective-permute-start(f32[8,520]{1,0:T(8,128)S(1)} %broadcast_select_fusion.19), channel_id=1, source_target_pairs={{1,2},{2,1},{5,6},{6,5},{9,10},{10,9},{13,14},{14,13},{17,18},{18,... | collective-permute-start | bytes 49928 | tf_op jit(solution)/shard_map/ppermute | solution.py:39
  66.6 12.6 %collective-permute-start.3 = (f32[8,520]{1,0:T(8,128)S(1)}, f32[8,520]{1,0:T(8,128)S(1)}, u32[]{:S(2)}, u32[]{:S(2)}) collective-permute-start(f32[8,520]{1,0:T(8,128)S(1)} %broadcast_select_fusion.18), channel_id=1, source_target_pairs={{0,1},{1,0},{2,3},{3,2},{4,5},{5,4},{6,7},{7,6},{8,9},{9,8},{10,11... | collective-permute-start | bytes 49928 | tf_op jit(solution)/shard_map/ppermute | solution.py:38
  70.8 38.6 %collective-permute-start.13 = (f32[256,256]{1,0:T(8,128)}, f32[256,256]{1,0:T(8,128)}, u32[]{:S(2)}, u32[]{:S(2)}) collective-permute-start(f32[256,256]{1,0:T(8,128)} %broadcast_select_fusion.12), channel_id=1, source_target_pairs={{0,16},{1,17},{2,18},{3,19}} | collective-permute-start | bytes 786440 | tf_op jit(solution)/shard_map/ppermute | solution.py:49
  74.6 1.9 %copy-start.8 = (f32[128,8,256]{2,1,0:T(8,128)}, f32[128,8,256]{2,1,0:T(8,128)S(1)}, u32[]{:S(2)}) copy-start(f32[128,8,256]{2,1,0:T(8,128)S(1)} %broadcast_select_fusion.4) | copy-start | bytes 3145732
  74.8 1.8 copy-start.10
  76.5 91.2 %collective-permute-start.10 = (f32[256,8,256]{2,1,0:T(8,128)}, f32[256,8,256]{2,1,0:T(8,128)}, u32[]{:S(2)}, u32[]{:S(2)}) collective-permute-start(f32[256,8,256]{2,1,0:T(8,128)} %pad_maximum_fusion), channel_id=1, source_target_pairs={{0,4},{8,12},{16,20},{24,28},{1,5},{9,13},{17,21},{25,29},{2,6},{1... | collective-permute-start | bytes 6291464 | tf_op jit(solution)/shard_map/ppermute | solution.py:49
  79.7 1.6 copy-start.1
  103.5 1.3 copy-start.2
  104.8 1.3 copy-start.4
  106.8 15.5 %all-to-all-start = ((f32[32,16,128]{2,1,0:T(8,128)}), f32[32,16,128]{2,1,0:T(8,128)S(1)}, u32[]{:S(2)}, u32[]{:S(2)}) async-start(f32[32,16,128]{2,1,0:T(8,128)} %broadcast_in_dim.5), calls=%async_computation | async-start | bytes 524288 | tf_op jit(solution)/shard_map/all_to_all | solution.py:486
  110.4 11.9 %copy-start.6 = (s32[512]{0:T(512)S(1)}, s32[512]{0:T(512)}, u32[]{:S(2)}) copy-start(s32[512]{0:T(512)} %param.14) | copy-start | bytes 6148
  110.4 10.3 %collective-permute-start.14 = (f32[256,256]{1,0:T(8,128)S(1)}, f32[256,256]{1,0:T(8,128)S(1)}, u32[]{:S(2)}, u32[]{:S(2)}) collective-permute-start(f32[256,256]{1,0:T(8,128)S(1)} %broadcast_select_fusion.13), channel_id=1, source_target_pairs={{0,8},{16,24},{1,9},{17,25},{2,10},{18,26},{3,11},{19,27}} | collective-permute-start | bytes 786440 | tf_op jit(solution)/shard_map/ppermute | solution.py:49
  116.4 49.8 %collective-permute-start.5 = (f32[4,256,256]{2,1,0:T(8,128)}, f32[4,256,256]{2,1,0:T(8,128)}, u32[]{:S(2)}, u32[]{:S(2)}) collective-permute-start(f32[4,256,256]{2,1,0:T(8,128)} %broadcast_select_fusion.5), channel_id=1, source_target_pairs={{0,1},{2,3},{4,5},{6,7},{8,9},{10,11},{12,13},{14,15},{16,17},{18,... | collective-permute-start | bytes 3145736 | tf_op jit(solution)/shard_map/ppermute | solution.py:49
  120.8 9.8 %collective-permute-start.15 = (f32[256,256]{1,0:T(8,128)S(1)}, f32[256,256]{1,0:T(8,128)S(1)}, u32[]{:S(2)}, u32[]{:S(2)}) collective-permute-start(f32[256,256]{1,0:T(8,128)S(1)} %broadcast_select_fusion.14), channel_id=1, source_target_pairs={{0,4},{8,12},{16,20},{24,28},{1,5},{9,13},{17,21},{25,29},{2,6},{1... | collective-permute-start | bytes 786440 | tf_op jit(solution)/shard_map/ppermute | solution.py:49
  122.3 1.6 copy-start.3
  123.9 1.6 copy-start.5
  130.6 37.6 %slice-start = ((s8[8388608]{0:T(1024)(128)(4,1)}), s8[4194304]{0:T(1024)(128)(4,1)S(1)}, s32[]{:S(2)}) async-start(s8[8388608]{0:T(1024)(128)(4,1)} %bitcast.49), calls=%async_computation.1 | async-start | bytes 8388608
  130.6 37.6 %slice-start.1 = ((s8[8388608]{0:T(1024)(128)(4,1)}), s8[4194304]{0:T(1024)(128)(4,1)S(1)}, s32[]{:S(2)}) async-start(s8[8388608]{0:T(1024)(128)(4,1)} %bitcast.49), calls=%async_computation.2 | async-start | bytes 8388608
  166.2 1.6 copy-start.9
  166.2 1.8 %copy-start.11 = (f32[128,8,256]{2,1,0:T(8,128)S(1)}, f32[128,8,256]{2,1,0:T(8,128)}, u32[]{:S(2)}) copy-start(f32[128,8,256]{2,1,0:T(8,128)} %copy-done.10) | copy-start | bytes 3145732

commit v2 on v1

--- a/solution.py
+++ b/solution.py
@@ -26,60 +26,209 @@
     return lax.dot_general(a, b, dims, precision=HIGHEST, preferred_element_type=F32)
 
 
+def cost(micros):
+    return pl.CostEstimate(flops=micros * 10**9, transcendentals=0, bytes_accessed=1 << 10)
+
+
 def params(mib):
     return pltpu.CompilerParams(vmem_limit_bytes=mib << 20)
 
 
-def pair_exchange(first, last, axis):
-    size, odd = lax.axis_size(axis), lax.axis_index(axis) % 2 == 1
-    near = [(i, i ^ 1) for i in range(size)]
-    far = [(i, i + 1) for i in range(1, size - 1, 2)]
-    far = far + [(j, i) for i, j in far]
-    got_near = lax.ppermute(jnp.where(odd, first, last), axis, near)
-    got_far = lax.ppermute(jnp.where(odd, last, first), axis, far)
-    before = jnp.where(odd, got_near, got_far)
-    after = jnp.where(odd, got_far, got_near)
-    return before, after
-
-
-def tree(block, axis, strides):
-    size, index = lax.axis_size(axis), lax.axis_index(axis)
-    for stride in strides:
-        pairs = [(i, i + stride) for i in range(0, size, 2 * stride)]
-        got = lax.ppermute(block, axis, pairs)
-        block = jnp.where(index % (2 * stride) == stride, got, block)
-    return block
-
-
-def halvings(size):
-    strides = []
-    while size > 1:
-        size //= 2
-        strides.append(size)
-    return strides
-
-
-def spread_row(block, axis):
-    size, index = lax.axis_size(axis), lax.axis_index(axis)
-    strides = halvings(size)
-    if len(strides) < 2:
-        return tree(block, axis, strides)
-    far, near = strides[:2]
-    half = block.shape[0] // 2
-    one, two = block[:half], block[half:]
-    got_one = lax.ppermute(one, axis, [(0, near)])
-    got_two = lax.ppermute(two, axis, [(0, far)])
-    one = jnp.where(index == near, got_one, one)
-    two = jnp.where(index == far, got_two, two)
-    got_one = lax.ppermute(one, axis, [(0, far), (near, near + far)])
-    got_two = lax.ppermute(two, axis, [(0, near), (far, near + far)])
-    one = jnp.where(index % (2 * far) >= far, got_one, one)
-    two = jnp.where((index == near) | (index == near + far), got_two, two)
-    return tree(jnp.concatenate([one, two], axis=0), axis, strides[2:])
+def trade(near, far, axis):
+    size = lax.axis_size(axis)
+    inside = [(i, i ^ 1) for i in range(size)]
+    between = [(i, i + 1) for i in range(1, size - 1, 2)]
+    between = between + [(j, i) for i, j in between]
+    return lax.ppermute(near, axis, inside), lax.ppermute(far, axis, between)
+
+
+def after(value, *others):
+    return lax.optimization_barrier((value,) + others)[0]
+
+
+def hop(block, axis, stride):
+    pairs = [(i, i + stride // 2) for i in range(0, lax.axis_size(axis), stride)]
+    return lax.ppermute(block, axis, pairs)
+
+
+def relay(source, held, target, sem):
+    copy = pltpu.make_async_copy(source, held, sem)
+    copy.start()
+    copy.wait()
+    copy = pltpu.make_async_copy(held, target, sem)
+    copy.start()
+    copy.wait()
+
+
+def merge_kernel(flag, got, _, out, held, sem):
+    @pl.when(flag[0] > 0)
+    def _():
+        relay(got, held, out, sem)
+
+
+def merge(got, block, axis, stride):
+    flag = (lax.axis_index(axis) % stride == stride // 2).astype(jnp.int32).reshape(1)
+    any_spec = pl.BlockSpec(memory_space=pl.ANY)
+    return pl.pallas_call(
+        merge_kernel,
+        out_shape=jax.ShapeDtypeStruct(block.shape, block.dtype),
+        in_specs=[pl.BlockSpec(memory_space=pltpu.SMEM), any_spec, any_spec],
+        out_specs=any_spec,
+        scratch_shapes=[pltpu.VMEM(block.shape, F32), pltpu.SemaphoreType.DMA],
+        input_output_aliases={2: 0},
+        compiler_params=params(60),
+        cost_estimate=cost(2),
+        name="merge",
+    )(flag, got, block)
+
+
+def extract_kernel(schur, raw, wide, held_raw, held_wide, sems):
+    parts = ((schur.at[:, :, 0, :], held_raw, raw), (schur.at[0], held_wide, wide))
+    loads = [pltpu.make_async_copy(a, b, sems.at[i]) for i, (a, b, _) in enumerate(parts)]
+    stores = [pltpu.make_async_copy(b, c, sems.at[2 + i]) for i, (_, b, c) in enumerate(parts)]
+    for copy in loads:
+        copy.start()
+    for load, store in zip(loads, stores):
+        load.wait()
+        store.start()
+    for copy in stores:
+        copy.wait()
+
+
+def corner_block_kernel(schur, corner, sem):
+    copy = pltpu.make_async_copy(schur.at[0, :, 0, :], corner, sem)
+    copy.start()
+    copy.wait()
+
+
+def corner_block(schur):
+    size = schur.shape[1]
+    return pl.pallas_call(
+        corner_block_kernel,
+        out_shape=jax.ShapeDtypeStruct((size, size), F32),
+        in_specs=[pl.BlockSpec(memory_space=pl.ANY)],
+        out_specs=pl.BlockSpec(memory_space=pltpu.VMEM),
+        scratch_shapes=[pltpu.SemaphoreType.DMA],
+        compiler_params=params(60),
+        cost_estimate=cost(2),
+        name="corner",
+    )(schur)
+
+
+def extract(schur):
+    count_rows, size, count, _ = schur.shape
+    any_spec = pl.BlockSpec(memory_space=pl.ANY)
+    return pl.pallas_call(
+        extract_kernel,
+        out_shape=(
+            jax.ShapeDtypeStruct((count_rows, size, size), F32),
+            jax.ShapeDtypeStruct((size, count, size), F32),
+        ),
+        in_specs=[any_spec],
+        out_specs=(any_spec, any_spec),
+        scratch_shapes=[
+            pltpu.VMEM((count_rows, size, size), F32),
+            pltpu.VMEM((size, count, size), F32),
+            pltpu.SemaphoreType.DMA((4,)),
+        ],
+        compiler_params=params(60),
+        cost_estimate=cost(3),
+        name="extract",
+    )(schur)
+
+
+def small_steps(n_row, n_col):
+    steps = []
+    for axis, stride in (("col", n_col), ("row", n_row)):
+        while stride > 1:
+            steps.append((axis, stride))
+            stride //= 2
+    return steps
+
+
+def small_hop(block, step):
+    axis, stride = step
+    got = hop(block, axis, stride)
+    return jnp.where(lax.axis_index(axis) % stride == stride // 2, got, block)
+
+
+def exchange(mine):
+    axes = ("row", "col")
+    devices = lax.axis_size("row") * lax.axis_size("col")
+    return lax.all_to_all(jnp.broadcast_to(mine, (devices,) + mine.shape), axes, 0, 0)
+
+
+def edge_kernel(flags, b_top, b_low, k_top, k_low, b_left, b_right, k_left, k_right, near, far, left, right):
+    odd = flags[4] > 0
+    for part, top, low in ((slice(0, HALO), b_top, b_low), (slice(HALO, 2 * HALO), k_top, k_low)):
+        first, last = top[0:HALO, :], low[8 - HALO : 8, :]
+        near[part, :] = jnp.where(odd, first, last)
+        far[part, :] = jnp.where(odd, last, first)
+    left[0:HALO, :] = b_left[...].T[0:HALO]
+    left[HALO:, :] = k_left[...].T[0:HALO]
+    right[0:HALO, :] = k_right[...].T[LANES - HALO :]
+    right[HALO:, :] = b_right[...].T[LANES - HALO :]
+
+
+def edge_messages(flags, b, kappa):
+    rows, cols = b.shape
+
+    def spec(shape, row, col):
+        return pl.BlockSpec(shape, lambda i: (row, col))
+
+    ends = [spec((8, cols), 0, 0), spec((8, cols), rows // 8 - 1, 0)]
+    sides = [spec((rows, LANES), 0, 0), spec((rows, LANES), 0, cols // LANES - 1)]
+    shapes = [(8, cols), (8, cols), (8, rows), (8, rows)]
+    return pl.pallas_call(
+        edge_kernel,
+        grid=(1,),
+        out_shape=[jax.ShapeDtypeStruct(shape, F32) for shape in shapes],
+        in_specs=[pl.BlockSpec(memory_space=pltpu.SMEM)] + ends * 2 + sides * 2,
+        out_specs=[spec(shape, 0, 0) for shape in shapes],
+        compiler_params=params(60),
+        cost_estimate=cost(2),
+        name="edges",
+    )(flags, b, b, kappa, kappa, b, b, kappa, kappa)
+
+
+def corner_kernel(flags, got_near, got_far, left, right, above, below, near, far):
+    odd, odd_col = flags[4] > 0, flags[5] > 0
+    above[...] = jnp.where(odd, got_near[...], got_far[...])
+    below[...] = jnp.where(odd, got_far[...], got_near[...])
+    cols, rows = above.shape[1], left.shape[1]
+    filler = jnp.zeros((LANES - 8, LANES), F32)
+
+    def turned(ref, start):
+        return jnp.concatenate([ref[:, start : start + LANES], filler], axis=0).T
+
+    def choose(at, first, last):
+        near[:, at] = jnp.where(odd_col, first, last)
+        far[:, at] = jnp.where(odd_col, last, first)
+
+    choose(slice(0, rows), left[...], right[...])
+    for index, ref in enumerate((above, below)):
+        first = turned(ref, 0)[0:8]
+        last = turned(ref, cols - LANES)[LANES - 8 :]
+        choose(slice(rows + index * LANES, rows + (index + 1) * LANES), first, last)
+
+
+def corner_messages(flags, got_near, got_far, left, right):
+    rows = left.shape[1]
+    vmem = pl.BlockSpec(memory_space=pltpu.VMEM)
+    shapes = [got_near.shape, got_near.shape, (8, rows + 2 * LANES), (8, rows + 2 * LANES)]
+    return pl.pallas_call(
+        corner_kernel,
+        out_shape=[jax.ShapeDtypeStruct(shape, F32) for shape in shapes],
+        in_specs=[pl.BlockSpec(memory_space=pltpu.SMEM)] + [vmem] * 4,
+        out_specs=[vmem] * 4,
+        compiler_params=params(2),
+        cost_estimate=cost(1),
+        name="corners",
+    )(flags, got_near, got_far, left, right)
 
 
 def raster_kernel(
-    flags, b_hbm, k_hbm, above, below, sides, tracts, county, pay, sums, two, four,
+    flags, b_hbm, k_hbm, above, below, got_near, got_far, tracts, county, pay, sums, two, four,
     bx, kx, v1, v2, v3, rows_b, rows_2, sems
 ):
     rows, cols = two.shape
@@ -89,11 +238,15 @@
     copy_k = pltpu.make_async_copy(k_hbm, kx.at[inner], sems.at[1])
     copy_b.start()
     copy_k.start()
-    turned = sides[...].T
+    odd = flags[5] > 0
+    before = jnp.where(odd, got_near[...], got_far[...])
+    after = jnp.where(odd, got_far[...], got_near[...])
+    filler = jnp.zeros((LANES - 16, before.shape[1]), F32)
+    turned = jnp.concatenate([after, filler, before], axis=0).T
     lane = iota((rows, LANES), 1)
-    for ref, left, right in (
-        (bx, turned, turned),
-        (kx, pltpu.roll(turned, HALO, 1), pltpu.roll(turned, LANES - HALO, 1)),
+    for ref, left, right, skip in (
+        (bx, turned, turned, 0),
+        (kx, pltpu.roll(turned, HALO, 1), pltpu.roll(turned, LANES - HALO, 1), HALO),
     ):
         ref[PAD - 8 : PAD, :] = jnp.zeros((8, wide), F32)
         ref[PAD + rows : PAD + rows + 8, :] = jnp.zeros((8, wide), F32)
@@ -104,10 +257,9 @@
             own = slice(start, start + LANES)
             ref[PAD : PAD + rows, own] = jnp.where(keep, part[:rows], 0.0)
             keep = keep[:HALO]
-            ref[PAD - HALO : PAD, own] = jnp.where(keep, part[rows : rows + HALO], 0.0)
-            ref[PAD + rows : PAD + rows + HALO, own] = jnp.where(
-                keep, part[rows + HALO : rows + 2 * HALO], 0.0
-            )
+            for place, at in ((PAD - HALO, rows), (PAD + rows, rows + LANES)):
+                corner = turned[at + skip : at + skip + HALO]
+                ref[place : place + HALO, own] = jnp.where(keep, corner, 0.0)
     for ref, part in ((bx, slice(0, HALO)), (kx, slice(HALO, 2 * HALO))):
         ref[PAD - HALO : PAD, inner[1]] = above[part, :]
         ref[PAD + rows : PAD + rows + HALO, inner[1]] = below[part, :]
@@ -210,7 +362,7 @@
             ]
 
 
-def raster(flags, b, kappa, above, below, sides, tracts, county):
+def raster(flags, b, kappa, above, below, got_near, got_far, tracts, county):
     rows, cols = b.shape
     shape = (rows + 2 * PAD, cols + 2 * LANES)
     any_spec = pl.BlockSpec(memory_space=pl.ANY)
@@ -223,15 +375,15 @@
             jax.ShapeDtypeStruct(b.shape, F32),
             jax.ShapeDtypeStruct(b.shape, F32),
         ),
-        in_specs=[pl.BlockSpec(memory_space=pltpu.SMEM), any_spec, any_spec] + [vmem] * 5,
+        in_specs=[pl.BlockSpec(memory_space=pltpu.SMEM), any_spec, any_spec] + [vmem] * 6,
         out_specs=(vmem, vmem, vmem, vmem),
         scratch_shapes=[pltpu.VMEM(shape, F32)] * 5
         + [pltpu.VMEM((rows // BLOCK, cols), F32)] * 2
         + [pltpu.SemaphoreType.DMA((2,))],
-        compiler_params=params(40),
-        cost_estimate=pl.CostEstimate(flops=40 * rows * cols, transcendentals=0, bytes_accessed=16 * rows * cols),
+        compiler_params=params(60),
+        cost_estimate=cost(25),
         name="raster",
-    )(flags, b, kappa, above, below, sides, tracts, county)
+    )(flags, b, kappa, above, below, got_near, got_far, tracts, county)
 
 
 def two_sum(a, b):
@@ -325,10 +477,15 @@
         in_specs=[fixed(got.shape), fixed(sums.shape), fixed(state.shape), tile, tile, tile],
         out_specs=[tile, tile] + [fixed(shape) for shape in small],
         scratch_shapes=[pltpu.VMEM((8, LANES), F32)],
-        compiler_params=params(24),
-        cost_estimate=pl.CostEstimate(flops=6 * rows * cols, transcendentals=0, bytes_accessed=20 * rows * cols),
+        compiler_params=params(60),
+        cost_estimate=cost(8),
         name="finish",
     )(got, sums, state, b, two, four)
+
+
+def invert_pair(a, b, c):
+    scale = 1.0 / (a * c - b * b)
+    return c * scale, -b * scale, a * scale
 
 
 def invert_block(rows):
@@ -336,20 +493,54 @@
     lane, sub = iota((8, size), 1), iota((8, size), 0)
     groups = size // 8
     pivots = [jnp.ones((8, size), F32)] * groups
-    for k in range(size):
+    for k in range(0, size, 4):
         g, s = divmod(k, 8)
-        pivot = jnp.broadcast_to(rows[g][s : s + 1, k : k + 1], (8, size))
-        line = jnp.broadcast_to(rows[g][s : s + 1, :], (8, size))
-        scaled = jnp.where(lane == k, 1.0, line) * (1.0 / pivot)
-        pivots[g] = jnp.where(sub == s, pivot, pivots[g])
+        block = jnp.logical_and(lane >= k, lane < k + 4)
+        factors = {
+            h: [jnp.broadcast_to(rows[h][:, k + c : k + c + 1], (8, size)) for c in range(4)]
+            for h in range(g, groups)
+        }
+
+        def at(i, j):
+            return jnp.broadcast_to(factors[g][j][s + i : s + i + 1, :], (8, size))
+
+        line = []
+        for i in range(4):
+            whole = jnp.broadcast_to(rows[g][s + i : s + i + 1, :], (8, size))
+            line.append(jnp.where(block, jnp.where(lane == k + i, 1.0, 0.0), whole))
+        p00, p10, p11 = at(0, 0), at(1, 0), at(1, 1)
+        q00, q01, q10, q11 = at(2, 0), at(2, 1), at(3, 0), at(3, 1)
+        i00, i10, i11 = invert_pair(p00, p10, p11)
+        t00, t01 = q00 * i00 + q01 * i10, q00 * i10 + q01 * i11
+        t10, t11 = q10 * i00 + q11 * i10, q10 * i10 + q11 * i11
+        c00 = at(2, 2) - (t00 * q00 + t01 * q01)
+        c10 = at(3, 2) - (t10 * q00 + t11 * q01)
+        c11 = at(3, 3) - (t10 * q10 + t11 * q11)
+        j00, j10, j11 = invert_pair(c00, c10, c11)
+        low_2 = line[2] - (t00 * line[0] + t01 * line[1])
+        low_3 = line[3] - (t10 * line[0] + t11 * line[1])
+        w_2, w_3 = j00 * low_2 + j10 * low_3, j10 * low_2 + j11 * low_3
+        w_0 = (i00 * line[0] + i10 * line[1]) - (t00 * w_2 + t10 * w_3)
+        w_1 = (i10 * line[0] + i11 * line[1]) - (t01 * w_2 + t11 * w_3)
         for h in range(g, groups):
-            factor = jnp.broadcast_to(rows[h][:, k : k + 1], (8, size))
-            updated = jnp.where(lane == k, 0.0, rows[h]) - factor * scaled
-            rows[h] = jnp.where(sub > s, updated, rows[h]) if h == g else updated
+            f = factors[h]
+            cut = (f[0] * w_0 + f[1] * w_1) + (f[2] * w_2 + f[3] * w_3)
+            updated = jnp.where(block, 0.0, rows[h]) - cut
+            if h > g:
+                rows[h] = updated
+                continue
+            l10, l32 = p10 / p00, c10 / c00
+            done = (line[0], line[1] - l10 * line[0], low_2, low_3 - l32 * low_2)
+            diagonal = (p00, p11 - l10 * p10, c00, c11 - l32 * c10)
+            own = jnp.where(sub >= s + 4, updated, rows[g])
+            pivot = pivots[g]
+            for i in range(4):
+                own = jnp.where(sub == s + i, done[i], own)
+                pivot = jnp.where(sub == s + i, diagonal[i], pivot)
+            rows[g], pivots[g] = own, pivot
     out = []
     for g in range(groups):
-        row = sub + 8 * g
-        kept = jnp.where(lane < row, rows[g], jnp.where(lane == row, 1.0, 0.0))
+        kept = jnp.where(lane <= sub + 8 * g, rows[g], 0.0)
         out.append(kept / jnp.sqrt(pivots[g]))
     return out
 
@@ -388,8 +579,8 @@
         in_specs=[pl.BlockSpec(memory_space=pltpu.VMEM)],
         out_specs=pl.BlockSpec(memory_space=pltpu.VMEM),
         scratch_shapes=[half, half],
-        compiler_params=params(16),
-        cost_estimate=pl.CostEstimate(flops=200 * size * size * size, transcendentals=0, bytes_accessed=8 * size * size),
+        compiler_params=params(60),
+        cost_estimate=cost(14),
         name="factor",
     )(a)
 
@@ -399,101 +590,127 @@
     return high, (value - high.astype(F32)).astype(jnp.bfloat16)
 
 
-def update_kernel(column, wide, inverse, schur, panel, updated, other):
+def update_kernel(flags, column, column_got, wide_hbm, wide_got, inverse, schur, panel, updated, wide, other, sem):
     size = inverse.shape[0]
     count = other.shape[0]
 
     @pl.when(pl.program_id(0) == 0)
     def _():
+        @pl.when(flags[4] > 0)
+        def _():
+            pltpu.make_async_copy(wide_got, wide, sem).start()
+
+        @pl.when(flags[4] == 0)
+        def _():
+            pltpu.make_async_copy(wide_hbm, wide, sem).start()
+
+        pltpu.make_async_copy(wide_hbm, wide, sem).wait()
         for index in range(count):
             high, low = split(dot(inverse[...], wide[:, index, :]))
             other[index, 0:size, :] = high
             other[index, size : 2 * size, :] = low
             other[index, 2 * size :, :] = high
 
-    own = dot(column[0], inverse[...], (1, 1))
+    own = jnp.where(flags[5] > 0, column_got[0], column[0])
+    own = dot(own, inverse[...], (1, 1))
     panel[0] = own
     high, low = split(own)
     lhs = jnp.concatenate([high, high, low], axis=1)
     for index in range(count):
         product = jnp.dot(lhs, other[index], preferred_element_type=F32)
-        updated[0, :, index, :] = schur[0, :, index, :] - product
-
-
-def update(column, wide, inverse, schur):
+        for part in range(size // LANES):
+            at = pl.ds(part * count + index, size, stride=count * (size // LANES))
+            updated[0, at, :] = schur[0, at, :] - product[:, part * LANES : (part + 1) * LANES]
+
+
+def update(flags, column, column_got, wide, wide_got, inverse, schur):
     count_rows, size, count, _ = schur.shape
+    parts = size // LANES
+    flat = schur.reshape(count_rows, size, count, parts, LANES).transpose(0, 1, 3, 2, 4)
+    flat = flat.reshape(count_rows, size * parts * count, LANES)
 
     def step(*block):
         return pl.BlockSpec((1,) + block, lambda i: (i,) + (0,) * len(block))
 
-    def fixed(shape):
-        return pl.BlockSpec(shape, lambda i: (0,) * len(shape))
-
+    any_spec = pl.BlockSpec(memory_space=pl.ANY)
+    inverse_spec = pl.BlockSpec(inverse.shape, lambda i: (0, 0))
     panel, updated = pl.pallas_call(
         update_kernel,
         grid=(count_rows,),
         out_shape=(
             jax.ShapeDtypeStruct(column.shape, F32),
-            jax.ShapeDtypeStruct(schur.shape, F32),
+            jax.ShapeDtypeStruct(flat.shape, F32),
         ),
-        in_specs=[step(size, size), fixed(wide.shape), fixed(inverse.shape), step(size, count, size)],
-        out_specs=(step(size, size), step(size, count, size)),
-        scratch_shapes=[pltpu.VMEM((count, 3 * size, size), jnp.bfloat16)],
-        compiler_params=params(40),
-        cost_estimate=pl.CostEstimate(flops=6 * schur.size * size, transcendentals=0, bytes_accessed=8 * schur.size),
+        in_specs=[pl.BlockSpec(memory_space=pltpu.SMEM), step(size, size), step(size, size)]
+        + [any_spec, any_spec, inverse_spec, step(*flat.shape[1:])],
+        out_specs=(step(size, size), step(*flat.shape[1:])),
+        scratch_shapes=[
+            pltpu.VMEM(wide.shape, F32),
+            pltpu.VMEM((count, 3 * size, size), jnp.bfloat16),
+            pltpu.SemaphoreType.DMA,
+        ],
+        compiler_params=params(60),
+        cost_estimate=cost(17),
         name="update",
-    )(column, wide, inverse, schur)
-    return panel, updated
-
-
-def halo_messages(b, kappa):
-    rows, cols = b.shape
-    top = jnp.concatenate([b[:HALO], kappa[:HALO]], axis=0)
-    bottom = jnp.concatenate([b[rows - HALO :], kappa[rows - HALO :]], axis=0)
-    above, below = pair_exchange(top, bottom, "row")
-
-    def strip(columns, which):
-        field, at = ((b, 0), (kappa, HALO))[which]
-        parts = [field[:, columns].T, above[at : at + HALO, columns].T, below[at : at + HALO, columns].T]
-        return jnp.concatenate(parts, axis=1)
-
-    first, last = slice(0, HALO), slice(cols - HALO, cols)
-    left = jnp.concatenate([strip(first, 0), strip(first, 1)], axis=0)
-    right = jnp.concatenate([strip(last, 1), strip(last, 0)], axis=0)
-    before, after = pair_exchange(left, right, "col")
-    length = before.shape[1]
-    sides = jnp.zeros((LANES, -(-length // LANES) * LANES), F32)
-    sides = sides.at[: 2 * HALO, :length].set(after)
-    sides = sides.at[LANES - 2 * HALO :, :length].set(before)
-    return above, below, sides
+    )(flags, column, column_got, wide, wide_got, inverse, flat)
+    updated = updated.reshape(count_rows, size, parts, count, LANES).transpose(0, 1, 3, 2, 4)
+    return panel, updated.reshape(schur.shape)
 
 
 def per_device(right_side, kappa_sq, block_tract, tract_county, county_state, schur):
     n_row, n_col = lax.axis_size("row"), lax.axis_size("col")
     row, col = lax.axis_index("row"), lax.axis_index("col")
-    above, below, sides = halo_messages(right_side, kappa_sq)
-    flags = jnp.stack([row > 0, row < n_row - 1, col > 0, col < n_col - 1]).astype(jnp.int32)
-
-    corner = tree(tree(schur[0, :, 0, :], "col", halvings(n_col)), "row", halvings(n_row))
-    column = tree(schur[:, :, 0, :], "col", halvings(n_col))
-    wide = spread_row(schur[0], "row")
+    flags = [row > 0, row < n_row - 1, col > 0, col < n_col - 1, row % 2 == 1, col % 2 == 1]
+    flags = jnp.stack(flags).astype(jnp.int32)
+
+    corner = corner_block(schur)
+    steps = small_steps(n_row, n_col)
+    corner = small_hop(corner, steps[0])
+    near, far, left, right = edge_messages(flags, right_side, kappa_sq)
+    near, far = trade(near, far, "row")
+    near, far, corner = lax.optimization_barrier((near, far, corner))
+    corner = small_hop(corner, steps[1])
+    above, below, near, far = corner_messages(flags, near, far, left, right)
+    near, far = trade(near, far, "col")
+    near, far, corner = lax.optimization_barrier((near, far, corner))
+    corner = small_hop(corner, steps[2])
+    column, wide = extract(after(schur, near))
+    column, wide, corner = lax.optimization_barrier((column, wide, corner))
+    column_got, wide_got = hop(column, "col", n_col), hop(wide, "row", n_row)
+    for step in steps[3:]:
+        corner = small_hop(corner, step)
+    near, far, corner = lax.optimization_barrier((near, far, corner))
 
     tracts = jnp.concatenate([block_tract, block_tract], axis=1)
     pay, sums, two, four = raster(
-        flags, right_side, kappa_sq, above, below, sides, tracts, tract_county[:, None]
+        flags, right_side, kappa_sq, above, below, near, far, tracts, tract_county[:, None]
     )
-    devices = n_row * n_col
-    got = lax.all_to_all(jnp.broadcast_to(pay[None], (devices,) + pay.shape), ("row", "col"), 0, 0)
+    pay, column_got, wide_got = lax.optimization_barrier((pay, column_got, wide_got))
+    got = exchange(pay).reshape(-1, LANES)
+    stride = n_col
+    while stride > 2:
+        column = merge(column_got, column, "col", stride)
+        stride //= 2
+        column_got = hop(column, "col", stride)
+    stride = n_row
+    wide = merge(wide_got, wide, "row", stride)
+    stride //= 2
+    wide_got = hop(wide, "row", stride)
     inverse = factor(corner)
+    wide_got, got = lax.optimization_barrier((wide_got, got))
+    while stride > 2:
+        wide = merge(wide_got, wide, "row", stride)
+        stride //= 2
+        wide_got = hop(wide, "row", stride)
     solution, residual, tract_totals, county_totals, state_totals = finish(
-        got.reshape(devices * 16, LANES),
+        after(got, inverse),
         sums,
         county_state.reshape(COUNTIES // LANES, LANES),
         right_side,
         two,
         four,
     )
-    panel, updated = update(column, wide, inverse, schur)
+    panel, updated = update(flags, column, column_got, wide, wide_got, inverse, schur)
     return (
         solution,
         residual,

time: 183 us -> 158 us (0.86)
  the two profiles are of different devices: /device:TPU:0 before, /device:TPU:2 now
where the time goes in v2:
time: 158 us; the launch traced here: 157 us
  Pallas kernels  75.9 us (48%)
  waiting for transfers between devices  36.8 us (23%)
  starting transfers between devices  31.4 us (20%)
  local copies, waits for them, and re-layouts  9.72 us (6%)
  other arithmetic  2.13 us (1%)
    pallas_call x1, Pallas kernels, raster(): pl.pallas_call(raster_kernel, out_shape=(jax.ShapeDtypeStruct((16, LANES)...  25 us
    all_to_all x1, waiting for transfers between devices, exchange(): lax.all_to_all(jnp.broadcast_to(mine, (devices,) + mine.shape), axes, 0, 0)  21.7 us
    ppermute x10, starting transfers between devices, hop(): return lax.ppermute(block, axis, pairs)  21.5 us
    pallas_call x1, Pallas kernels, update(): pl.pallas_call(update_kernel, grid=(count_rows,), out_shape=(jax.ShapeDty...  17.4 us
    pallas_call x1, Pallas kernels, factor(): pl.pallas_call(factor_kernel, out_shape=jax.ShapeDtypeStruct(a.shape, F32...  14.5 us
    ppermute x10, waiting for transfers between devices, hop(): return lax.ppermute(block, axis, pairs)  11.4 us
    pallas_call x1, Pallas kernels, finish(): pl.pallas_call(functools.partial(finish_kernel, devices), grid=(rows // s...  8.13 us
    unnamed x34, local copies, waits for them, and re-layouts  7.07 us
  transfers between devices with their start and end apart: 15, of which 6 were waited for; matrix products, arithmetic and copies ran while one was open for 3% of the time, Pallas kernels for 36%

profile of v2, /device:TPU:2, one launch (start us, length us, event | category | flops | bytes accessed | tf_op | source)
XLA Modules:
  0.0 157.1 jit_solution(12459602699158739480)
XLA Ops:
  0.6 1.7 %corner.1 = f32[256,256]{1,0:T(8,128)} custom-call(f32[4,256,8,256]{3,2,1,0:T(8,128)} %schur.2), custom_call_target="tpu_custom_call" | custom-call | flops 2000000000 | bytes 1024 | tf_op jit(solution)/shard_map/corner/pallas_call | solution.py:106
  2.3 4.5 %collective-permute-start.2 = (f32[256,256]{1,0:T(8,128)}, f32[256,256]{1,0:T(8,128)S(1)}, u32[]{:S(2)}, u32[]{:S(2)}) collective-permute-start(f32[256,256]{1,0:T(8,128)} %corner.1), channel_id=1, source_target_pairs={{0,2},{4,6},{8,10},{12,14},{16,18},{20,22},{24,26},{28,30}} | collective-permute-start | bytes 786440 | tf_op jit(solution)/shard_map/ppermute | solution.py:51
  6.9 0.1 stack.27
  7.0 0.6 convert_element_type.2.flags
  7.6 2.3 %edges.1 = (f32[8,1024]{1,0:T(8,128)}, f32[8,1024]{1,0:T(8,128)}, f32[8,512]{1,0:T(8,128)}, f32[8,512]{1,0:T(8,128)}) custom-call(s32[6]{0:T(128)} %convert_element_type.2.flags, f32[512,1024]{1,0:T(8,128)} %b.1, f32[512,1024]{1,0:T(8,128)} %b.1, f32[512,1024]{1,0:T(8,128)} %k_hbm.1, f32[512,1024]{1,0:T(8,128)} %k_hbm.1, f32[512,1024]{1,0:T(8,128)} %b.1, ...), custom_call_target="tpu_custom_call" | custom-call | flops 2000000000 | bytes 1024 | tf_op jit(solution)/shard_map/edges/pallas_call | solution.py:182
  9.8 2.5 %collective-permute-start.1 = (f32[8,1024]{1,0:T(8,128)}, f32[8,1024]{1,0:T(8,128)S(1)}, u32[]{:S(2)}, u32[]{:S(2)}) collective-permute-start(f32[8,1024]{1,0:T(8,128)} %get-tuple-element.48), channel_id=1, source_target_pairs={{4,8},{12,16},{20,24},{8,4},{16,12},{24,20},{5,9},{13,17},{21,25},... | collective-permute-start | bytes 98312 | tf_op jit(solution)/shard_map/ppermute | solution.py:42
  12.4 0.3 collective-permute-done.2
  12.8 2.5 %collective-permute-done.1.got_far = f32[8,1024]{1,0:T(8,128)S(1)} collective-permute-done((f32[8,1024]{1,0:T(8,128)}, f32[8,1024]{1,0:T(8,128)S(1)}, u32[]{:S(2)}, u32[]{:S(2)}) %collective-permute-start.1) | collective-permute-done | bytes 32800 | tf_op jit(solution)/shard_map/ppermute | solution.py:42
  15.3 1.3 collective-permute-start.5
  16.6 0.0 copy-start.1
  16.6 0.7 copy-done.1
  17.3 0.7 copy-done.2
  18.0 0.7 corners.1
  18.7 0.0 copy-start.3
  18.7 0.6 copy-done.3
  19.3 0.6 copy-done.4
  19.9 0.7 collective-permute-start.4
  20.6 2.0 %collective-permute-done.5 = f32[256,256]{1,0:T(8,128)S(1)} collective-permute-done((f32[256,256]{1,0:T(8,128)S(1)}, f32[256,256]{1,0:T(8,128)S(1)}, u32[]{:S(2)}, u32[]{:S(2)}) %collective-permute-start.5) | collective-permute-done | bytes 262176 | tf_op jit(solution)/shard_map/ppermute | solution.py:51
  22.6 0.0 copy-start.9
  22.6 0.0 copy-start.7
  22.6 1.1 collective-permute-done.3.got_near
  23.8 0.7 collective-permute-start.6
  24.5 3.3 %extract.1 = (f32[4,256,256]{2,1,0:T(8,128)}, f32[256,8,256]{2,1,0:T(8,128)}) custom-call(f32[4,256,8,256]{3,2,1,0:T(8,128)} %schur.2), custom_call_target="tpu_custom_call" | custom-call | flops 3000000000 | bytes 1024 | tf_op jit(solution)/shard_map/extract/pallas_call | solution.py:121
  27.8 1.3 collective-permute-start.7
  29.2 9.1 %collective-permute-done.7 = f32[256,256]{1,0:T(8,128)S(1)} collective-permute-done((f32[256,256]{1,0:T(8,128)S(1)}, f32[256,256]{1,0:T(8,128)S(1)}, u32[]{:S(2)}, u32[]{:S(2)}) %collective-permute-start.7) | collective-permute-done | bytes 262176 | tf_op jit(solution)/shard_map/ppermute | solution.py:51
  38.3 1.3 collective-permute-start.8
  39.6 0.7 copy.16.county
  40.3 0.7 pad_add_fusion.tracts
  41.0 5.3 %collective-permute-start.9 = (f32[4,256,256]{2,1,0:T(8,128)}, f32[4,256,256]{2,1,0:T(8,128)S(1)}, u32[]{:S(2)}, u32[]{:S(2)}) collective-permute-start(f32[4,256,256]{2,1,0:T(8,128)} %get-tuple-element.68._), channel_id=1, source_target_pairs={{0,2},{4,6},{8,10},{12,14},{16,18},{20,22},{24,26},{28,30}} | collective-permute-start | bytes 3145736 | tf_op jit(solution)/shard_map/ppermute | solution.py:51
  46.3 0.8 collective-permute-start.10
  47.1 0.7 broadcast_select_fusion.2.a
  47.9 25.0 %raster.1 = (f32[16,128]{1,0:T(8,128)}, f32[64,128]{1,0:T(8,128)}, f32[512,1024]{1,0:T(8,128)}, f32[512,1024]{1,0:T(8,128)}) custom-call(s32[6]{0:T(128)} %convert_element_type.2.flags, f32[512,1024]{1,0:T(8,128)} %b.1, f32[512,1024]{1,0:T(8,128)} %k_hbm.1, f32[8,1024]{1,0:T(8,128)} %copy-done.3, f32[8,1024]{1,0:T(8,128)} %copy-done.4, f32[8,768]{1,0:T(8,128)} %copy-done.15, ...), custom_call_target="tpu_custom_call" | custom-call | flops 24999999488 | bytes 1024 | tf_op jit(solution)/shard_map/raster/pallas_call | solution.py:370
  72.9 0.0 copy-start.11
  72.9 1.3 copy-done.11
  74.3 1.3 collective-permute-start.11
  75.6 0.7 broadcast_in_dim.7
  76.3 6.7 %all-to-all-start = ((f32[32,16,128]{2,1,0:T(8,128)}), f32[32,16,128]{2,1,0:T(8,128)S(1)}, u32[]{:S(2)}, u32[]{:S(2)}) async-start(f32[32,16,128]{2,1,0:T(8,128)} %broadcast_in_dim.7), calls=%async_computation | async-start | bytes 524288 | tf_op jit(solution)/shard_map/all_to_all | solution.py:158
  83.1 3.4 %collective-permute-start.12 = (f32[4,256,256]{2,1,0:T(8,128)}, f32[4,256,256]{2,1,0:T(8,128)S(1)}, u32[]{:S(2)}, u32[]{:S(2)}) collective-permute-start(f32[4,256,256]{2,1,0:T(8,128)} %merge.4.column), channel_id=1, source_target_pairs={{0,1},{2,3},{4,5},{6,7},{8,9},{10,11},{12,13},{14,15},{16,17},{18,... | collective-permute-start | bytes 3145736 | tf_op jit(solution)/shard_map/ppermute | solution.py:51
  86.5 21.7 %all-to-all-done = f32[32,16,128]{2,1,0:T(8,128)S(1)} async-done(((f32[32,16,128]{2,1,0:T(8,128)}), f32[32,16,128]{2,1,0:T(8,128)S(1)}, u32[]{:S(2)}, u32[]{:S(2)}) %all-to-all-start) | async-done | bytes 262176 | tf_op jit(solution)/shard_map/all_to_all | solution.py:158
  108.2 1.3 copy-done.10
  109.6 2.9 %merge.5.wide_hbm = f32[256,8,256]{2,1,0:T(8,128)} custom-call(s32[1]{0:T(128)} %bitcast.14.flag, f32[256,8,256]{2,1,0:T(8,128)} %copy-done.10, f32[256,8,256]{2,1,0:T(8,128)} %merge.3._), custom_call_target="tpu_custom_call", output_to_operand_aliasing={{}: (2, {})} | custom-call | flops 2000000000 | bytes 1024 | tf_op jit(solution)/shard_map/merge/pallas_call | solution.py:72
  112.5 1.6 %collective-permute-start.13 = (f32[256,8,256]{2,1,0:T(8,128)}, f32[256,8,256]{2,1,0:T(8,128)S(1)}, u32[]{:S(2)}, u32[]{:S(2)}) collective-permute-start(f32[256,8,256]{2,1,0:T(8,128)} %merge.5.wide_hbm), channel_id=1, source_target_pairs={{0,4},{8,12},{16,20},{24,28},{1,5},{9,13},{17,21},{25,29},{2,6},{1... | collective-permute-start | bytes 6291464 | tf_op jit(solution)/shard_map/ppermute | solution.py:51
  114.1 14.5 %factor.1.inverse = f32[256,256]{1,0:T(8,128)} custom-call(f32[256,256]{1,0:T(8,128)} %broadcast_select_fusion.2.a), custom_call_target="tpu_custom_call" | custom-call | flops 14000000000 | bytes 1024 | tf_op jit(solution)/shard_map/factor/pallas_call | solution.py:576
  128.7 8.1 %finish.1 = (f32[512,1024]{1,0:T(8,128)}, f32[512,1024]{1,0:T(8,128)}, f32[1,64]{1,0:T(1,128)}, f32[4,128]{1,0:T(4,128)}, f32[1,64]{1,0:T(1,128)}) custom-call(f32[512,128]{1,0:T(8,128)} %bitcast.27, f32[64,128]{1,0:T(8,128)} %get-tuple-element.75.sums, s32[4,128]{1,0:T(4,128)} %bitcast.29, f32[512,1024]{1,0:T(8,128)} %b.1, ...), custom_call_target="tpu_custom_call" | custom-call | flops 8000000000 | bytes 1024 | tf_op jit(solution)/shard_map/finish/pallas_call | solution.py:472
  136.8 1.1 slice_bitcast_fusion
  137.9 1.0 copy-done.14
  138.9 0.7 copy-done.12
  139.6 17.4 %update.1 = (f32[4,256,256]{2,1,0:T(8,128)}, f32[4,4096,128]{2,1,0:T(8,128)}) custom-call(s32[6]{0:T(128)} %convert_element_type.2.flags, f32[4,256,256]{2,1,0:T(8,128)} %merge.4.column, f32[4,256,256]{2,1,0:T(8,128)} %copy-done.14, f32[256,8,256]{2,1,0:T(8,128)} %merge.5.wide_hbm, f32[256,8,256]{2,1,0:T(8,128)} %copy-done.12, f32[256,256]{1,0:T(8,128)} %factor.1.inverse, ...), custom_call_target="tpu_custom_call" | custom-call | flops 16999999488 | bytes 1024 | tf_op jit(solution)/shard_map/update/pallas_call | solution.py:637
  (38 shorter events, 0.2 us)
Async XLA Ops:
  2.3 10.4 %collective-permute-start.2 = (f32[256,256]{1,0:T(8,128)}, f32[256,256]{1,0:T(8,128)S(1)}, u32[]{:S(2)}, u32[]{:S(2)}) collective-permute-start(f32[256,256]{1,0:T(8,128)} %corner.1), channel_id=1, source_target_pairs={{0,2},{4,6},{8,10},{12,14},{16,18},{20,22},{24,26},{28,30}} | collective-permute-start | bytes 786440 | tf_op jit(solution)/shard_map/ppermute | solution.py:51
  7.6 5.1 %copy-start.5 = (f32[256,256]{1,0:T(8,128)S(1)}, f32[256,256]{1,0:T(8,128)}, u32[]{:S(2)}) copy-start(f32[256,256]{1,0:T(8,128)} %corner.1) | copy-start | bytes 786436
  7.6 9.0 %copy-start = (s32[6]{0:T(128)S(1)}, s32[6]{0:T(128)}, u32[]{:S(2)}) copy-start(s32[6]{0:T(128)} %convert_element_type.2.flags) | copy-start | bytes 76
  9.8 2.9 %collective-permute-start = (f32[8,1024]{1,0:T(8,128)}, f32[8,1024]{1,0:T(8,128)S(1)}, u32[]{:S(2)}, u32[]{:S(2)}) collective-permute-start(f32[8,1024]{1,0:T(8,128)} %get-tuple-element.47), channel_id=1, source_target_pairs={{0,4},{4,0},{8,12},{12,8},{16,20},{20,16},{24,28},{28,24},{1,5},{5... | collective-permute-start | bytes 98312 | tf_op jit(solution)/shard_map/ppermute | solution.py:42
  9.8 5.4 %collective-permute-start.1 = (f32[8,1024]{1,0:T(8,128)}, f32[8,1024]{1,0:T(8,128)S(1)}, u32[]{:S(2)}, u32[]{:S(2)}) collective-permute-start(f32[8,1024]{1,0:T(8,128)} %get-tuple-element.48), channel_id=1, source_target_pairs={{4,8},{12,16},{20,24},{8,4},{16,12},{24,20},{5,9},{13,17},{21,25},... | collective-permute-start | bytes 98312 | tf_op jit(solution)/shard_map/ppermute | solution.py:42
  15.3 7.3 %collective-permute-start.5 = (f32[256,256]{1,0:T(8,128)S(1)}, f32[256,256]{1,0:T(8,128)S(1)}, u32[]{:S(2)}, u32[]{:S(2)}) collective-permute-start(f32[256,256]{1,0:T(8,128)S(1)} %broadcast_select_fusion.4), channel_id=1, source_target_pairs={{0,1},{2,3},{4,5},{6,7},{8,9},{10,11},{12,13},{14,15},{16,17},{18,... | collective-permute-start | bytes 786440 | tf_op jit(solution)/shard_map/ppermute | solution.py:51
  16.6 0.7 copy-start.1
  17.3 0.7 copy-start.2
  18.7 0.6 copy-start.3
  19.3 0.6 copy-start.4
  19.9 3.8 %collective-permute-start.3 = (f32[8,768]{1,0:T(8,128)S(1)}, f32[8,768]{1,0:T(8,128)S(1)}, u32[]{:S(2)}, u32[]{:S(2)}) collective-permute-start(f32[8,768]{1,0:T(8,128)S(1)} %get-tuple-element.55), channel_id=1, source_target_pairs={{0,1},{1,0},{2,3},{3,2},{4,5},{5,4},{6,7},{7,6},{8,9},{9,8},{10,11... | collective-permute-start | bytes 73736 | tf_op jit(solution)/shard_map/ppermute | solution.py:42
  19.9 3.8 %collective-permute-start.4 = (f32[8,768]{1,0:T(8,128)S(1)}, f32[8,768]{1,0:T(8,128)S(1)}, u32[]{:S(2)}, u32[]{:S(2)}) collective-permute-start(f32[8,768]{1,0:T(8,128)S(1)} %get-tuple-element.56), channel_id=1, source_target_pairs={{1,2},{2,1},{5,6},{6,5},{9,10},{10,9},{13,14},{14,13},{17,18},{18,... | collective-permute-start | bytes 73736 | tf_op jit(solution)/shard_map/ppermute | solution.py:42
  22.6 17.0 %copy-start.9 = (s32[64]{0:T(128)S(1)}, s32[64]{0:T(128)}, u32[]{:S(2)}) copy-start(s32[64]{0:T(128)} %param.9) | copy-start | bytes 772
  22.6 17.7 %copy-start.7 = (s32[32,64]{1,0:T(8,128)S(1)}, s32[32,64]{1,0:T(8,128)}, u32[]{:S(2)}) copy-start(s32[32,64]{1,0:T(8,128)} %param.8) | copy-start | bytes 24580
  23.8 4.0 %copy-start.15 = (f32[8,768]{1,0:T(8,128)}, f32[8,768]{1,0:T(8,128)S(1)}, u32[]{:S(2)}) copy-start(f32[8,768]{1,0:T(8,128)S(1)} %collective-permute-done.3.got_near) | copy-start | bytes 73732
  23.8 4.0 %copy-start.16 = (f32[8,768]{1,0:T(8,128)}, f32[8,768]{1,0:T(8,128)S(1)}, u32[]{:S(2)}) copy-start(f32[8,768]{1,0:T(8,128)S(1)} %collective-permute-done.4.got_far) | copy-start | bytes 73732
  23.8 4.0 %collective-permute-start.6 = (f32[256,256]{1,0:T(8,128)S(1)}, f32[256,256]{1,0:T(8,128)S(1)}, u32[]{:S(2)}, u32[]{:S(2)}) collective-permute-start(f32[256,256]{1,0:T(8,128)S(1)} %broadcast_select_fusion.3), channel_id=1, source_target_pairs={{0,16},{1,17},{2,18},{3,19}} | collective-permute-start | bytes 786440 | tf_op jit(solution)/shard_map/ppermute | solution.py:51
  27.8 10.4 %collective-permute-start.7 = (f32[256,256]{1,0:T(8,128)S(1)}, f32[256,256]{1,0:T(8,128)S(1)}, u32[]{:S(2)}, u32[]{:S(2)}) collective-permute-start(f32[256,256]{1,0:T(8,128)S(1)} %broadcast_select_fusion), channel_id=1, source_target_pairs={{0,8},{16,24},{1,9},{17,25},{2,10},{18,26},{3,11},{19,27}} | collective-permute-start | bytes 786440 | tf_op jit(solution)/shard_map/ppermute | solution.py:51
  38.3 8.8 %collective-permute-start.8 = (f32[256,256]{1,0:T(8,128)S(1)}, f32[256,256]{1,0:T(8,128)S(1)}, u32[]{:S(2)}, u32[]{:S(2)}) collective-permute-start(f32[256,256]{1,0:T(8,128)S(1)} %broadcast_select_fusion.1), channel_id=1, source_target_pairs={{0,4},{8,12},{16,20},{24,28},{1,5},{9,13},{17,21},{25,29},{2,6},{1... | collective-permute-start | bytes 786440 | tf_op jit(solution)/shard_map/ppermute | solution.py:51
  41.0 31.9 %collective-permute-start.9 = (f32[4,256,256]{2,1,0:T(8,128)}, f32[4,256,256]{2,1,0:T(8,128)S(1)}, u32[]{:S(2)}, u32[]{:S(2)}) collective-permute-start(f32[4,256,256]{2,1,0:T(8,128)} %get-tuple-element.68._), channel_id=1, source_target_pairs={{0,2},{4,6},{8,10},{12,14},{16,18},{20,22},{24,26},{28,30}} | collective-permute-start | bytes 3145736 | tf_op jit(solution)/shard_map/ppermute | solution.py:51
  46.3 26.6 %collective-permute-start.10 = (f32[256,8,256]{2,1,0:T(8,128)}, f32[256,8,256]{2,1,0:T(8,128)S(1)}, u32[]{:S(2)}, u32[]{:S(2)}) collective-permute-start(f32[256,8,256]{2,1,0:T(8,128)} %get-tuple-element.69._), channel_id=1, source_target_pairs={{0,16},{1,17},{2,18},{3,19}} | collective-permute-start | bytes 6291464 | tf_op jit(solution)/shard_map/ppermute | solution.py:51
  72.9 10.2 %copy-start.13 = (f32[4,256,256]{2,1,0:T(8,128)}, f32[4,256,256]{2,1,0:T(8,128)S(1)}, u32[]{:S(2)}) copy-start(f32[4,256,256]{2,1,0:T(8,128)S(1)} %collective-permute-done.9.got) | copy-start | bytes 3145732
  72.9 1.4 copy-start.11
  74.3 1.3 copy-start.8
  74.3 34.0 %collective-permute-start.11 = (f32[256,8,256]{2,1,0:T(8,128)}, f32[256,8,256]{2,1,0:T(8,128)S(1)}, u32[]{:S(2)}, u32[]{:S(2)}) collective-permute-start(f32[256,8,256]{2,1,0:T(8,128)} %merge.3._), channel_id=1, source_target_pairs={{0,8},{16,24},{1,9},{17,25},{2,10},{18,26},{3,11},{19,27}} | collective-permute-start | bytes 6291464 | tf_op jit(solution)/shard_map/ppermute | solution.py:51
  76.3 31.9 %all-to-all-start = ((f32[32,16,128]{2,1,0:T(8,128)}), f32[32,16,128]{2,1,0:T(8,128)S(1)}, u32[]{:S(2)}, u32[]{:S(2)}) async-start(f32[32,16,128]{2,1,0:T(8,128)} %broadcast_in_dim.7), calls=%async_computation | async-start | bytes 524288 | tf_op jit(solution)/shard_map/all_to_all | solution.py:158
  83.1 54.8 %collective-permute-start.12 = (f32[4,256,256]{2,1,0:T(8,128)}, f32[4,256,256]{2,1,0:T(8,128)S(1)}, u32[]{:S(2)}, u32[]{:S(2)}) collective-permute-start(f32[4,256,256]{2,1,0:T(8,128)} %merge.4.column), channel_id=1, source_target_pairs={{0,1},{2,3},{4,5},{6,7},{8,9},{10,11},{12,13},{14,15},{16,17},{18,... | collective-permute-start | bytes 3145736 | tf_op jit(solution)/shard_map/ppermute | solution.py:51
  108.2 4.3 %copy-start.6 = (f32[32,16,128]{2,1,0:T(8,128)}, f32[32,16,128]{2,1,0:T(8,128)S(1)}, u32[]{:S(2)}) copy-start(f32[32,16,128]{2,1,0:T(8,128)S(1)} %all-to-all-done) | copy-start | bytes 786436
  108.2 1.3 copy-start.10
  112.5 25.4 %collective-permute-start.13 = (f32[256,8,256]{2,1,0:T(8,128)}, f32[256,8,256]{2,1,0:T(8,128)S(1)}, u32[]{:S(2)}, u32[]{:S(2)}) collective-permute-start(f32[256,8,256]{2,1,0:T(8,128)} %merge.5.wide_hbm), channel_id=1, source_target_pairs={{0,4},{8,12},{16,20},{24,28},{1,5},{9,13},{17,21},{25,29},{2,6},{1... | collective-permute-start | bytes 6291464 | tf_op jit(solution)/shard_map/ppermute | solution.py:51
  137.9 1.0 copy-start.14
  137.9 1.7 %copy-start.12 = (f32[256,8,256]{2,1,0:T(8,128)}, f32[256,8,256]{2,1,0:T(8,128)S(1)}, u32[]{:S(2)}) copy-start(f32[256,8,256]{2,1,0:T(8,128)S(1)} %collective-permute-done.13.wide_got) | copy-start | bytes 6291460

commit v3 on v2

--- a/solution.py
+++ b/solution.py
@@ -82,8 +82,15 @@
     )(flag, got, block)
 
 
-def extract_kernel(schur, raw, wide, held_raw, held_wide, sems):
-    parts = ((schur.at[:, :, 0, :], held_raw, raw), (schur.at[0], held_wide, wide))
+def lane_tiles(schur):
+    count_rows, size, count, width = schur.shape
+    parts = width // LANES
+    flat = schur.reshape(count_rows, size, count, parts, LANES).transpose(0, 1, 3, 2, 4)
+    return flat.reshape(count_rows, size * parts * count, LANES)
+
+
+def extract_kernel(schur, flat, raw, wide, held_raw, held_wide, sems):
+    parts = ((schur.at[:, :, 0, :], held_raw, raw), (flat.at[0], held_wide, wide))
     loads = [pltpu.make_async_copy(a, b, sems.at[i]) for i, (a, b, _) in enumerate(parts)]
     stores = [pltpu.make_async_copy(b, c, sems.at[2 + i]) for i, (_, b, c) in enumerate(parts)]
     for copy in loads:
@@ -115,26 +122,26 @@
     )(schur)
 
 
-def extract(schur):
-    count_rows, size, count, _ = schur.shape
+def extract(schur, flat):
+    count_rows, size, _, _ = schur.shape
     any_spec = pl.BlockSpec(memory_space=pl.ANY)
     return pl.pallas_call(
         extract_kernel,
         out_shape=(
             jax.ShapeDtypeStruct((count_rows, size, size), F32),
-            jax.ShapeDtypeStruct((size, count, size), F32),
+            jax.ShapeDtypeStruct(flat.shape[1:], F32),
         ),
-        in_specs=[any_spec],
+        in_specs=[any_spec, any_spec],
         out_specs=(any_spec, any_spec),
         scratch_shapes=[
             pltpu.VMEM((count_rows, size, size), F32),
-            pltpu.VMEM((size, count, size), F32),
+            pltpu.VMEM(flat.shape[1:], F32),
             pltpu.SemaphoreType.DMA((4,)),
         ],
         compiler_params=params(60),
         cost_estimate=cost(3),
         name="extract",
-    )(schur)
+    )(schur, flat)
 
 
 def small_steps(n_row, n_col):
@@ -330,12 +337,12 @@
 
     zero = jnp.zeros((8, cols), F32)
     edges(bx, v1)
-    sum_0, sum_1 = lax.fori_loop(0, rows // BLOCK, sweep_one, (zero, zero))
+    sum_0, sum_1 = lax.fori_loop(0, rows // BLOCK, sweep_one, (zero, zero), unroll=4)
     edges(v1, v2)
-    sum_2 = lax.fori_loop(0, rows // BLOCK, sweep_two, zero)
+    sum_2 = lax.fori_loop(0, rows // BLOCK, sweep_two, zero, unroll=4)
     edges(v2, v3)
-    sum_3 = lax.fori_loop(0, rows // 8, sweep_three, zero)
-    lax.fori_loop(0, rows // 8, sweep_four, 0)
+    sum_3 = lax.fori_loop(0, rows // 8, sweep_three, zero, unroll=8)
+    lax.fori_loop(0, rows // 8, sweep_four, 0, unroll=8)
 
     pay[...] = jnp.zeros(pay.shape, F32)
     for index, value in enumerate((sum_0, sum_1, sum_2, sum_3)):
@@ -461,7 +468,7 @@
 
 def finish(got, sums, state, b, two, four):
     rows, cols = b.shape
-    step = 64
+    step = 128
     devices = got.shape[0] // 16
 
     def fixed(shape):
@@ -590,6 +597,14 @@
     return high, (value - high.astype(F32)).astype(jnp.bfloat16)
 
 
+def tile_rows(ref, index, size, count):
+    parts = [
+        ref[pl.ds(part * count + index, size, stride=count * (size // LANES)), :]
+        for part in range(size // LANES)
+    ]
+    return jnp.concatenate(parts, axis=1)
+
+
 def update_kernel(flags, column, column_got, wide_hbm, wide_got, inverse, schur, panel, updated, wide, other, sem):
     size = inverse.shape[0]
     count = other.shape[0]
@@ -606,7 +621,7 @@
 
         pltpu.make_async_copy(wide_hbm, wide, sem).wait()
         for index in range(count):
-            high, low = split(dot(inverse[...], wide[:, index, :]))
+            high, low = split(dot(inverse[...], tile_rows(wide, index, size, count)))
             other[index, 0:size, :] = high
             other[index, size : 2 * size, :] = low
             other[index, 2 * size :, :] = high
@@ -626,8 +641,7 @@
 def update(flags, column, column_got, wide, wide_got, inverse, schur):
     count_rows, size, count, _ = schur.shape
     parts = size // LANES
-    flat = schur.reshape(count_rows, size, count, parts, LANES).transpose(0, 1, 3, 2, 4)
-    flat = flat.reshape(count_rows, size * parts * count, LANES)
+    flat = lane_tiles(schur)
 
     def step(*block):
         return pl.BlockSpec((1,) + block, lambda i: (i,) + (0,) * len(block))
@@ -674,7 +688,8 @@
     near, far = trade(near, far, "col")
     near, far, corner = lax.optimization_barrier((near, far, corner))
     corner = small_hop(corner, steps[2])
-    column, wide = extract(after(schur, near))
+    held, flat, near = lax.optimization_barrier((schur, lane_tiles(schur), near))
+    column, wide = extract(held, flat)
     column, wide, corner = lax.optimization_barrier((column, wide, corner))
     column_got, wide_got = hop(column, "col", n_col), hop(wide, "row", n_row)
     for step in steps[3:]:
@@ -697,13 +712,13 @@
     stride //= 2
     wide_got = hop(wide, "row", stride)
     inverse = factor(corner)
-    wide_got, got = lax.optimization_barrier((wide_got, got))
+    wide_got, got, inverse, column_got = lax.optimization_barrier((wide_got, got, inverse, column_got))
     while stride > 2:
         wide = merge(wide_got, wide, "row", stride)
         stride //= 2
         wide_got = hop(wide, "row", stride)
     solution, residual, tract_totals, county_totals, state_totals = finish(
-        after(got, inverse),
+        got,
         sums,
         county_state.reshape(COUNTIES // LANES, LANES),
         right_side,

time: 158 us -> 145 us (0.918)
  the two profiles are of different devices: /device:TPU:2 before, /device:TPU:10 now
where the time goes in v3:
time: 145 us; the launch traced here: 144 us
  Pallas kernels  62.8 us (43%)
  starting transfers between devices  40.1 us (28%)
  waiting for transfers between devices  28.1 us (19%)
  local copies, waits for them, and re-layouts  9.45 us (7%)
  other arithmetic  2.14 us (1%)
    all_to_all x1, starting transfers between devices, exchange(): lax.all_to_all(jnp.broadcast_to(mine, (devices,) + mine.shape), axes, 0, 0)  20.3 us
    pallas_call x1, Pallas kernels, update(): pl.pallas_call(update_kernel, grid=(count_rows,), out_shape=(jax.ShapeDty...  17.3 us
    ppermute x10, waiting for transfers between devices, hop(): return lax.ppermute(block, axis, pairs)  15.5 us
    pallas_call x1, Pallas kernels, factor(): pl.pallas_call(factor_kernel, out_shape=jax.ShapeDtypeStruct(a.shape, F32...  14.5 us
    pallas_call x1, Pallas kernels, raster(): pl.pallas_call(raster_kernel, out_shape=(jax.ShapeDtypeStruct((16, LANES)...  13.6 us
    ppermute x10, starting transfers between devices, hop(): return lax.ppermute(block, axis, pairs)  11.1 us
    ppermute x4, starting transfers between devices, trade(): return (lax.ppermute(near, axis, inside), lax.ppermute(far, axis, between))  8.75 us
    all_to_all x1, waiting for transfers between devices, exchange(): lax.all_to_all(jnp.broadcast_to(mine, (devices,) + mine.shape), axes, 0, 0)  7.18 us
  transfers between devices with their start and end apart: 15, of which 7 were waited for; matrix products, arithmetic and copies ran while one was open for 3% of the time, Pallas kernels for 28%

profile of v3, /device:TPU:10, one launch (start us, length us, event | category | flops | bytes accessed | tf_op | source)
XLA Modules:
  0.0 143.8 jit_solution(8420096806235856577)
XLA Ops:
  0.6 1.7 %corner.1 = f32[256,256]{1,0:T(8,128)} custom-call(f32[4,256,8,256]{3,2,1,0:T(8,128)} %schur.2), custom_call_target="tpu_custom_call" | custom-call | flops 2000000000 | bytes 1024 | tf_op jit(solution)/shard_map/corner/pallas_call | solution.py:113
  2.3 0.7 collective-permute-start.2
  3.1 0.1 stack.27
  3.2 0.6 convert_element_type.2.flags
  3.7 2.3 %edges.1 = (f32[8,1024]{1,0:T(8,128)}, f32[8,1024]{1,0:T(8,128)}, f32[8,512]{1,0:T(8,128)}, f32[8,512]{1,0:T(8,128)}) custom-call(s32[6]{0:T(128)} %convert_element_type.2.flags, f32[512,1024]{1,0:T(8,128)} %b.1, f32[512,1024]{1,0:T(8,128)} %b.1, f32[512,1024]{1,0:T(8,128)} %k_hbm.1, f32[512,1024]{1,0:T(8,128)} %k_hbm.1, f32[512,1024]{1,0:T(8,128)} %b.1, ...), custom_call_target="tpu_custom_call" | custom-call | flops 2000000000 | bytes 1024 | tf_op jit(solution)/shard_map/edges/pallas_call | solution.py:189
  6.0 2.5 %collective-permute-start.1 = (f32[8,1024]{1,0:T(8,128)}, f32[8,1024]{1,0:T(8,128)S(1)}, u32[]{:S(2)}, u32[]{:S(2)}) collective-permute-start(f32[8,1024]{1,0:T(8,128)} %get-tuple-element.51), channel_id=1, source_target_pairs={{4,8},{12,16},{20,24},{8,4},{16,12},{24,20},{5,9},{13,17},{21,25},... | collective-permute-start | bytes 98312 | tf_op jit(solution)/shard_map/ppermute | solution.py:42
  8.6 2.8 %collective-permute-done.1.got_far = f32[8,1024]{1,0:T(8,128)S(1)} collective-permute-done((f32[8,1024]{1,0:T(8,128)}, f32[8,1024]{1,0:T(8,128)S(1)}, u32[]{:S(2)}, u32[]{:S(2)}) %collective-permute-start.1) | collective-permute-done | bytes 32800 | tf_op jit(solution)/shard_map/ppermute | solution.py:42
  11.4 1.3 collective-permute-start.5
  12.7 0.0 copy-start.1
  12.8 0.7 copy-done.1
  13.5 0.7 copy-done.2
  14.2 0.7 corners.1
  14.8 0.0 copy-start.3
  14.9 0.6 copy-done.3
  15.5 0.6 copy-done.4
  16.1 4.3 %collective-permute-start.3 = (f32[8,768]{1,0:T(8,128)S(1)}, f32[8,768]{1,0:T(8,128)S(1)}, u32[]{:S(2)}, u32[]{:S(2)}) collective-permute-start(f32[8,768]{1,0:T(8,128)S(1)} %get-tuple-element.58), channel_id=1, source_target_pairs={{0,1},{1,0},{2,3},{3,2},{4,5},{5,4},{6,7},{7,6},{8,9},{9,8},{10,11... | collective-permute-start | bytes 73736 | tf_op jit(solution)/shard_map/ppermute | solution.py:42
  20.4 1.9 %collective-permute-start.4 = (f32[8,768]{1,0:T(8,128)S(1)}, f32[8,768]{1,0:T(8,128)S(1)}, u32[]{:S(2)}, u32[]{:S(2)}) collective-permute-start(f32[8,768]{1,0:T(8,128)S(1)} %get-tuple-element.59), channel_id=1, source_target_pairs={{1,2},{2,1},{5,6},{6,5},{9,10},{10,9},{13,14},{14,13},{17,18},{18,... | collective-permute-start | bytes 73736 | tf_op jit(solution)/shard_map/ppermute | solution.py:42
  22.3 1.2 collective-permute-done.5
  23.5 0.5 collective-permute-done.3.got_near
  24.0 2.2 %collective-permute-done.4.got_far = f32[8,768]{1,0:T(8,128)S(1)} collective-permute-done((f32[8,768]{1,0:T(8,128)S(1)}, f32[8,768]{1,0:T(8,128)S(1)}, u32[]{:S(2)}, u32[]{:S(2)}) %collective-permute-start.4) | collective-permute-done | bytes 24608 | tf_op jit(solution)/shard_map/ppermute | solution.py:42
  26.2 0.8 collective-permute-start.6
  27.0 3.3 %extract.1 = (f32[4,256,256]{2,1,0:T(8,128)}, f32[4096,128]{1,0:T(8,128)}) custom-call(f32[4,256,8,256]{3,2,1,0:T(8,128)} %schur.2, f32[4,4096,128]{2,1,0:T(8,128)} %bitcast.26), custom_call_target="tpu_custom_call" | custom-call | flops 3000000000 | bytes 1024 | tf_op jit(solution)/shard_map/extract/pallas_call | solution.py:128
  30.4 1.3 collective-permute-start.7
  31.7 9.0 %collective-permute-done.7 = f32[256,256]{1,0:T(8,128)S(1)} collective-permute-done((f32[256,256]{1,0:T(8,128)S(1)}, f32[256,256]{1,0:T(8,128)S(1)}, u32[]{:S(2)}, u32[]{:S(2)}) %collective-permute-start.7) | collective-permute-done | bytes 262176 | tf_op jit(solution)/shard_map/ppermute | solution.py:51
  40.7 1.3 collective-permute-start.8
  42.1 0.7 copy.16.county
  42.8 0.7 pad_add_fusion.tracts
  43.5 0.7 collective-permute-start.9
  44.2 0.8 collective-permute-start.10
  45.0 0.7 broadcast_select_fusion.2.a
  45.7 13.6 %raster.1 = (f32[16,128]{1,0:T(8,128)}, f32[64,128]{1,0:T(8,128)}, f32[512,1024]{1,0:T(8,128)}, f32[512,1024]{1,0:T(8,128)}) custom-call(s32[6]{0:T(128)} %convert_element_type.2.flags, f32[512,1024]{1,0:T(8,128)} %b.1, f32[512,1024]{1,0:T(8,128)} %k_hbm.1, f32[8,1024]{1,0:T(8,128)} %copy-done.3, f32[8,1024]{1,0:T(8,128)} %copy-done.4, f32[8,768]{1,0:T(8,128)} %copy-done.15, ...), custom_call_target="tpu_custom_call" | custom-call | flops 24999999488 | bytes 1024 | tf_op jit(solution)/shard_map/raster/pallas_call | solution.py:377
  59.3 0.0 copy-start.13
  59.3 0.0 copy-start.11
  59.4 1.3 copy-done.11
  60.7 1.3 collective-permute-start.11
  62.0 0.7 broadcast_in_dim.7
  62.7 20.3 %all-to-all-start = ((f32[32,16,128]{2,1,0:T(8,128)}), f32[32,16,128]{2,1,0:T(8,128)S(1)}, u32[]{:S(2)}, u32[]{:S(2)}) async-start(f32[32,16,128]{2,1,0:T(8,128)} %broadcast_in_dim.7), calls=%async_computation | async-start | bytes 524288 | tf_op jit(solution)/shard_map/all_to_all | solution.py:165
  83.1 1.3 collective-permute-start.12
  84.4 14.5 %factor.1.inverse = f32[256,256]{1,0:T(8,128)} custom-call(f32[256,256]{1,0:T(8,128)} %broadcast_select_fusion.2.a), custom_call_target="tpu_custom_call" | custom-call | flops 14000000000 | bytes 1024 | tf_op jit(solution)/shard_map/factor/pallas_call | solution.py:583
  98.9 7.2 %all-to-all-done = f32[32,16,128]{2,1,0:T(8,128)S(1)} async-done(((f32[32,16,128]{2,1,0:T(8,128)}), f32[32,16,128]{2,1,0:T(8,128)S(1)}, u32[]{:S(2)}, u32[]{:S(2)}) %all-to-all-start) | async-done | bytes 262176 | tf_op jit(solution)/shard_map/all_to_all | solution.py:165
  106.1 5.3 %collective-permute-done.12.column_got = f32[4,256,256]{2,1,0:T(8,128)S(1)} collective-permute-done((f32[4,256,256]{2,1,0:T(8,128)}, f32[4,256,256]{2,1,0:T(8,128)S(1)}, u32[]{:S(2)}, u32[]{:S(2)}) %collective-permute-start.12) | collective-permute-done | bytes 1048608 | tf_op jit(solution)/shard_map/ppermute | solution.py:51
  111.4 1.3 copy-done.10
  112.7 2.9 %merge.5.wide_hbm = f32[4096,128]{1,0:T(8,128)} custom-call(s32[1]{0:T(128)} %bitcast.17.flag, f32[4096,128]{1,0:T(8,128)} %copy-done.10, f32[4096,128]{1,0:T(8,128)} %merge.3._), custom_call_target="tpu_custom_call", output_to_operand_aliasing={{}: (2, {})} | custom-call | flops 2000000000 | bytes 1024 | tf_op jit(solution)/shard_map/merge/pallas_call | solution.py:72
  115.7 1.6 %collective-permute-start.13 = (f32[4096,128]{1,0:T(8,128)}, f32[4096,128]{1,0:T(8,128)S(1)}, u32[]{:S(2)}, u32[]{:S(2)}) collective-permute-start(f32[4096,128]{1,0:T(8,128)} %merge.5.wide_hbm), channel_id=1, source_target_pairs={{0,4},{8,12},{16,20},{24,28},{1,5},{9,13},{17,21},{25,29},{2,6},{1... | collective-permute-start | bytes 6291464 | tf_op jit(solution)/shard_map/ppermute | solution.py:51
  117.3 6.5 %finish.1 = (f32[512,1024]{1,0:T(8,128)}, f32[512,1024]{1,0:T(8,128)}, f32[1,64]{1,0:T(1,128)}, f32[4,128]{1,0:T(4,128)}, f32[1,64]{1,0:T(1,128)}) custom-call(f32[512,128]{1,0:T(8,128)} %bitcast.28, f32[64,128]{1,0:T(8,128)} %get-tuple-element.80.sums, s32[4,128]{1,0:T(4,128)} %bitcast.30, f32[512,1024]{1,0:T(8,128)} %b.1, ...), custom_call_target="tpu_custom_call" | custom-call | flops 8000000000 | bytes 1024 | tf_op jit(solution)/shard_map/finish/pallas_call | solution.py:479
  123.8 1.1 slice_bitcast_fusion
  125.0 1.4 copy-done.12
  126.3 17.3 %update.1 = (f32[4,256,256]{2,1,0:T(8,128)}, f32[4,4096,128]{2,1,0:T(8,128)}) custom-call(s32[6]{0:T(128)} %convert_element_type.2.flags, f32[4,256,256]{2,1,0:T(8,128)} %merge.4.column, f32[4,256,256]{2,1,0:T(8,128)} %copy-done.14, f32[4096,128]{1,0:T(8,128)} %merge.5.wide_hbm, f32[4096,128]{1,0:T(8,128)} %copy-done.12, f32[256,256]{1,0:T(8,128)} %factor.1.inverse, ...), custom_call_target="tpu_custom_call" | custom-call | flops 16999999488 | bytes 1024 | tf_op jit(solution)/shard_map/update/pallas_call | solution.py:651
  (38 shorter events, 0.2 us)
Async XLA Ops:
  2.3 6.2 %collective-permute-start.2 = (f32[256,256]{1,0:T(8,128)}, f32[256,256]{1,0:T(8,128)S(1)}, u32[]{:S(2)}, u32[]{:S(2)}) collective-permute-start(f32[256,256]{1,0:T(8,128)} %corner.1), channel_id=1, source_target_pairs={{0,2},{4,6},{8,10},{12,14},{16,18},{20,22},{24,26},{28,30}} | collective-permute-start | bytes 786440 | tf_op jit(solution)/shard_map/ppermute | solution.py:51
  3.7 4.8 %copy-start.5 = (f32[256,256]{1,0:T(8,128)S(1)}, f32[256,256]{1,0:T(8,128)}, u32[]{:S(2)}) copy-start(f32[256,256]{1,0:T(8,128)} %corner.1) | copy-start | bytes 786436
  3.7 9.0 %copy-start = (s32[6]{0:T(128)S(1)}, s32[6]{0:T(128)}, u32[]{:S(2)}) copy-start(s32[6]{0:T(128)} %convert_element_type.2.flags) | copy-start | bytes 76
  6.0 2.6 %collective-permute-start = (f32[8,1024]{1,0:T(8,128)}, f32[8,1024]{1,0:T(8,128)S(1)}, u32[]{:S(2)}, u32[]{:S(2)}) collective-permute-start(f32[8,1024]{1,0:T(8,128)} %get-tuple-element.50), channel_id=1, source_target_pairs={{0,4},{4,0},{8,12},{12,8},{16,20},{20,16},{24,28},{28,24},{1,5},{5... | collective-permute-start | bytes 98312 | tf_op jit(solution)/shard_map/ppermute | solution.py:42
  6.0 5.4 %collective-permute-start.1 = (f32[8,1024]{1,0:T(8,128)}, f32[8,1024]{1,0:T(8,128)S(1)}, u32[]{:S(2)}, u32[]{:S(2)}) collective-permute-start(f32[8,1024]{1,0:T(8,128)} %get-tuple-element.51), channel_id=1, source_target_pairs={{4,8},{12,16},{20,24},{8,4},{16,12},{24,20},{5,9},{13,17},{21,25},... | collective-permute-start | bytes 98312 | tf_op jit(solution)/shard_map/ppermute | solution.py:42
  11.4 12.0 %collective-permute-start.5 = (f32[256,256]{1,0:T(8,128)S(1)}, f32[256,256]{1,0:T(8,128)S(1)}, u32[]{:S(2)}, u32[]{:S(2)}) collective-permute-start(f32[256,256]{1,0:T(8,128)S(1)} %broadcast_select_fusion.4), channel_id=1, source_target_pairs={{0,1},{2,3},{4,5},{6,7},{8,9},{10,11},{12,13},{14,15},{16,17},{18,... | collective-permute-start | bytes 786440 | tf_op jit(solution)/shard_map/ppermute | solution.py:51
  12.7 0.7 copy-start.1
  13.5 0.7 copy-start.2
  14.8 0.6 copy-start.3
  15.5 0.6 copy-start.4
  16.1 7.9 %collective-permute-start.3 = (f32[8,768]{1,0:T(8,128)S(1)}, f32[8,768]{1,0:T(8,128)S(1)}, u32[]{:S(2)}, u32[]{:S(2)}) collective-permute-start(f32[8,768]{1,0:T(8,128)S(1)} %get-tuple-element.58), channel_id=1, source_target_pairs={{0,1},{1,0},{2,3},{3,2},{4,5},{5,4},{6,7},{7,6},{8,9},{9,8},{10,11... | collective-permute-start | bytes 73736 | tf_op jit(solution)/shard_map/ppermute | solution.py:42
  20.4 5.8 %collective-permute-start.4 = (f32[8,768]{1,0:T(8,128)S(1)}, f32[8,768]{1,0:T(8,128)S(1)}, u32[]{:S(2)}, u32[]{:S(2)}) collective-permute-start(f32[8,768]{1,0:T(8,128)S(1)} %get-tuple-element.59), channel_id=1, source_target_pairs={{1,2},{2,1},{5,6},{6,5},{9,10},{10,9},{13,14},{14,13},{17,18},{18,... | collective-permute-start | bytes 73736 | tf_op jit(solution)/shard_map/ppermute | solution.py:42
  24.0 6.3 %copy-start.15 = (f32[8,768]{1,0:T(8,128)}, f32[8,768]{1,0:T(8,128)S(1)}, u32[]{:S(2)}) copy-start(f32[8,768]{1,0:T(8,128)S(1)} %collective-permute-done.3.got_near) | copy-start | bytes 73732
  26.2 4.1 %copy-start.16 = (f32[8,768]{1,0:T(8,128)}, f32[8,768]{1,0:T(8,128)S(1)}, u32[]{:S(2)}) copy-start(f32[8,768]{1,0:T(8,128)S(1)} %collective-permute-done.4.got_far) | copy-start | bytes 73732
  26.2 15.9 %copy-start.9 = (s32[64]{0:T(128)S(1)}, s32[64]{0:T(128)}, u32[]{:S(2)}) copy-start(s32[64]{0:T(128)} %param.9) | copy-start | bytes 772
  26.2 16.6 %copy-start.7 = (s32[32,64]{1,0:T(8,128)S(1)}, s32[32,64]{1,0:T(8,128)}, u32[]{:S(2)}) copy-start(s32[32,64]{1,0:T(8,128)} %param.8) | copy-start | bytes 24580
  26.2 4.1 %collective-permute-start.6 = (f32[256,256]{1,0:T(8,128)S(1)}, f32[256,256]{1,0:T(8,128)S(1)}, u32[]{:S(2)}, u32[]{:S(2)}) collective-permute-start(f32[256,256]{1,0:T(8,128)S(1)} %broadcast_select_fusion.3), channel_id=1, source_target_pairs={{0,16},{1,17},{2,18},{3,19}} | collective-permute-start | bytes 786440 | tf_op jit(solution)/shard_map/ppermute | solution.py:51
  30.4 10.3 %collective-permute-start.7 = (f32[256,256]{1,0:T(8,128)S(1)}, f32[256,256]{1,0:T(8,128)S(1)}, u32[]{:S(2)}, u32[]{:S(2)}) collective-permute-start(f32[256,256]{1,0:T(8,128)S(1)} %broadcast_select_fusion), channel_id=1, source_target_pairs={{0,8},{16,24},{1,9},{17,25},{2,10},{18,26},{3,11},{19,27}} | collective-permute-start | bytes 786440 | tf_op jit(solution)/shard_map/ppermute | solution.py:51
  40.7 4.2 %collective-permute-start.8 = (f32[256,256]{1,0:T(8,128)S(1)}, f32[256,256]{1,0:T(8,128)S(1)}, u32[]{:S(2)}, u32[]{:S(2)}) collective-permute-start(f32[256,256]{1,0:T(8,128)S(1)} %broadcast_select_fusion.1), channel_id=1, source_target_pairs={{0,4},{8,12},{16,20},{24,28},{1,5},{9,13},{17,21},{25,29},{2,6},{1... | collective-permute-start | bytes 786440 | tf_op jit(solution)/shard_map/ppermute | solution.py:51
  43.5 15.9 %collective-permute-start.9 = (f32[4,256,256]{2,1,0:T(8,128)}, f32[4,256,256]{2,1,0:T(8,128)S(1)}, u32[]{:S(2)}, u32[]{:S(2)}) collective-permute-start(f32[4,256,256]{2,1,0:T(8,128)} %get-tuple-element.73._), channel_id=1, source_target_pairs={{0,2},{4,6},{8,10},{12,14},{16,18},{20,22},{24,26},{28,30}} | collective-permute-start | bytes 3145736 | tf_op jit(solution)/shard_map/ppermute | solution.py:51
  44.2 15.2 %collective-permute-start.10 = (f32[4096,128]{1,0:T(8,128)}, f32[4096,128]{1,0:T(8,128)S(1)}, u32[]{:S(2)}, u32[]{:S(2)}) collective-permute-start(f32[4096,128]{1,0:T(8,128)} %get-tuple-element.74._), channel_id=1, source_target_pairs={{0,16},{1,17},{2,18},{3,19}} | collective-permute-start | bytes 6291464 | tf_op jit(solution)/shard_map/ppermute | solution.py:51
  59.3 23.7 %copy-start.13 = (f32[4,256,256]{2,1,0:T(8,128)}, f32[4,256,256]{2,1,0:T(8,128)S(1)}, u32[]{:S(2)}) copy-start(f32[4,256,256]{2,1,0:T(8,128)S(1)} %collective-permute-done.9.got) | copy-start | bytes 3145732
  59.3 1.4 copy-start.11
  60.7 1.3 copy-start.8
  60.7 50.7 %collective-permute-start.11 = (f32[4096,128]{1,0:T(8,128)}, f32[4096,128]{1,0:T(8,128)S(1)}, u32[]{:S(2)}, u32[]{:S(2)}) collective-permute-start(f32[4096,128]{1,0:T(8,128)} %merge.3._), channel_id=1, source_target_pairs={{0,8},{16,24},{1,9},{17,25},{2,10},{18,26},{3,11},{19,27}} | collective-permute-start | bytes 6291464 | tf_op jit(solution)/shard_map/ppermute | solution.py:51
  62.7 43.4 %all-to-all-start = ((f32[32,16,128]{2,1,0:T(8,128)}), f32[32,16,128]{2,1,0:T(8,128)S(1)}, u32[]{:S(2)}, u32[]{:S(2)}) async-start(f32[32,16,128]{2,1,0:T(8,128)} %broadcast_in_dim.7), calls=%async_computation | async-start | bytes 524288 | tf_op jit(solution)/shard_map/all_to_all | solution.py:165
  83.1 28.3 %collective-permute-start.12 = (f32[4,256,256]{2,1,0:T(8,128)}, f32[4,256,256]{2,1,0:T(8,128)S(1)}, u32[]{:S(2)}, u32[]{:S(2)}) collective-permute-start(f32[4,256,256]{2,1,0:T(8,128)} %merge.4.column), channel_id=1, source_target_pairs={{0,1},{2,3},{4,5},{6,7},{8,9},{10,11},{12,13},{14,15},{16,17},{18,... | collective-permute-start | bytes 3145736 | tf_op jit(solution)/shard_map/ppermute | solution.py:51
  106.1 9.6 %copy-start.6 = (f32[32,16,128]{2,1,0:T(8,128)}, f32[32,16,128]{2,1,0:T(8,128)S(1)}, u32[]{:S(2)}) copy-start(f32[32,16,128]{2,1,0:T(8,128)S(1)} %all-to-all-done) | copy-start | bytes 786436
  111.4 12.4 %copy-start.14 = (f32[4,256,256]{2,1,0:T(8,128)}, f32[4,256,256]{2,1,0:T(8,128)S(1)}, u32[]{:S(2)}) copy-start(f32[4,256,256]{2,1,0:T(8,128)S(1)} %collective-permute-done.12.column_got) | copy-start | bytes 3145732
  111.4 1.3 copy-start.10
  115.7 9.3 %collective-permute-start.13 = (f32[4096,128]{1,0:T(8,128)}, f32[4096,128]{1,0:T(8,128)S(1)}, u32[]{:S(2)}, u32[]{:S(2)}) collective-permute-start(f32[4096,128]{1,0:T(8,128)} %merge.5.wide_hbm), channel_id=1, source_target_pairs={{0,4},{8,12},{16,20},{24,28},{1,5},{9,13},{17,21},{25,29},{2,6},{1... | collective-permute-start | bytes 6291464 | tf_op jit(solution)/shard_map/ppermute | solution.py:51
  124.9 1.4 copy-start.12

commit v4 on v3

--- a/solution.py
+++ b/solution.py
@@ -388,7 +388,7 @@
         + [pltpu.VMEM((rows // BLOCK, cols), F32)] * 2
         + [pltpu.SemaphoreType.DMA((2,))],
         compiler_params=params(60),
-        cost_estimate=cost(25),
+        cost_estimate=cost(1),
         name="raster",
     )(flags, b, kappa, above, below, got_near, got_far, tracts, county)
 
@@ -468,7 +468,7 @@
 
 def finish(got, sums, state, b, two, four):
     rows, cols = b.shape
-    step = 128
+    step = 256
     devices = got.shape[0] // 16
 
     def fixed(shape):
@@ -587,7 +587,7 @@
         out_specs=pl.BlockSpec(memory_space=pltpu.VMEM),
         scratch_shapes=[half, half],
         compiler_params=params(60),
-        cost_estimate=cost(14),
+        cost_estimate=cost(1),
         name="factor",
     )(a)
 

time: 145 us -> 130 us (0.90)
  starting transfers between devices: 40.1 us -> 30 us
  waiting for transfers between devices: 28.1 us -> 24.4 us
    all_to_all x1, starting transfers between devices: 20.3 us -> 9.21 us  [exchange(): lax.all_to_all(jnp.broadcast_to(mine, (devices,) + mine.shape), axes, 0, 0)]
    ppermute x10, waiting for transfers between devices: 15.5 us -> 12.2 us  [hop(): return lax.ppermute(block, axis, pairs)]
    unnamed x34 -> x32, local copies, waits for them, and re-layouts: 6.77 us -> 6.71 us
  transfers between devices with their start and end apart: 15 -> 15, of which waited for: 7 -> 6; matrix products, arithmetic and copies ran while one was open for 3% -> 4% of each run, Pallas kernels for 28% -> 31%
where the time goes in v4:
time: 130 us; the launch traced here: 129 us
  Pallas kernels  61.8 us (48%)
  starting transfers between devices  30 us (23%)
  waiting for transfers between devices  24.4 us (19%)
  local copies, waits for them, and re-layouts  9.42 us (7%)
  other arithmetic  2.04 us (2%)
    pallas_call x1, Pallas kernels, update(): pl.pallas_call(update_kernel, grid=(count_rows,), out_shape=(jax.ShapeDty...  17.3 us
    pallas_call x1, Pallas kernels, factor(): pl.pallas_call(factor_kernel, out_shape=jax.ShapeDtypeStruct(a.shape, F32...  14.5 us
    pallas_call x1, Pallas kernels, raster(): pl.pallas_call(raster_kernel, out_shape=(jax.ShapeDtypeStruct((16, LANES)...  13.6 us
    ppermute x10, waiting for transfers between devices, hop(): return lax.ppermute(block, axis, pairs)  12.2 us
    ppermute x10, starting transfers between devices, hop(): return lax.ppermute(block, axis, pairs)  12 us
    all_to_all x1, starting transfers between devices, exchange(): lax.all_to_all(jnp.broadcast_to(mine, (devices,) + mine.shape), axes, 0, 0)  9.21 us
    ppermute x4, starting transfers between devices, trade(): return (lax.ppermute(near, axis, inside), lax.ppermute(far, axis, between))  8.75 us
    unnamed x32, local copies, waits for them, and re-layouts  6.71 us
  transfers between devices with their start and end apart: 15, of which 6 were waited for; matrix products, arithmetic and copies ran while one was open for 4% of the time, Pallas kernels for 31%

profile of v4, /device:TPU:10, one launch (start us, length us, event | category | flops | bytes accessed | tf_op | source)
XLA Modules:
  0.0 128.8 jit_solution(4101752176434118435)
XLA Ops:
  0.6 1.7 %corner.1 = f32[256,256]{1,0:T(8,128)} custom-call(f32[4,256,8,256]{3,2,1,0:T(8,128)} %schur.2), custom_call_target="tpu_custom_call" | custom-call | flops 2000000000 | bytes 1024 | tf_op jit(solution)/shard_map/corner/pallas_call | solution.py:113
  2.3 0.7 collective-permute-start.2
  3.1 0.1 stack.27
  3.2 0.5 convert_element_type.2.flags
  3.7 2.3 %edges.1 = (f32[8,1024]{1,0:T(8,128)}, f32[8,1024]{1,0:T(8,128)}, f32[8,512]{1,0:T(8,128)}, f32[8,512]{1,0:T(8,128)}) custom-call(s32[6]{0:T(128)} %convert_element_type.2.flags, f32[512,1024]{1,0:T(8,128)} %b.1, f32[512,1024]{1,0:T(8,128)} %b.1, f32[512,1024]{1,0:T(8,128)} %k_hbm.1, f32[512,1024]{1,0:T(8,128)} %k_hbm.1, f32[512,1024]{1,0:T(8,128)} %b.1, ...), custom_call_target="tpu_custom_call" | custom-call | flops 2000000000 | bytes 1024 | tf_op jit(solution)/shard_map/edges/pallas_call | solution.py:189
  5.9 2.5 %collective-permute-start.1 = (f32[8,1024]{1,0:T(8,128)}, f32[8,1024]{1,0:T(8,128)S(1)}, u32[]{:S(2)}, u32[]{:S(2)}) collective-permute-start(f32[8,1024]{1,0:T(8,128)} %get-tuple-element.51), channel_id=1, source_target_pairs={{4,8},{12,16},{20,24},{8,4},{16,12},{24,20},{5,9},{13,17},{21,25},... | collective-permute-start | bytes 98312 | tf_op jit(solution)/shard_map/ppermute | solution.py:42
  8.5 0.0 collective-permute-done.got_near
  8.6 2.8 %collective-permute-done.1.got_far = f32[8,1024]{1,0:T(8,128)S(1)} collective-permute-done((f32[8,1024]{1,0:T(8,128)}, f32[8,1024]{1,0:T(8,128)S(1)}, u32[]{:S(2)}, u32[]{:S(2)}) %collective-permute-start.1) | collective-permute-done | bytes 32800 | tf_op jit(solution)/shard_map/ppermute | solution.py:42
  11.3 1.3 collective-permute-start.5
  12.7 0.0 copy-start.3
  12.7 0.7 copy-done.3
  13.4 0.7 copy-done.4
  14.1 0.7 corners.1
  14.8 0.0 copy-start
  14.8 0.6 copy-done
  15.4 0.6 copy-done.1
  16.0 4.3 %collective-permute-start.3 = (f32[8,768]{1,0:T(8,128)S(1)}, f32[8,768]{1,0:T(8,128)S(1)}, u32[]{:S(2)}, u32[]{:S(2)}) collective-permute-start(f32[8,768]{1,0:T(8,128)S(1)} %get-tuple-element.58), channel_id=1, source_target_pairs={{0,1},{1,0},{2,3},{3,2},{4,5},{5,4},{6,7},{7,6},{8,9},{9,8},{10,11... | collective-permute-start | bytes 73736 | tf_op jit(solution)/shard_map/ppermute | solution.py:42
  20.3 1.9 %collective-permute-start.4 = (f32[8,768]{1,0:T(8,128)S(1)}, f32[8,768]{1,0:T(8,128)S(1)}, u32[]{:S(2)}, u32[]{:S(2)}) collective-permute-start(f32[8,768]{1,0:T(8,128)S(1)} %get-tuple-element.59), channel_id=1, source_target_pairs={{1,2},{2,1},{5,6},{6,5},{9,10},{10,9},{13,14},{14,13},{17,18},{18,... | collective-permute-start | bytes 73736 | tf_op jit(solution)/shard_map/ppermute | solution.py:42
  22.2 1.2 collective-permute-done.5
  23.4 0.5 collective-permute-done.3.got_near
  23.9 2.2 %collective-permute-done.4.got_far = f32[8,768]{1,0:T(8,128)S(1)} collective-permute-done((f32[8,768]{1,0:T(8,128)S(1)}, f32[8,768]{1,0:T(8,128)S(1)}, u32[]{:S(2)}, u32[]{:S(2)}) %collective-permute-start.4) | collective-permute-done | bytes 24608 | tf_op jit(solution)/shard_map/ppermute | solution.py:42
  26.1 0.8 collective-permute-start.6
  26.9 3.3 %extract.1 = (f32[4,256,256]{2,1,0:T(8,128)}, f32[4096,128]{1,0:T(8,128)}) custom-call(f32[4,256,8,256]{3,2,1,0:T(8,128)} %schur.2, f32[4,4096,128]{2,1,0:T(8,128)} %bitcast.26), custom_call_target="tpu_custom_call" | custom-call | flops 3000000000 | bytes 1024 | tf_op jit(solution)/shard_map/extract/pallas_call | solution.py:128
  30.3 0.8 collective-permute-start.10
  31.1 1.3 %collective-permute-start.7 = (f32[256,256]{1,0:T(8,128)S(1)}, f32[256,256]{1,0:T(8,128)S(1)}, u32[]{:S(2)}, u32[]{:S(2)}) collective-permute-start(f32[256,256]{1,0:T(8,128)S(1)} %broadcast_select_fusion), channel_id=1, source_target_pairs={{0,8},{16,24},{1,9},{17,25},{2,10},{18,26},{3,11},{19,27}} | collective-permute-start | bytes 786440 | tf_op jit(solution)/shard_map/ppermute | solution.py:51
  32.4 1.7 %collective-permute-start.9 = (f32[4,256,256]{2,1,0:T(8,128)}, f32[4,256,256]{2,1,0:T(8,128)}, u32[]{:S(2)}, u32[]{:S(2)}) collective-permute-start(f32[4,256,256]{2,1,0:T(8,128)} %get-tuple-element.73._), channel_id=1, source_target_pairs={{0,2},{4,6},{8,10},{12,14},{16,18},{20,22},{24,26},{28,30}} | collective-permute-start | bytes 3145736 | tf_op jit(solution)/shard_map/ppermute | solution.py:51
  34.1 11.1 %collective-permute-done.7 = f32[256,256]{1,0:T(8,128)S(1)} collective-permute-done((f32[256,256]{1,0:T(8,128)S(1)}, f32[256,256]{1,0:T(8,128)S(1)}, u32[]{:S(2)}, u32[]{:S(2)}) %collective-permute-start.7) | collective-permute-done | bytes 262176 | tf_op jit(solution)/shard_map/ppermute | solution.py:51
  45.2 1.3 %collective-permute-start.8 = (f32[256,256]{1,0:T(8,128)S(1)}, f32[256,256]{1,0:T(8,128)S(1)}, u32[]{:S(2)}, u32[]{:S(2)}) collective-permute-start(f32[256,256]{1,0:T(8,128)S(1)} %broadcast_select_fusion.1), channel_id=1, source_target_pairs={{0,4},{8,12},{16,20},{24,28},{1,5},{9,13},{17,21},{25,29},{2,6},{1... | collective-permute-start | bytes 786440 | tf_op jit(solution)/shard_map/ppermute | solution.py:51
  46.5 0.7 copy.16.county
  47.2 0.7 pad_add_fusion.tracts
  47.9 0.7 broadcast_select_fusion.2.a
  48.6 13.6 %raster.1 = (f32[16,128]{1,0:T(8,128)}, f32[64,128]{1,0:T(8,128)}, f32[512,1024]{1,0:T(8,128)}, f32[512,1024]{1,0:T(8,128)}) custom-call(s32[6]{0:T(128)} %convert_element_type.2.flags, f32[512,1024]{1,0:T(8,128)} %b.1, f32[512,1024]{1,0:T(8,128)} %k_hbm.1, f32[8,1024]{1,0:T(8,128)} %copy-done, f32[8,1024]{1,0:T(8,128)} %copy-done.1, f32[8,768]{1,0:T(8,128)} %copy-done.7, ...), custom_call_target="tpu_custom_call" | custom-call | flops 1000000000 | bytes 1024 | tf_op jit(solution)/shard_map/raster/pallas_call | solution.py:377
  62.2 0.0 copy-start.12
  62.2 1.3 %copy-done.12 = f32[4096,128]{1,0:T(8,128)} copy-done((f32[4096,128]{1,0:T(8,128)}, f32[4096,128]{1,0:T(8,128)S(1)}, u32[]{:S(2)}) %copy-start.12) | copy-done | bytes 2097176
  63.6 1.3 %collective-permute-start.11 = (f32[4096,128]{1,0:T(8,128)}, f32[4096,128]{1,0:T(8,128)S(1)}, u32[]{:S(2)}, u32[]{:S(2)}) collective-permute-start(f32[4096,128]{1,0:T(8,128)} %merge.3._), channel_id=1, source_target_pairs={{0,8},{16,24},{1,9},{17,25},{2,10},{18,26},{3,11},{19,27}} | collective-permute-start | bytes 6291464 | tf_op jit(solution)/shard_map/ppermute | solution.py:51
  64.9 1.3 %collective-permute-start.12 = (f32[4,256,256]{2,1,0:T(8,128)}, f32[4,256,256]{2,1,0:T(8,128)S(1)}, u32[]{:S(2)}, u32[]{:S(2)}) collective-permute-start(f32[4,256,256]{2,1,0:T(8,128)} %merge.4.column), channel_id=1, source_target_pairs={{0,1},{2,3},{4,5},{6,7},{8,9},{10,11},{12,13},{14,15},{16,17},{18,... | collective-permute-start | bytes 3145736 | tf_op jit(solution)/shard_map/ppermute | solution.py:51
  66.2 0.7 broadcast_in_dim.7
  66.9 9.2 %all-to-all-start = ((f32[32,16,128]{2,1,0:T(8,128)}), f32[32,16,128]{2,1,0:T(8,128)S(1)}, u32[]{:S(2)}, u32[]{:S(2)}) async-start(f32[32,16,128]{2,1,0:T(8,128)} %broadcast_in_dim.7), calls=%async_computation | async-start | bytes 524288 | tf_op jit(solution)/shard_map/all_to_all | solution.py:165
  76.1 14.5 %factor.1.inverse = f32[256,256]{1,0:T(8,128)} custom-call(f32[256,256]{1,0:T(8,128)} %broadcast_select_fusion.2.a), custom_call_target="tpu_custom_call" | custom-call | flops 1000000000 | bytes 1024 | tf_op jit(solution)/shard_map/factor/pallas_call | solution.py:583
  90.7 6.7 %all-to-all-done = f32[32,16,128]{2,1,0:T(8,128)S(1)} async-done(((f32[32,16,128]{2,1,0:T(8,128)}), f32[32,16,128]{2,1,0:T(8,128)S(1)}, u32[]{:S(2)}, u32[]{:S(2)}) %all-to-all-start) | async-done | bytes 262176 | tf_op jit(solution)/shard_map/all_to_all | solution.py:165
  97.4 0.0 copy-start.13
  97.4 1.3 %copy-done.13 = f32[4096,128]{1,0:T(8,128)} copy-done((f32[4096,128]{1,0:T(8,128)}, f32[4096,128]{1,0:T(8,128)S(1)}, u32[]{:S(2)}) %copy-start.13) | copy-done | bytes 2097176
  98.7 2.9 %merge.5.wide_hbm = f32[4096,128]{1,0:T(8,128)} custom-call(s32[1]{0:T(128)} %bitcast.17.flag, f32[4096,128]{1,0:T(8,128)} %copy-done.13, f32[4096,128]{1,0:T(8,128)} %merge.3._), custom_call_target="tpu_custom_call", output_to_operand_aliasing={{}: (2, {})} | custom-call | flops 2000000000 | bytes 1024 | tf_op jit(solution)/shard_map/merge/pallas_call | solution.py:72
  101.7 1.6 %collective-permute-start.13 = (f32[4096,128]{1,0:T(8,128)}, f32[4096,128]{1,0:T(8,128)S(1)}, u32[]{:S(2)}, u32[]{:S(2)}) collective-permute-start(f32[4096,128]{1,0:T(8,128)} %merge.5.wide_hbm), channel_id=1, source_target_pairs={{0,4},{8,12},{16,20},{24,28},{1,5},{9,13},{17,21},{25,29},{2,6},{1... | collective-permute-start | bytes 6291464 | tf_op jit(solution)/shard_map/ppermute | solution.py:51
  103.3 5.6 %finish.1 = (f32[512,1024]{1,0:T(8,128)}, f32[512,1024]{1,0:T(8,128)}, f32[1,64]{1,0:T(1,128)}, f32[4,128]{1,0:T(4,128)}, f32[1,64]{1,0:T(1,128)}) custom-call(f32[512,128]{1,0:T(8,128)} %bitcast.28, f32[64,128]{1,0:T(8,128)} %get-tuple-element.80.sums, s32[4,128]{1,0:T(4,128)} %bitcast.30, f32[512,1024]{1,0:T(8,128)} %b.1, ...), custom_call_target="tpu_custom_call" | custom-call | flops 8000000000 | bytes 1024 | tf_op jit(solution)/shard_map/finish/pallas_call | solution.py:479
  108.8 1.2 slice_bitcast_fusion
  110.0 1.4 %copy-done.14 = f32[4096,128]{1,0:T(8,128)} copy-done((f32[4096,128]{1,0:T(8,128)}, f32[4096,128]{1,0:T(8,128)S(1)}, u32[]{:S(2)}) %copy-start.14) | copy-done | bytes 2097176
  111.4 17.3 %update.1 = (f32[4,256,256]{2,1,0:T(8,128)}, f32[4,4096,128]{2,1,0:T(8,128)}) custom-call(s32[6]{0:T(128)} %convert_element_type.2.flags, f32[4,256,256]{2,1,0:T(8,128)} %merge.4.column, f32[4,256,256]{2,1,0:T(8,128)} %copy-done.15, f32[4096,128]{1,0:T(8,128)} %merge.5.wide_hbm, f32[4096,128]{1,0:T(8,128)} %copy-done.14, f32[256,256]{1,0:T(8,128)} %factor.1.inverse, ...), custom_call_target="tpu_custom_call" | custom-call | flops 16999999488 | bytes 1024 | tf_op jit(solution)/shard_map/update/pallas_call | solution.py:651
  (36 shorter events, 0.2 us)
Async XLA Ops:
  2.3 6.1 %collective-permute-start.2 = (f32[256,256]{1,0:T(8,128)}, f32[256,256]{1,0:T(8,128)S(1)}, u32[]{:S(2)}, u32[]{:S(2)}) collective-permute-start(f32[256,256]{1,0:T(8,128)} %corner.1), channel_id=1, source_target_pairs={{0,2},{4,6},{8,10},{12,14},{16,18},{20,22},{24,26},{28,30}} | collective-permute-start | bytes 786440 | tf_op jit(solution)/shard_map/ppermute | solution.py:51
  3.6 4.8 %copy-start.5 = (f32[256,256]{1,0:T(8,128)S(1)}, f32[256,256]{1,0:T(8,128)}, u32[]{:S(2)}) copy-start(f32[256,256]{1,0:T(8,128)} %corner.1) | copy-start | bytes 786436
  3.7 9.0 %copy-start.2 = (s32[6]{0:T(128)S(1)}, s32[6]{0:T(128)}, u32[]{:S(2)}) copy-start(s32[6]{0:T(128)} %convert_element_type.2.flags) | copy-start | bytes 76
  5.9 2.6 %collective-permute-start = (f32[8,1024]{1,0:T(8,128)}, f32[8,1024]{1,0:T(8,128)S(1)}, u32[]{:S(2)}, u32[]{:S(2)}) collective-permute-start(f32[8,1024]{1,0:T(8,128)} %get-tuple-element.50), channel_id=1, source_target_pairs={{0,4},{4,0},{8,12},{12,8},{16,20},{20,16},{24,28},{28,24},{1,5},{5... | collective-permute-start | bytes 98312 | tf_op jit(solution)/shard_map/ppermute | solution.py:42
  5.9 5.4 %collective-permute-start.1 = (f32[8,1024]{1,0:T(8,128)}, f32[8,1024]{1,0:T(8,128)S(1)}, u32[]{:S(2)}, u32[]{:S(2)}) collective-permute-start(f32[8,1024]{1,0:T(8,128)} %get-tuple-element.51), channel_id=1, source_target_pairs={{4,8},{12,16},{20,24},{8,4},{16,12},{24,20},{5,9},{13,17},{21,25},... | collective-permute-start | bytes 98312 | tf_op jit(solution)/shard_map/ppermute | solution.py:42
  11.3 12.0 %collective-permute-start.5 = (f32[256,256]{1,0:T(8,128)S(1)}, f32[256,256]{1,0:T(8,128)S(1)}, u32[]{:S(2)}, u32[]{:S(2)}) collective-permute-start(f32[256,256]{1,0:T(8,128)S(1)} %broadcast_select_fusion.4), channel_id=1, source_target_pairs={{0,1},{2,3},{4,5},{6,7},{8,9},{10,11},{12,13},{14,15},{16,17},{18,... | collective-permute-start | bytes 786440 | tf_op jit(solution)/shard_map/ppermute | solution.py:51
  12.7 0.7 copy-start.3
  13.4 0.7 copy-start.4
  14.8 0.6 copy-start
  15.4 0.6 copy-start.1
  16.0 7.9 %collective-permute-start.3 = (f32[8,768]{1,0:T(8,128)S(1)}, f32[8,768]{1,0:T(8,128)S(1)}, u32[]{:S(2)}, u32[]{:S(2)}) collective-permute-start(f32[8,768]{1,0:T(8,128)S(1)} %get-tuple-element.58), channel_id=1, source_target_pairs={{0,1},{1,0},{2,3},{3,2},{4,5},{5,4},{6,7},{7,6},{8,9},{9,8},{10,11... | collective-permute-start | bytes 73736 | tf_op jit(solution)/shard_map/ppermute | solution.py:42
  20.3 5.8 %collective-permute-start.4 = (f32[8,768]{1,0:T(8,128)S(1)}, f32[8,768]{1,0:T(8,128)S(1)}, u32[]{:S(2)}, u32[]{:S(2)}) collective-permute-start(f32[8,768]{1,0:T(8,128)S(1)} %get-tuple-element.59), channel_id=1, source_target_pairs={{1,2},{2,1},{5,6},{6,5},{9,10},{10,9},{13,14},{14,13},{17,18},{18,... | collective-permute-start | bytes 73736 | tf_op jit(solution)/shard_map/ppermute | solution.py:42
  23.9 6.3 %copy-start.7 = (f32[8,768]{1,0:T(8,128)}, f32[8,768]{1,0:T(8,128)S(1)}, u32[]{:S(2)}) copy-start(f32[8,768]{1,0:T(8,128)S(1)} %collective-permute-done.3.got_near) | copy-start | bytes 73732
  26.1 4.1 %copy-start.8 = (f32[8,768]{1,0:T(8,128)}, f32[8,768]{1,0:T(8,128)S(1)}, u32[]{:S(2)}) copy-start(f32[8,768]{1,0:T(8,128)S(1)} %collective-permute-done.4.got_far) | copy-start | bytes 73732
  26.1 20.4 %copy-start.11 = (s32[64]{0:T(128)S(1)}, s32[64]{0:T(128)}, u32[]{:S(2)}) copy-start(s32[64]{0:T(128)} %param.9) | copy-start | bytes 772
  26.1 21.1 %copy-start.9 = (s32[32,64]{1,0:T(8,128)S(1)}, s32[32,64]{1,0:T(8,128)}, u32[]{:S(2)}) copy-start(s32[32,64]{1,0:T(8,128)} %param.8) | copy-start | bytes 24580
  26.1 4.1 %collective-permute-start.6 = (f32[256,256]{1,0:T(8,128)S(1)}, f32[256,256]{1,0:T(8,128)S(1)}, u32[]{:S(2)}, u32[]{:S(2)}) collective-permute-start(f32[256,256]{1,0:T(8,128)S(1)} %broadcast_select_fusion.3), channel_id=1, source_target_pairs={{0,16},{1,17},{2,18},{3,19}} | collective-permute-start | bytes 786440 | tf_op jit(solution)/shard_map/ppermute | solution.py:51
  30.3 31.9 %collective-permute-start.10 = (f32[4096,128]{1,0:T(8,128)}, f32[4096,128]{1,0:T(8,128)S(1)}, u32[]{:S(2)}, u32[]{:S(2)}) collective-permute-start(f32[4096,128]{1,0:T(8,128)} %get-tuple-element.74._), channel_id=1, source_target_pairs={{0,16},{1,17},{2,18},{3,19}} | collective-permute-start | bytes 6291464 | tf_op jit(solution)/shard_map/ppermute | solution.py:51
  31.1 14.0 %collective-permute-start.7 = (f32[256,256]{1,0:T(8,128)S(1)}, f32[256,256]{1,0:T(8,128)S(1)}, u32[]{:S(2)}, u32[]{:S(2)}) collective-permute-start(f32[256,256]{1,0:T(8,128)S(1)} %broadcast_select_fusion), channel_id=1, source_target_pairs={{0,8},{16,24},{1,9},{17,25},{2,10},{18,26},{3,11},{19,27}} | collective-permute-start | bytes 786440 | tf_op jit(solution)/shard_map/ppermute | solution.py:51
  32.4 29.8 %collective-permute-start.9 = (f32[4,256,256]{2,1,0:T(8,128)}, f32[4,256,256]{2,1,0:T(8,128)}, u32[]{:S(2)}, u32[]{:S(2)}) collective-permute-start(f32[4,256,256]{2,1,0:T(8,128)} %get-tuple-element.73._), channel_id=1, source_target_pairs={{0,2},{4,6},{8,10},{12,14},{16,18},{20,22},{24,26},{28,30}} | collective-permute-start | bytes 3145736 | tf_op jit(solution)/shard_map/ppermute | solution.py:51
  45.2 2.7 %collective-permute-start.8 = (f32[256,256]{1,0:T(8,128)S(1)}, f32[256,256]{1,0:T(8,128)S(1)}, u32[]{:S(2)}, u32[]{:S(2)}) collective-permute-start(f32[256,256]{1,0:T(8,128)S(1)} %broadcast_select_fusion.1), channel_id=1, source_target_pairs={{0,4},{8,12},{16,20},{24,28},{1,5},{9,13},{17,21},{25,29},{2,6},{1... | collective-permute-start | bytes 786440 | tf_op jit(solution)/shard_map/ppermute | solution.py:51
  62.2 1.3 %copy-start.12 = (f32[4096,128]{1,0:T(8,128)}, f32[4096,128]{1,0:T(8,128)S(1)}, u32[]{:S(2)}) copy-start(f32[4096,128]{1,0:T(8,128)S(1)} %collective-permute-done.10.got) | copy-start | bytes 6291460
  63.6 33.8 %collective-permute-start.11 = (f32[4096,128]{1,0:T(8,128)}, f32[4096,128]{1,0:T(8,128)S(1)}, u32[]{:S(2)}, u32[]{:S(2)}) collective-permute-start(f32[4096,128]{1,0:T(8,128)} %merge.3._), channel_id=1, source_target_pairs={{0,8},{16,24},{1,9},{17,25},{2,10},{18,26},{3,11},{19,27}} | collective-permute-start | bytes 6291464 | tf_op jit(solution)/shard_map/ppermute | solution.py:51
  64.9 1.3 %copy-start.10 = (f32[16,128]{1,0:T(8,128)S(1)}, f32[16,128]{1,0:T(8,128)}, u32[]{:S(2)}) copy-start(f32[16,128]{1,0:T(8,128)} %get-tuple-element.76) | copy-start | bytes 24580
  64.9 32.5 %collective-permute-start.12 = (f32[4,256,256]{2,1,0:T(8,128)}, f32[4,256,256]{2,1,0:T(8,128)S(1)}, u32[]{:S(2)}, u32[]{:S(2)}) collective-permute-start(f32[4,256,256]{2,1,0:T(8,128)} %merge.4.column), channel_id=1, source_target_pairs={{0,1},{2,3},{4,5},{6,7},{8,9},{10,11},{12,13},{14,15},{16,17},{18,... | collective-permute-start | bytes 3145736 | tf_op jit(solution)/shard_map/ppermute | solution.py:51
  66.9 30.4 %all-to-all-start = ((f32[32,16,128]{2,1,0:T(8,128)}), f32[32,16,128]{2,1,0:T(8,128)S(1)}, u32[]{:S(2)}, u32[]{:S(2)}) async-start(f32[32,16,128]{2,1,0:T(8,128)} %broadcast_in_dim.7), calls=%async_computation | async-start | bytes 524288 | tf_op jit(solution)/shard_map/all_to_all | solution.py:165
  97.4 4.3 %copy-start.6 = (f32[32,16,128]{2,1,0:T(8,128)}, f32[32,16,128]{2,1,0:T(8,128)S(1)}, u32[]{:S(2)}) copy-start(f32[32,16,128]{2,1,0:T(8,128)S(1)} %all-to-all-done) | copy-start | bytes 786436
  97.4 11.5 %copy-start.15 = (f32[4,256,256]{2,1,0:T(8,128)}, f32[4,256,256]{2,1,0:T(8,128)S(1)}, u32[]{:S(2)}) copy-start(f32[4,256,256]{2,1,0:T(8,128)S(1)} %collective-permute-done.12.column_got) | copy-start | bytes 3145732
  97.4 1.3 %copy-start.13 = (f32[4096,128]{1,0:T(8,128)}, f32[4096,128]{1,0:T(8,128)S(1)}, u32[]{:S(2)}) copy-start(f32[4096,128]{1,0:T(8,128)S(1)} %collective-permute-done.11.got) | copy-start | bytes 6291460
  101.7 8.3 %collective-permute-start.13 = (f32[4096,128]{1,0:T(8,128)}, f32[4096,128]{1,0:T(8,128)S(1)}, u32[]{:S(2)}, u32[]{:S(2)}) collective-permute-start(f32[4096,128]{1,0:T(8,128)} %merge.5.wide_hbm), channel_id=1, source_target_pairs={{0,4},{8,12},{16,20},{24,28},{1,5},{9,13},{17,21},{25,29},{2,6},{1... | collective-permute-start | bytes 6291464 | tf_op jit(solution)/shard_map/ppermute | solution.py:51
  110.0 1.4 %copy-start.14 = (f32[4096,128]{1,0:T(8,128)}, f32[4096,128]{1,0:T(8,128)S(1)}, u32[]{:S(2)}) copy-start(f32[4096,128]{1,0:T(8,128)S(1)} %collective-permute-done.13.wide_got) | copy-start | bytes 6291460

commit v5 on v4

--- a/solution.py
+++ b/solution.py
@@ -337,12 +337,12 @@
 
     zero = jnp.zeros((8, cols), F32)
     edges(bx, v1)
-    sum_0, sum_1 = lax.fori_loop(0, rows // BLOCK, sweep_one, (zero, zero), unroll=4)
+    sum_0, sum_1 = lax.fori_loop(0, rows // BLOCK, sweep_one, (zero, zero), unroll=8)
     edges(v1, v2)
-    sum_2 = lax.fori_loop(0, rows // BLOCK, sweep_two, zero, unroll=4)
+    sum_2 = lax.fori_loop(0, rows // BLOCK, sweep_two, zero, unroll=8)
     edges(v2, v3)
-    sum_3 = lax.fori_loop(0, rows // 8, sweep_three, zero, unroll=8)
-    lax.fori_loop(0, rows // 8, sweep_four, 0, unroll=8)
+    sum_3 = lax.fori_loop(0, rows // 8, sweep_three, zero, unroll=16)
+    lax.fori_loop(0, rows // 8, sweep_four, 0, unroll=16)
 
     pay[...] = jnp.zeros(pay.shape, F32)
     for index, value in enumerate((sum_0, sum_1, sum_2, sum_3)):

time: 130 us -> 130 us (level)
  transfers between devices with their start and end apart: 15 -> 15, of which waited for: 6 -> 6; matrix products, arithmetic and copies ran while one was open for 4% -> 4% of each run, Pallas kernels for 31% -> 30%
where the time goes in v5:
time: 130 us; the launch traced here: 129 us
  Pallas kernels  60.8 us (47%)
  starting transfers between devices  31 us (24%)
  waiting for transfers between devices  24.4 us (19%)
  local copies, waits for them, and re-layouts  9.42 us (7%)
  other arithmetic  2.04 us (2%)
    pallas_call x1, Pallas kernels, update(): pl.pallas_call(update_kernel, grid=(count_rows,), out_shape=(jax.ShapeDty...  17.3 us
    pallas_call x1, Pallas kernels, factor(): pl.pallas_call(factor_kernel, out_shape=jax.ShapeDtypeStruct(a.shape, F32...  14.5 us
    pallas_call x1, Pallas kernels, raster(): pl.pallas_call(raster_kernel, out_shape=(jax.ShapeDtypeStruct((16, LANES)...  12.6 us
    ppermute x10, waiting for transfers between devices, hop(): return lax.ppermute(block, axis, pairs)  12.2 us
    ppermute x10, starting transfers between devices, hop(): return lax.ppermute(block, axis, pairs)  12 us
    all_to_all x1, starting transfers between devices, exchange(): lax.all_to_all(jnp.broadcast_to(mine, (devices,) + mine.shape), axes, 0, 0)  10.2 us
    ppermute x4, starting transfers between devices, trade(): return (lax.ppermute(near, axis, inside), lax.ppermute(far, axis, between))  8.75 us
    unnamed x32, local copies, waits for them, and re-layouts  6.71 us
  transfers between devices with their start and end apart: 15, of which 6 were waited for; matrix products, arithmetic and copies ran while one was open for 4% of the time, Pallas kernels for 30%

profile of v5, /device:TPU:10, one launch (start us, length us, event | category | flops | bytes accessed | tf_op | source)
XLA Modules:
  0.0 128.8 jit_solution(2131940453648865234)
XLA Ops:
  0.6 1.7 %corner.1 = f32[256,256]{1,0:T(8,128)} custom-call(f32[4,256,8,256]{3,2,1,0:T(8,128)} %schur.2), custom_call_target="tpu_custom_call" | custom-call | flops 2000000000 | bytes 1024 | tf_op jit(solution)/shard_map/corner/pallas_call | solution.py:113
  2.3 0.7 collective-permute-start.2
  3.1 0.1 stack.27
  3.2 0.5 convert_element_type.2.flags
  3.7 2.3 %edges.1 = (f32[8,1024]{1,0:T(8,128)}, f32[8,1024]{1,0:T(8,128)}, f32[8,512]{1,0:T(8,128)}, f32[8,512]{1,0:T(8,128)}) custom-call(s32[6]{0:T(128)} %convert_element_type.2.flags, f32[512,1024]{1,0:T(8,128)} %b.1, f32[512,1024]{1,0:T(8,128)} %b.1, f32[512,1024]{1,0:T(8,128)} %k_hbm.1, f32[512,1024]{1,0:T(8,128)} %k_hbm.1, f32[512,1024]{1,0:T(8,128)} %b.1, ...), custom_call_target="tpu_custom_call" | custom-call | flops 2000000000 | bytes 1024 | tf_op jit(solution)/shard_map/edges/pallas_call | solution.py:189
  5.9 2.5 %collective-permute-start.1 = (f32[8,1024]{1,0:T(8,128)}, f32[8,1024]{1,0:T(8,128)S(1)}, u32[]{:S(2)}, u32[]{:S(2)}) collective-permute-start(f32[8,1024]{1,0:T(8,128)} %get-tuple-element.51), channel_id=1, source_target_pairs={{4,8},{12,16},{20,24},{8,4},{16,12},{24,20},{5,9},{13,17},{21,25},... | collective-permute-start | bytes 98312 | tf_op jit(solution)/shard_map/ppermute | solution.py:42
  8.5 0.0 collective-permute-done.got_near
  8.6 2.8 %collective-permute-done.1.got_far = f32[8,1024]{1,0:T(8,128)S(1)} collective-permute-done((f32[8,1024]{1,0:T(8,128)}, f32[8,1024]{1,0:T(8,128)S(1)}, u32[]{:S(2)}, u32[]{:S(2)}) %collective-permute-start.1) | collective-permute-done | bytes 32800 | tf_op jit(solution)/shard_map/ppermute | solution.py:42
  11.3 1.3 collective-permute-start.5
  12.7 0.0 copy-start.3
  12.7 0.7 copy-done.3
  13.4 0.7 copy-done.4
  14.1 0.7 corners.1
  14.8 0.0 copy-start
  14.8 0.6 copy-done
  15.4 0.6 copy-done.1
  16.0 4.3 %collective-permute-start.3 = (f32[8,768]{1,0:T(8,128)S(1)}, f32[8,768]{1,0:T(8,128)S(1)}, u32[]{:S(2)}, u32[]{:S(2)}) collective-permute-start(f32[8,768]{1,0:T(8,128)S(1)} %get-tuple-element.58), channel_id=1, source_target_pairs={{0,1},{1,0},{2,3},{3,2},{4,5},{5,4},{6,7},{7,6},{8,9},{9,8},{10,11... | collective-permute-start | bytes 73736 | tf_op jit(solution)/shard_map/ppermute | solution.py:42
  20.3 1.9 %collective-permute-start.4 = (f32[8,768]{1,0:T(8,128)S(1)}, f32[8,768]{1,0:T(8,128)S(1)}, u32[]{:S(2)}, u32[]{:S(2)}) collective-permute-start(f32[8,768]{1,0:T(8,128)S(1)} %get-tuple-element.59), channel_id=1, source_target_pairs={{1,2},{2,1},{5,6},{6,5},{9,10},{10,9},{13,14},{14,13},{17,18},{18,... | collective-permute-start | bytes 73736 | tf_op jit(solution)/shard_map/ppermute | solution.py:42
  22.2 1.2 collective-permute-done.5
  23.4 0.5 collective-permute-done.3.got_near
  23.9 2.2 %collective-permute-done.4.got_far = f32[8,768]{1,0:T(8,128)S(1)} collective-permute-done((f32[8,768]{1,0:T(8,128)S(1)}, f32[8,768]{1,0:T(8,128)S(1)}, u32[]{:S(2)}, u32[]{:S(2)}) %collective-permute-start.4) | collective-permute-done | bytes 24608 | tf_op jit(solution)/shard_map/ppermute | solution.py:42
  26.1 0.8 collective-permute-start.6
  26.9 3.3 %extract.1 = (f32[4,256,256]{2,1,0:T(8,128)}, f32[4096,128]{1,0:T(8,128)}) custom-call(f32[4,256,8,256]{3,2,1,0:T(8,128)} %schur.2, f32[4,4096,128]{2,1,0:T(8,128)} %bitcast.26), custom_call_target="tpu_custom_call" | custom-call | flops 3000000000 | bytes 1024 | tf_op jit(solution)/shard_map/extract/pallas_call | solution.py:128
  30.3 0.8 collective-permute-start.10
  31.1 1.3 %collective-permute-start.7 = (f32[256,256]{1,0:T(8,128)S(1)}, f32[256,256]{1,0:T(8,128)S(1)}, u32[]{:S(2)}, u32[]{:S(2)}) collective-permute-start(f32[256,256]{1,0:T(8,128)S(1)} %broadcast_select_fusion), channel_id=1, source_target_pairs={{0,8},{16,24},{1,9},{17,25},{2,10},{18,26},{3,11},{19,27}} | collective-permute-start | bytes 786440 | tf_op jit(solution)/shard_map/ppermute | solution.py:51
  32.4 1.7 %collective-permute-start.9 = (f32[4,256,256]{2,1,0:T(8,128)}, f32[4,256,256]{2,1,0:T(8,128)}, u32[]{:S(2)}, u32[]{:S(2)}) collective-permute-start(f32[4,256,256]{2,1,0:T(8,128)} %get-tuple-element.73._), channel_id=1, source_target_pairs={{0,2},{4,6},{8,10},{12,14},{16,18},{20,22},{24,26},{28,30}} | collective-permute-start | bytes 3145736 | tf_op jit(solution)/shard_map/ppermute | solution.py:51
  34.1 11.1 %collective-permute-done.7 = f32[256,256]{1,0:T(8,128)S(1)} collective-permute-done((f32[256,256]{1,0:T(8,128)S(1)}, f32[256,256]{1,0:T(8,128)S(1)}, u32[]{:S(2)}, u32[]{:S(2)}) %collective-permute-start.7) | collective-permute-done | bytes 262176 | tf_op jit(solution)/shard_map/ppermute | solution.py:51
  45.2 1.3 %collective-permute-start.8 = (f32[256,256]{1,0:T(8,128)S(1)}, f32[256,256]{1,0:T(8,128)S(1)}, u32[]{:S(2)}, u32[]{:S(2)}) collective-permute-start(f32[256,256]{1,0:T(8,128)S(1)} %broadcast_select_fusion.1), channel_id=1, source_target_pairs={{0,4},{8,12},{16,20},{24,28},{1,5},{9,13},{17,21},{25,29},{2,6},{1... | collective-permute-start | bytes 786440 | tf_op jit(solution)/shard_map/ppermute | solution.py:51
  46.5 0.7 copy.16.county
  47.2 0.7 pad_add_fusion.tracts
  47.9 0.7 broadcast_select_fusion.2.a
  48.6 12.6 %raster.1 = (f32[16,128]{1,0:T(8,128)}, f32[64,128]{1,0:T(8,128)}, f32[512,1024]{1,0:T(8,128)}, f32[512,1024]{1,0:T(8,128)}) custom-call(s32[6]{0:T(128)} %convert_element_type.2.flags, f32[512,1024]{1,0:T(8,128)} %b.1, f32[512,1024]{1,0:T(8,128)} %k_hbm.1, f32[8,1024]{1,0:T(8,128)} %copy-done, f32[8,1024]{1,0:T(8,128)} %copy-done.1, f32[8,768]{1,0:T(8,128)} %copy-done.7, ...), custom_call_target="tpu_custom_call" | custom-call | flops 1000000000 | bytes 1024 | tf_op jit(solution)/shard_map/raster/pallas_call | solution.py:377
  61.2 0.0 copy-start.12
  61.2 1.3 %copy-done.12 = f32[4096,128]{1,0:T(8,128)} copy-done((f32[4096,128]{1,0:T(8,128)}, f32[4096,128]{1,0:T(8,128)S(1)}, u32[]{:S(2)}) %copy-start.12) | copy-done | bytes 2097176
  62.6 1.3 %collective-permute-start.11 = (f32[4096,128]{1,0:T(8,128)}, f32[4096,128]{1,0:T(8,128)S(1)}, u32[]{:S(2)}, u32[]{:S(2)}) collective-permute-start(f32[4096,128]{1,0:T(8,128)} %merge.3._), channel_id=1, source_target_pairs={{0,8},{16,24},{1,9},{17,25},{2,10},{18,26},{3,11},{19,27}} | collective-permute-start | bytes 6291464 | tf_op jit(solution)/shard_map/ppermute | solution.py:51
  63.9 1.3 %collective-permute-start.12 = (f32[4,256,256]{2,1,0:T(8,128)}, f32[4,256,256]{2,1,0:T(8,128)S(1)}, u32[]{:S(2)}, u32[]{:S(2)}) collective-permute-start(f32[4,256,256]{2,1,0:T(8,128)} %merge.4.column), channel_id=1, source_target_pairs={{0,1},{2,3},{4,5},{6,7},{8,9},{10,11},{12,13},{14,15},{16,17},{18,... | collective-permute-start | bytes 3145736 | tf_op jit(solution)/shard_map/ppermute | solution.py:51
  65.2 0.7 broadcast_in_dim.7
  65.9 10.2 %all-to-all-start = ((f32[32,16,128]{2,1,0:T(8,128)}), f32[32,16,128]{2,1,0:T(8,128)S(1)}, u32[]{:S(2)}, u32[]{:S(2)}) async-start(f32[32,16,128]{2,1,0:T(8,128)} %broadcast_in_dim.7), calls=%async_computation | async-start | bytes 524288 | tf_op jit(solution)/shard_map/all_to_all | solution.py:165
  76.1 14.5 %factor.1.inverse = f32[256,256]{1,0:T(8,128)} custom-call(f32[256,256]{1,0:T(8,128)} %broadcast_select_fusion.2.a), custom_call_target="tpu_custom_call" | custom-call | flops 1000000000 | bytes 1024 | tf_op jit(solution)/shard_map/factor/pallas_call | solution.py:583
  90.7 6.7 %all-to-all-done = f32[32,16,128]{2,1,0:T(8,128)S(1)} async-done(((f32[32,16,128]{2,1,0:T(8,128)}), f32[32,16,128]{2,1,0:T(8,128)S(1)}, u32[]{:S(2)}, u32[]{:S(2)}) %all-to-all-start) | async-done | bytes 262176 | tf_op jit(solution)/shard_map/all_to_all | solution.py:165
  97.4 0.0 copy-start.13
  97.4 1.3 %copy-done.13 = f32[4096,128]{1,0:T(8,128)} copy-done((f32[4096,128]{1,0:T(8,128)}, f32[4096,128]{1,0:T(8,128)S(1)}, u32[]{:S(2)}) %copy-start.13) | copy-done | bytes 2097176
  98.7 2.9 %merge.5.wide_hbm = f32[4096,128]{1,0:T(8,128)} custom-call(s32[1]{0:T(128)} %bitcast.17.flag, f32[4096,128]{1,0:T(8,128)} %copy-done.13, f32[4096,128]{1,0:T(8,128)} %merge.3._), custom_call_target="tpu_custom_call", output_to_operand_aliasing={{}: (2, {})} | custom-call | flops 2000000000 | bytes 1024 | tf_op jit(solution)/shard_map/merge/pallas_call | solution.py:72
  101.7 1.6 %collective-permute-start.13 = (f32[4096,128]{1,0:T(8,128)}, f32[4096,128]{1,0:T(8,128)S(1)}, u32[]{:S(2)}, u32[]{:S(2)}) collective-permute-start(f32[4096,128]{1,0:T(8,128)} %merge.5.wide_hbm), channel_id=1, source_target_pairs={{0,4},{8,12},{16,20},{24,28},{1,5},{9,13},{17,21},{25,29},{2,6},{1... | collective-permute-start | bytes 6291464 | tf_op jit(solution)/shard_map/ppermute | solution.py:51
  103.3 5.6 %finish.1 = (f32[512,1024]{1,0:T(8,128)}, f32[512,1024]{1,0:T(8,128)}, f32[1,64]{1,0:T(1,128)}, f32[4,128]{1,0:T(4,128)}, f32[1,64]{1,0:T(1,128)}) custom-call(f32[512,128]{1,0:T(8,128)} %bitcast.28, f32[64,128]{1,0:T(8,128)} %get-tuple-element.80.sums, s32[4,128]{1,0:T(4,128)} %bitcast.30, f32[512,1024]{1,0:T(8,128)} %b.1, ...), custom_call_target="tpu_custom_call" | custom-call | flops 8000000000 | bytes 1024 | tf_op jit(solution)/shard_map/finish/pallas_call | solution.py:479
  108.8 1.2 slice_bitcast_fusion
  110.0 1.4 %copy-done.14 = f32[4096,128]{1,0:T(8,128)} copy-done((f32[4096,128]{1,0:T(8,128)}, f32[4096,128]{1,0:T(8,128)S(1)}, u32[]{:S(2)}) %copy-start.14) | copy-done | bytes 2097176
  111.4 17.3 %update.1 = (f32[4,256,256]{2,1,0:T(8,128)}, f32[4,4096,128]{2,1,0:T(8,128)}) custom-call(s32[6]{0:T(128)} %convert_element_type.2.flags, f32[4,256,256]{2,1,0:T(8,128)} %merge.4.column, f32[4,256,256]{2,1,0:T(8,128)} %copy-done.15, f32[4096,128]{1,0:T(8,128)} %merge.5.wide_hbm, f32[4096,128]{1,0:T(8,128)} %copy-done.14, f32[256,256]{1,0:T(8,128)} %factor.1.inverse, ...), custom_call_target="tpu_custom_call" | custom-call | flops 16999999488 | bytes 1024 | tf_op jit(solution)/shard_map/update/pallas_call | solution.py:651
  (36 shorter events, 0.2 us)
Async XLA Ops:
  2.3 6.1 %collective-permute-start.2 = (f32[256,256]{1,0:T(8,128)}, f32[256,256]{1,0:T(8,128)S(1)}, u32[]{:S(2)}, u32[]{:S(2)}) collective-permute-start(f32[256,256]{1,0:T(8,128)} %corner.1), channel_id=1, source_target_pairs={{0,2},{4,6},{8,10},{12,14},{16,18},{20,22},{24,26},{28,30}} | collective-permute-start | bytes 786440 | tf_op jit(solution)/shard_map/ppermute | solution.py:51
  3.6 4.8 %copy-start.5 = (f32[256,256]{1,0:T(8,128)S(1)}, f32[256,256]{1,0:T(8,128)}, u32[]{:S(2)}) copy-start(f32[256,256]{1,0:T(8,128)} %corner.1) | copy-start | bytes 786436
  3.7 9.0 %copy-start.2 = (s32[6]{0:T(128)S(1)}, s32[6]{0:T(128)}, u32[]{:S(2)}) copy-start(s32[6]{0:T(128)} %convert_element_type.2.flags) | copy-start | bytes 76
  5.9 2.6 %collective-permute-start = (f32[8,1024]{1,0:T(8,128)}, f32[8,1024]{1,0:T(8,128)S(1)}, u32[]{:S(2)}, u32[]{:S(2)}) collective-permute-start(f32[8,1024]{1,0:T(8,128)} %get-tuple-element.50), channel_id=1, source_target_pairs={{0,4},{4,0},{8,12},{12,8},{16,20},{20,16},{24,28},{28,24},{1,5},{5... | collective-permute-start | bytes 98312 | tf_op jit(solution)/shard_map/ppermute | solution.py:42
  5.9 5.4 %collective-permute-start.1 = (f32[8,1024]{1,0:T(8,128)}, f32[8,1024]{1,0:T(8,128)S(1)}, u32[]{:S(2)}, u32[]{:S(2)}) collective-permute-start(f32[8,1024]{1,0:T(8,128)} %get-tuple-element.51), channel_id=1, source_target_pairs={{4,8},{12,16},{20,24},{8,4},{16,12},{24,20},{5,9},{13,17},{21,25},... | collective-permute-start | bytes 98312 | tf_op jit(solution)/shard_map/ppermute | solution.py:42
  11.3 12.0 %collective-permute-start.5 = (f32[256,256]{1,0:T(8,128)S(1)}, f32[256,256]{1,0:T(8,128)S(1)}, u32[]{:S(2)}, u32[]{:S(2)}) collective-permute-start(f32[256,256]{1,0:T(8,128)S(1)} %broadcast_select_fusion.4), channel_id=1, source_target_pairs={{0,1},{2,3},{4,5},{6,7},{8,9},{10,11},{12,13},{14,15},{16,17},{18,... | collective-permute-start | bytes 786440 | tf_op jit(solution)/shard_map/ppermute | solution.py:51
  12.7 0.7 copy-start.3
  13.4 0.7 copy-start.4
  14.8 0.6 copy-start
  15.4 0.6 copy-start.1
  16.0 7.9 %collective-permute-start.3 = (f32[8,768]{1,0:T(8,128)S(1)}, f32[8,768]{1,0:T(8,128)S(1)}, u32[]{:S(2)}, u32[]{:S(2)}) collective-permute-start(f32[8,768]{1,0:T(8,128)S(1)} %get-tuple-element.58), channel_id=1, source_target_pairs={{0,1},{1,0},{2,3},{3,2},{4,5},{5,4},{6,7},{7,6},{8,9},{9,8},{10,11... | collective-permute-start | bytes 73736 | tf_op jit(solution)/shard_map/ppermute | solution.py:42
  20.3 5.8 %collective-permute-start.4 = (f32[8,768]{1,0:T(8,128)S(1)}, f32[8,768]{1,0:T(8,128)S(1)}, u32[]{:S(2)}, u32[]{:S(2)}) collective-permute-start(f32[8,768]{1,0:T(8,128)S(1)} %get-tuple-element.59), channel_id=1, source_target_pairs={{1,2},{2,1},{5,6},{6,5},{9,10},{10,9},{13,14},{14,13},{17,18},{18,... | collective-permute-start | bytes 73736 | tf_op jit(solution)/shard_map/ppermute | solution.py:42
  23.9 6.3 %copy-start.7 = (f32[8,768]{1,0:T(8,128)}, f32[8,768]{1,0:T(8,128)S(1)}, u32[]{:S(2)}) copy-start(f32[8,768]{1,0:T(8,128)S(1)} %collective-permute-done.3.got_near) | copy-start | bytes 73732
  26.1 4.1 %copy-start.8 = (f32[8,768]{1,0:T(8,128)}, f32[8,768]{1,0:T(8,128)S(1)}, u32[]{:S(2)}) copy-start(f32[8,768]{1,0:T(8,128)S(1)} %collective-permute-done.4.got_far) | copy-start | bytes 73732
  26.1 20.4 %copy-start.11 = (s32[64]{0:T(128)S(1)}, s32[64]{0:T(128)}, u32[]{:S(2)}) copy-start(s32[64]{0:T(128)} %param.9) | copy-start | bytes 772
  26.1 21.1 %copy-start.9 = (s32[32,64]{1,0:T(8,128)S(1)}, s32[32,64]{1,0:T(8,128)}, u32[]{:S(2)}) copy-start(s32[32,64]{1,0:T(8,128)} %param.8) | copy-start | bytes 24580
  26.1 4.1 %collective-permute-start.6 = (f32[256,256]{1,0:T(8,128)S(1)}, f32[256,256]{1,0:T(8,128)S(1)}, u32[]{:S(2)}, u32[]{:S(2)}) collective-permute-start(f32[256,256]{1,0:T(8,128)S(1)} %broadcast_select_fusion.3), channel_id=1, source_target_pairs={{0,16},{1,17},{2,18},{3,19}} | collective-permute-start | bytes 786440 | tf_op jit(solution)/shard_map/ppermute | solution.py:51
  30.3 30.9 %collective-permute-start.10 = (f32[4096,128]{1,0:T(8,128)}, f32[4096,128]{1,0:T(8,128)S(1)}, u32[]{:S(2)}, u32[]{:S(2)}) collective-permute-start(f32[4096,128]{1,0:T(8,128)} %get-tuple-element.74._), channel_id=1, source_target_pairs={{0,16},{1,17},{2,18},{3,19}} | collective-permute-start | bytes 6291464 | tf_op jit(solution)/shard_map/ppermute | solution.py:51
  31.1 14.0 %collective-permute-start.7 = (f32[256,256]{1,0:T(8,128)S(1)}, f32[256,256]{1,0:T(8,128)S(1)}, u32[]{:S(2)}, u32[]{:S(2)}) collective-permute-start(f32[256,256]{1,0:T(8,128)S(1)} %broadcast_select_fusion), channel_id=1, source_target_pairs={{0,8},{16,24},{1,9},{17,25},{2,10},{18,26},{3,11},{19,27}} | collective-permute-start | bytes 786440 | tf_op jit(solution)/shard_map/ppermute | solution.py:51
  32.4 28.8 %collective-permute-start.9 = (f32[4,256,256]{2,1,0:T(8,128)}, f32[4,256,256]{2,1,0:T(8,128)}, u32[]{:S(2)}, u32[]{:S(2)}) collective-permute-start(f32[4,256,256]{2,1,0:T(8,128)} %get-tuple-element.73._), channel_id=1, source_target_pairs={{0,2},{4,6},{8,10},{12,14},{16,18},{20,22},{24,26},{28,30}} | collective-permute-start | bytes 3145736 | tf_op jit(solution)/shard_map/ppermute | solution.py:51
  45.2 2.7 %collective-permute-start.8 = (f32[256,256]{1,0:T(8,128)S(1)}, f32[256,256]{1,0:T(8,128)S(1)}, u32[]{:S(2)}, u32[]{:S(2)}) collective-permute-start(f32[256,256]{1,0:T(8,128)S(1)} %broadcast_select_fusion.1), channel_id=1, source_target_pairs={{0,4},{8,12},{16,20},{24,28},{1,5},{9,13},{17,21},{25,29},{2,6},{1... | collective-permute-start | bytes 786440 | tf_op jit(solution)/shard_map/ppermute | solution.py:51
  61.2 1.3 %copy-start.12 = (f32[4096,128]{1,0:T(8,128)}, f32[4096,128]{1,0:T(8,128)S(1)}, u32[]{:S(2)}) copy-start(f32[4096,128]{1,0:T(8,128)S(1)} %collective-permute-done.10.got) | copy-start | bytes 6291460
  62.6 34.8 %collective-permute-start.11 = (f32[4096,128]{1,0:T(8,128)}, f32[4096,128]{1,0:T(8,128)S(1)}, u32[]{:S(2)}, u32[]{:S(2)}) collective-permute-start(f32[4096,128]{1,0:T(8,128)} %merge.3._), channel_id=1, source_target_pairs={{0,8},{16,24},{1,9},{17,25},{2,10},{18,26},{3,11},{19,27}} | collective-permute-start | bytes 6291464 | tf_op jit(solution)/shard_map/ppermute | solution.py:51
  63.9 1.3 %copy-start.10 = (f32[16,128]{1,0:T(8,128)S(1)}, f32[16,128]{1,0:T(8,128)}, u32[]{:S(2)}) copy-start(f32[16,128]{1,0:T(8,128)} %get-tuple-element.76) | copy-start | bytes 24580
  63.9 33.5 %collective-permute-start.12 = (f32[4,256,256]{2,1,0:T(8,128)}, f32[4,256,256]{2,1,0:T(8,128)S(1)}, u32[]{:S(2)}, u32[]{:S(2)}) collective-permute-start(f32[4,256,256]{2,1,0:T(8,128)} %merge.4.column), channel_id=1, source_target_pairs={{0,1},{2,3},{4,5},{6,7},{8,9},{10,11},{12,13},{14,15},{16,17},{18,... | collective-permute-start | bytes 3145736 | tf_op jit(solution)/shard_map/ppermute | solution.py:51
  65.9 31.4 %all-to-all-start = ((f32[32,16,128]{2,1,0:T(8,128)}), f32[32,16,128]{2,1,0:T(8,128)S(1)}, u32[]{:S(2)}, u32[]{:S(2)}) async-start(f32[32,16,128]{2,1,0:T(8,128)} %broadcast_in_dim.7), calls=%async_computation | async-start | bytes 524288 | tf_op jit(solution)/shard_map/all_to_all | solution.py:165
  97.4 4.3 %copy-start.6 = (f32[32,16,128]{2,1,0:T(8,128)}, f32[32,16,128]{2,1,0:T(8,128)S(1)}, u32[]{:S(2)}) copy-start(f32[32,16,128]{2,1,0:T(8,128)S(1)} %all-to-all-done) | copy-start | bytes 786436
  97.4 11.5 %copy-start.15 = (f32[4,256,256]{2,1,0:T(8,128)}, f32[4,256,256]{2,1,0:T(8,128)S(1)}, u32[]{:S(2)}) copy-start(f32[4,256,256]{2,1,0:T(8,128)S(1)} %collective-permute-done.12.column_got) | copy-start | bytes 3145732
  97.4 1.3 %copy-start.13 = (f32[4096,128]{1,0:T(8,128)}, f32[4096,128]{1,0:T(8,128)S(1)}, u32[]{:S(2)}) copy-start(f32[4096,128]{1,0:T(8,128)S(1)} %collective-permute-done.11.got) | copy-start | bytes 6291460
  101.7 8.3 %collective-permute-start.13 = (f32[4096,128]{1,0:T(8,128)}, f32[4096,128]{1,0:T(8,128)S(1)}, u32[]{:S(2)}, u32[]{:S(2)}) collective-permute-start(f32[4096,128]{1,0:T(8,128)} %merge.5.wide_hbm), channel_id=1, source_target_pairs={{0,4},{8,12},{16,20},{24,28},{1,5},{9,13},{17,21},{25,29},{2,6},{1... | collective-permute-start | bytes 6291464 | tf_op jit(solution)/shard_map/ppermute | solution.py:51
  110.0 1.4 %copy-start.14 = (f32[4096,128]{1,0:T(8,128)}, f32[4096,128]{1,0:T(8,128)S(1)}, u32[]{:S(2)}) copy-start(f32[4096,128]{1,0:T(8,128)S(1)} %collective-permute-done.13.wide_got) | copy-start | bytes 6291460
